TPU v7x, 256 devices: a whole 4x4x8 slice. The times are simulated.
256 devices in a mesh: seq: 64 (over y, z, core), tp: 4 (over x).
Axes of the slice: x: 4, y: 4, z: 8, core: 2. Of those that a mesh axis runs over, the one named last changes fastest.
Arguments:
- stream: bfloat16 [8192, 2048], P('seq'), may hold values from -256 to 256
- lengths: int32 [6], replicated, may hold values from 1 to 7168, 8192 in all
- q_weight: bfloat16 [2048, 1536], P(None, 'tp'), may hold values from -0.125 to 0.125
- kv_down: bfloat16 [2048, 576], replicated, may hold values from -0.125 to 0.125
- latent_gain: float32 [512], replicated, may hold values from 0.1 to 1.9
- kv_up: bfloat16 [8, 512, 256], P('tp'), may hold values from -0.25 to 0.25
- out_weight: bfloat16 [1024, 2048], P('tp'), may hold values from -0.1875 to 0.1875
- moe_gain: float32 [2048], replicated, may hold values from 0.1 to 1.9
- routes: int32 [8192, 6], P('seq'), may hold values from 0 to 63, all different within a row; in each aligned block of 128 rows (0 to 127, 128 to 255, ...) at most 24 rows name the same one
- route_weight: float32 [8192, 6], P('seq'), may hold values from 0.05 to 0.5
- expert_gate: bfloat16 [64, 2048, 1408], P('seq', None, 'tp'), may hold values from -0.125 to 0.125
- expert_up: bfloat16 [64, 2048, 1408], P('seq', None, 'tp'), may hold values from -0.125 to 0.125
- expert_down: bfloat16 [64, 1408, 2048], P('seq', 'tp'), may hold values from -0.15625 to 0.15625
Outputs:
- layer_out: bfloat16 [8192, 2048], P('seq')
- latent_cache: bfloat16 [8192, 576], P('seq')
Inputs may be any that keep to these rules, and one draw needn't show every extreme that they name: 6 lengths summing to 8192, the longest exactly 7168. In each aligned block of 128 rows no expert is named by more than 24 routes, a bound that some block reaches.
All inputs are finite; a program needn't handle non-finite values.
Results may differ from a plain program's by a relative error of at most 0.0075.
Values may be sent and summed in bfloat16 or wider, within the bound.
A program may use at most 128 MiB of HBM per device.

v0:
```python
import jax
import jax.numpy as jnp
from jax import lax
from jax.sharding import PartitionSpec as P

D = 2048
NOPE = 128
ROPE = 64
LATENT = 512
VDIM = 128


THETA = 50000.0


def place(token_index, lengths):
    prompt_ends = jnp.cumsum(lengths)
    before = (prompt_ends[None, :] <= token_index[:, None]).astype(jnp.int32)
    segment = jnp.sum(before, axis=1)
    prompt_start = jnp.sum(before * lengths[None, :], axis=1)
    return (segment, token_index - prompt_start)


def angles(position):
    half_rope = ROPE // 2
    frequency = THETA ** (-2.0 * jnp.arange(half_rope, dtype=jnp.float32) / ROPE)
    angle_table = position.astype(jnp.float32)[:, None] * frequency[None, :]
    return (jnp.cos(angle_table), jnp.sin(angle_table))


def rotate(values, cos_table, sin_table):
    half_rope = ROPE // 2
    first_half = values[..., :half_rope]
    second = values[..., half_rope:]
    return jnp.concatenate(
        [first_half * cos_table - second * sin_table, first_half * sin_table + second * cos_table],
        axis=-1,
    )


def on_device(
    stream,
    lengths,
    q_weight,
    kv_down,
    latent_gain,
    kv_up,
    out_weight,
    moe_gain,
    routes,
    route_weight,
    expert_gate,
    expert_up,
    expert_down,
):
    tok_count = stream.shape[0]
    head_count = kv_up.shape[0]
    first_row = lax.axis_index("seq") * tok_count
    token_index = first_row + jnp.arange(tok_count, dtype=jnp.int32)
    segment, position = place(token_index, lengths)
    cos_table, sin_table = angles(position)
    kv_proj = jnp.dot(stream, kv_down, preferred_element_type=jnp.float32)
    compressed = kv_proj[:, :LATENT]
    factor = lax.rsqrt(jnp.mean(compressed * compressed, axis=1, keepdims=True) + 1e-06)
    latent = jnp.concatenate(
        [
            compressed * factor * latent_gain[None, :],
            rotate(kv_proj[:, LATENT:], cos_table, sin_table),
        ],
        axis=1,
    ).astype(jnp.bfloat16)
    q_proj = jnp.dot(stream, q_weight, preferred_element_type=jnp.float32).astype(jnp.bfloat16)
    q_proj = q_proj.reshape(tok_count, head_count, NOPE + ROPE)
    absorbed = jnp.einsum(
        "thj,hcj->thc", q_proj[:, :, :NOPE], kv_up[:, :, :NOPE], preferred_element_type=jnp.float32
    )
    rotated = rotate(
        q_proj[:, :, NOPE:].astype(jnp.float32), cos_table[:, None, :], sin_table[:, None, :]
    )
    softmax_scale = (NOPE + ROPE) ** (-0.5)
    queries = (jnp.concatenate([absorbed, rotated], axis=2) * softmax_scale).astype(jnp.bfloat16)
    queries = queries.reshape(tok_count * head_count, LATENT + ROPE)
    row_segment = jnp.repeat(segment, head_count)
    row_index = jnp.repeat(token_index, head_count)
    row_total = tok_count * head_count
    shard_rows = lax.all_gather(latent, "seq", axis=0, tiled=True)
    key_count = shard_rows.shape[0]
    key_index = jnp.arange(key_count, dtype=jnp.int32)
    key_segment, unused = place(key_index, lengths)
    allowed = (row_segment[:, None] == key_segment[None, :]) & (
        key_index[None, :] <= row_index[:, None]
    )
    running_max = jnp.full((row_total,), -1e30, jnp.float32)
    scores = jnp.einsum("ra,ka->rk", queries, shard_rows, preferred_element_type=jnp.float32)
    block_peak = jnp.max(jnp.where(allowed, scores, -jnp.inf), axis=1)
    new_peak = jnp.maximum(running_max, block_peak)
    weights = jnp.where(allowed, jnp.exp(scores - new_peak[:, None]), 0.0)
    running_sum = jnp.sum(weights, axis=1)
    context_sum = jnp.dot(
        weights.astype(jnp.bfloat16), shard_rows[:, :LATENT], preferred_element_type=jnp.float32
    )
    running_max, running_sum, context_sum = (new_peak, running_sum, context_sum)
    context = (context_sum / running_sum[:, None]).reshape(tok_count, head_count, LATENT)
    heads_out = jnp.einsum(
        "thc,hcv->thv",
        context,
        kv_up[:, :, NOPE:].astype(jnp.float32),
        precision=lax.Precision.HIGHEST,
    )
    heads_out = heads_out.astype(jnp.bfloat16).reshape(tok_count, head_count * VDIM)
    partial_attention = jnp.dot(heads_out, out_weight, preferred_element_type=jnp.float32)
    attention = lax.psum(partial_attention.astype(jnp.bfloat16), "tp").astype(jnp.float32)
    hidden = stream.astype(jnp.float32) + attention
    normed = (
        hidden
        * lax.rsqrt(jnp.mean(hidden * hidden, axis=1, keepdims=True) + 1e-06)
        * moe_gain[None, :]
    ).astype(jnp.bfloat16)
    experts = lax.axis_size("seq")
    top_k = routes.shape[1]
    capacity = min(tok_count, max(2, 2 * tok_count * top_k // experts))
    flat_routes = routes.reshape(-1)
    onehot = (flat_routes[:, None] == jnp.arange(experts, dtype=jnp.int32)[None, :]).astype(
        jnp.int32
    )
    slot_rank = jnp.sum((jnp.cumsum(onehot, axis=0) - onehot) * onehot, axis=1)
    slot_index = flat_routes * capacity + slot_rank
    slot_table = (
        slot_index[:, None] == jnp.arange(experts * capacity, dtype=jnp.int32)[None, :]
    ).astype(jnp.bfloat16)
    placing = jnp.sum(slot_table.reshape(tok_count, top_k, experts * capacity), axis=1)
    outgoing = jnp.einsum("ts,td->sd", placing, normed, preferred_element_type=jnp.float32).astype(
        jnp.bfloat16
    )
    outgoing = outgoing.reshape(experts, capacity, D)
    received = lax.all_to_all(outgoing, "seq", split_axis=0, concat_axis=0, tiled=True)
    sources, slot_count, features = received.shape
    flat_rows = received.reshape(sources * slot_count, features)
    gate_act = jnp.dot(flat_rows, expert_gate[0], preferred_element_type=jnp.float32)
    up_act = jnp.dot(flat_rows, expert_up[0], preferred_element_type=jnp.float32)
    hidden_units = (jax.nn.silu(gate_act) * up_act).astype(jnp.bfloat16)
    expert_out = jnp.dot(hidden_units, expert_down[0], preferred_element_type=jnp.float32).astype(
        jnp.bfloat16
    )
    expert_out = expert_out.reshape(sources, slot_count, features)
    returned = lax.all_to_all(expert_out, "seq", split_axis=0, concat_axis=0, tiled=True)
    width_back = returned.shape[2]
    gathered = returned.reshape(experts * capacity, width_back)[slot_index].reshape(
        tok_count, top_k, width_back
    )
    partial_moe = jnp.zeros((tok_count, width_back), jnp.float32)
    for route_slot in range(top_k):
        partial_moe = partial_moe + route_weight[:, route_slot][:, None] * gathered[
            :, route_slot
        ].astype(jnp.float32)
    moe = lax.psum(partial_moe.astype(jnp.bfloat16), "tp").astype(jnp.float32)
    layer_out = (hidden + moe).astype(jnp.bfloat16)
    return (layer_out, latent)


def solution(mesh):
    return jax.shard_map(
        on_device,
        mesh=mesh,
        in_specs=(
            P("seq", None),
            P(),
            P(None, "tp"),
            P(),
            P(),
            P("tp", None, None),
            P("tp", None),
            P(),
            P("seq", None),
            P("seq", None),
            P("seq", None, "tp"),
            P("seq", None, "tp"),
            P("seq", "tp", None),
        ),
        out_specs=(P("seq", None), P("seq", None)),
        check_vma=False,
    )
```

profile of v0, /device:TPU:32, one launch (start us, length us, event | category | flops | bytes accessed | tf_op | source)
XLA Modules:
  0.0 581.4 jit_solution(7485038137034330372)
XLA Ops:
  7.3 1.0 reduce-window.18
  9.0 1.8 fusion.54
  13.8 1.8 convolution_convert_fusion.3
  17.5 2.0 reduce-window.19
  20.0 82.9 %all-gather.2.cloned.1.call-done = bf16[8192,576]{0,1:T(8,128)(2,1)} async-done(((bf16[128,576]{0,1:T(8,128)(2,1)}), bf16[8192,576]{0,1:T(8,128)(2,1)}) %all-gather.2.cloned.1.call-update) | async-done | bytes 9437200 | tf_op jit(solution)/shard_map/all_gather | solution.py:86
  102.9 6.8 %select_reduce_fusion = (f32[256]{0:T(256)S(1)}, f32[256,8192]{1,0:T(8,128)S(1)}) fusion(s32[256]{0:T(256)S(1)} %le.48, s32[8192]{0:T(1024)S(1)} %convert_reduce_fusion, s32[256]{0:T(256)S(1)} %eq.54, bf16[8192,576]{0,1:T(8,128)(2,1)} %all-gather.2.cloned.1.call-done, f32[256,32]{1,0:T(8,128)S(1)} %bitcast.105, f32[256,32]{1,0:T(8,128)S(1)} %bitcast.104, ...), kind=kOutput, calls=%fused_computation.4 | convolution fusion | flops 2426994432 | bytes 18451456 | tf_op jit(solution)/shard_map/ra,ka->rk/dot_general | solution.py:94
  109.7 2.8 fusion.3
  112.5 6.3 %fusion.18 = f32[256,512]{1,0:T(8,128)S(1)} fusion(bf16[8192,576]{0,1:T(8,128)(2,1)} %all-gather.2.cloned.1.call-done, f32[256,8192]{1,0:T(8,128)S(1)} %get-tuple-element.27, f32[256]{0:T(256)S(1)} %broadcast_maximum_fusion, s32[256]{0:T(256)S(1)} %le.48, s32[8192]{0:T(1024)S(1)} %convert_reduce_fusion, s32[256]{0:T(256)S(1)} %eq.54, f32[256]{0:T(256)S(1)} %fusion.3), kind=kOutput, calls=%fused_computation.29 | convolution fusion | flops 2160197632 | bytes 17338368 | tf_op jit(solution)/shard_map/dot_general | solution.py:99
  119.7 1.1 convolution_convert_fusion.2
  121.9 47.6 %all-reduce.3.cloned.1.call-done = bf16[128,2048]{1,0:T(8,128)(2,1)} async-done(((bf16[128,2048]{1,0:T(8,128)(2,1)}), bf16[128,2048]{1,0:T(8,128)(2,1)}) %all-reduce.3.cloned.1.call-update) | async-done | bytes 524304 | tf_op jit(solution)/shard_map/psum | solution.py:112
  169.5 1.3 multiply_reduce_fusion
  170.9 2.9 convolution_convert_fusion.1
  173.8 150.0 %all_to_all.10 = bf16[64,24,2048]{2,1,0:T(8,128)(2,1)S(1)} all-to-all(bf16[64,24,2048]{2,1,0:T(8,128)(2,1)S(1)} %bitcast.97), channel_id=1, replica_groups=mesh['seq'=64,'tp'=4] {'seq'}, dimensions={0} | all-to-all | bytes 12582912 | tf_op jit(solution)/shard_map/all_to_all | solution.py:136
  323.8 2.6 copy-done.3
  326.4 3.8 fusion.16
  330.2 12.3 %convolution_convert_fusion = bf16[1536,2048]{1,0:T(8,128)(2,1)} fusion(bf16[1,352,2048]{2,1,0:T(8,128)(2,1)} %param.25, bf16[1536,2048]{1,0:T(8,128)(2,1)} %bitcast.100, f32[1536,352]{0,1:T(8,128)} %fusion.16, bf16[1,2048,352]{1,2,0:T(8,128)(2,1)} %param.24), kind=kOutput, calls=%fused_computation.7 | convolution fusion | flops 4435574784 | bytes 17629184 | tf_op jit(solution)/shard_map/dot_general | solution.py:142
  342.4 7.6 %all-to-all-start.1 = ((bf16[64,24,2048]{2,1,0:T(8,128)(2,1)}), bf16[64,24,2048]{2,1,0:T(8,128)(2,1)}, u32[]{:S(2)}, u32[]{:S(2)}) async-start(bf16[64,24,2048]{2,1,0:T(8,128)(2,1)} %bitcast.98), calls=%async_computation.1 | async-start | bytes 12582912 | tf_op jit(solution)/shard_map/all_to_all | solution.py:146
  350.3 138.6 %all-to-all-done.1 = bf16[64,24,2048]{2,1,0:T(8,128)(2,1)} async-done(((bf16[64,24,2048]{2,1,0:T(8,128)(2,1)}), bf16[64,24,2048]{2,1,0:T(8,128)(2,1)}, u32[]{:S(2)}, u32[]{:S(2)}) %all-to-all-start.1) | async-done | bytes 6291488 | tf_op jit(solution)/shard_map/all_to_all | solution.py:146
  489.0 11.0 %gather_fusion = bf16[768,2048]{1,0:T(8,128)(2,1)} fusion(bf16[1536,2048]{1,0:T(8,128)(2,1)} %bitcast.16, s32[1024]{0:T(1024)S(1)} %pad_clamp_fusion), kind=kCustom, calls=%fused_computation | custom fusion | bytes 6294528 | tf_op jit(solution)/shard_map/gather | solution.py:148
  499.9 6.2 %reshape.226 = bf16[128,6,2048]{2,1,0:T(8,128)(2,1)} reshape(bf16[768,2048]{1,0:T(8,128)(2,1)} %gather_fusion) | data formatting | bytes 6291456 | tf_op jit(solution)/shard_map/reshape | solution.py:148
  506.2 16.0 %fusion.53 = (bf16[128,1,2048]{2,1,0:T(2,128)(2,1)S(1)}, bf16[128,1,2048]{2,1,0:T(2,128)(2,1)S(1)}, bf16[128,1,2048]{2,1,0:T(2,128)(2,1)S(1)}, bf16[128,1,2048]{...) fusion(bf16[128,6,2048]{2,1,0:T(8,128)(2,1)} %reshape.226), kind=kLoop, calls=%fused_computation.108 | loop fusion | bytes 6291456 | tf_op jit(solution)/shard_map/slice | solution.py:153
  522.2 4.2 fusion.24
  526.5 46.2 %all-reduce.5.cloned.1.call-done = bf16[128,2048]{1,0:T(8,128)(2,1)} async-done(((bf16[128,2048]{1,0:T(8,128)(2,1)}), bf16[128,2048]{1,0:T(8,128)(2,1)}) %all-reduce.5.cloned.1.call-update) | async-done | bytes 524304 | tf_op jit(solution)/shard_map/psum | solution.py:156
  572.8 2.1 add_convert_fusion
  (66 shorter events, 8.1 us)
Async XLA Ops:
  7.2 1.9 copy-start
  7.2 6.6 %copy-start.2 = (bf16[128,2048]{1,0:T(8,128)(2,1)S(1)}, bf16[128,2048]{1,0:T(8,128)(2,1)}, u32[]{:S(2)}) copy-start(bf16[128,2048]{1,0:T(8,128)(2,1)} %param.13) | copy-start | bytes 1572868
  7.2 9.3 %copy-start.6 = (bf16[2,512,256]{2,1,0:T(8,128)(2,1)S(1)}, bf16[2,512,256]{2,1,0:T(8,128)(2,1)}, u32[]{:S(2)}) copy-start(bf16[2,512,256]{2,1,0:T(8,128)(2,1)} %param.18) | copy-start | bytes 1572868
  7.2 95.7 %all-gather.2.cloned.1.call-start = ((), (), s32[]{:S(2)}) async-start(), calls=%async_computation.2 | async-start | bytes 9584640 | tf_op jit(solution)/shard_map/all_gather | solution.py:86
  12.6 156.9 %all-reduce.3.cloned.1.call-start = ((), (), s32[]{:S(2)}) async-start(), calls=%async_computation.3 | async-start | bytes 1048576 | tf_op jit(solution)/shard_map/psum | solution.py:112
  112.5 7.2 %copy-start.5 = (bf16[256,2048]{1,0:T(8,128)(2,1)S(1)}, bf16[256,2048]{1,0:T(8,128)(2,1)}, u32[]{:S(2)}) copy-start(bf16[256,2048]{1,0:T(8,128)(2,1)} %param.19) | copy-start | bytes 3145732
  118.9 52.0 %copy-start.7 = (f32[2048]{0:T(1024)S(1)}, f32[2048]{0:T(1024)}, u32[]{:S(2)}) copy-start(f32[2048]{0:T(1024)} %param.20) | copy-start | bytes 24580
  173.8 152.6 %copy-start.9 = (bf16[1,2048,352]{1,2,0:T(8,128)(2,1)S(1)}, bf16[1,2048,352]{1,2,0:T(8,128)(2,1)}, u32[]{:S(2)}) copy-start(bf16[1,2048,352]{1,2,0:T(8,128)(2,1)} %param.23) | copy-start | bytes 4325380
  323.8 2.6 copy-start.3
  342.4 7.9 %copy-start.8 = (f32[128,6]{0,1:T(8,128)S(1)}, f32[128,6]{0,1:T(8,128)}, u32[]{:S(2)}) copy-start(f32[128,6]{0,1:T(8,128)} %param.22) | copy-start | bytes 9220
  342.4 146.5 %all-to-all-start.1 = ((bf16[64,24,2048]{2,1,0:T(8,128)(2,1)}), bf16[64,24,2048]{2,1,0:T(8,128)(2,1)}, u32[]{:S(2)}, u32[]{:S(2)}) async-start(bf16[64,24,2048]{2,1,0:T(8,128)(2,1)} %bitcast.98), calls=%async_computation.1 | async-start | bytes 12582912 | tf_op jit(solution)/shard_map/all_to_all | solution.py:146
  350.1 222.7 %all-reduce.5.cloned.1.call-start = ((), (), s32[]{:S(2)}) async-start(), calls=%async_computation.4 | async-start | bytes 1048576 | tf_op jit(solution)/shard_map/psum | solution.py:156
  522.2 50.5 %copy-start.4 = (bf16[128,2048]{1,0:T(8,128)(2,1)S(1)}, bf16[128,2048]{1,0:T(8,128)(2,1)}, u32[]{:S(2)}) copy-start(bf16[128,2048]{1,0:T(8,128)(2,1)} %all-reduce.3.cloned.1.call-done) | copy-start | bytes 1572868
  522.2 52.6 %copy-start.1 = (bf16[2048,576]{0,1:T(8,128)(2,1)S(1)}, bf16[2048,576]{0,1:T(8,128)(2,1)}, u32[]{:S(2)}) copy-start(bf16[2048,576]{0,1:T(8,128)(2,1)} %param.16) | copy-start | bytes 7077892
Sparse Core Ops, SparseCore 0:
  12.7 90.1 all-gather.1
  121.0 48.5 all-reduce.2
  526.6 46.0 all-reduce.4
where the time goes:
time: 582 us; the launch traced here: 581 us
  waiting for transfers between devices  315 us (54%)
  blocking collectives  150 us (26%)
  local copies, waits for them, and re-layouts  39.4 us (7%)
  matrix products  37.6 us (6%)
  other arithmetic  17 us (3%)
  between operations  14.1 us (2%)
  starting transfers between devices  7.77 us (1%)
    all_to_all x1, blocking collectives, on_device(): lax.all_to_all(outgoing, 'seq', split_axis=0, concat_axis=0, tiled=True)  150 us
    all_to_all x1, waiting for transfers between devices, on_device(): lax.all_to_all(expert_out, 'seq', split_axis=0, concat_axis=0, tiled=True)  139 us
    all_gather x1, waiting for transfers between devices, on_device(): shard_rows = lax.all_gather(latent, 'seq', axis=0, tiled=True)  82.9 us
    psum x1, waiting for transfers between devices, on_device(): lax.psum(partial_attention.astype(jnp.bfloat16), 'tp').astype(jnp.float32)  47.6 us
    psum x1, waiting for transfers between devices, on_device(): moe = lax.psum(partial_moe.astype(jnp.bfloat16), 'tp').astype(jnp.float32)  46.2 us
    slice x1, local copies, waits for them, and re-layouts, on_device(): gathered[:, route_slot].astype(jnp.float32)  16 us
    dot_general x1, matrix products, on_device(): jnp.dot(hidden_units, expert_down[0], preferred_element_type=jnp.float32)  12.3 us
  transfers between devices with their start and end apart: 4, of which 4 were waited for; matrix products, arithmetic and copies ran while one was open for 1% of the time, Pallas kernels for 0%

commit v1 on v0

--- a/solution.py
+++ b/solution.py
@@ -109,13 +109,17 @@
     )
     heads_out = heads_out.astype(jnp.bfloat16).reshape(tok_count, head_count * VDIM)
     partial_attention = jnp.dot(heads_out, out_weight, preferred_element_type=jnp.float32)
-    attention = lax.psum(partial_attention.astype(jnp.bfloat16), "tp").astype(jnp.float32)
-    hidden = stream.astype(jnp.float32) + attention
-    normed = (
-        hidden
-        * lax.rsqrt(jnp.mean(hidden * hidden, axis=1, keepdims=True) + 1e-06)
-        * moe_gain[None, :]
-    ).astype(jnp.bfloat16)
+    tp_count = lax.axis_size("tp")
+    col_width = D // tp_count
+    col_start = lax.axis_index("tp") * col_width
+    attention_part = lax.psum_scatter(
+        partial_attention.astype(jnp.bfloat16), "tp", scatter_dimension=1, tiled=True
+    ).astype(jnp.float32)
+    stream_part = lax.dynamic_slice_in_dim(stream, col_start, col_width, 1)
+    hidden = stream_part.astype(jnp.float32) + attention_part
+    square_sum = lax.psum(jnp.sum(hidden * hidden, axis=1, keepdims=True), "tp")
+    gain_part = lax.dynamic_slice_in_dim(moe_gain, col_start, col_width, 0)
+    normed = (hidden * lax.rsqrt(square_sum / D + 1e-06) * gain_part[None, :]).astype(jnp.bfloat16)
     experts = lax.axis_size("seq")
     top_k = routes.shape[1]
     capacity = min(tok_count, max(2, 2 * tok_count * top_k // experts))
@@ -132,29 +136,30 @@
     outgoing = jnp.einsum("ts,td->sd", placing, normed, preferred_element_type=jnp.float32).astype(
         jnp.bfloat16
     )
-    outgoing = outgoing.reshape(experts, capacity, D)
+    outgoing = outgoing.reshape(experts, capacity, col_width)
     received = lax.all_to_all(outgoing, "seq", split_axis=0, concat_axis=0, tiled=True)
-    sources, slot_count, features = received.shape
-    flat_rows = received.reshape(sources * slot_count, features)
+    sources, slot_count, _ = received.shape
+    flat_part = received.reshape(sources * slot_count, col_width)
+    flat_rows = lax.all_gather(flat_part, "tp", axis=1, tiled=True)
     gate_act = jnp.dot(flat_rows, expert_gate[0], preferred_element_type=jnp.float32)
     up_act = jnp.dot(flat_rows, expert_up[0], preferred_element_type=jnp.float32)
     hidden_units = (jax.nn.silu(gate_act) * up_act).astype(jnp.bfloat16)
     expert_out = jnp.dot(hidden_units, expert_down[0], preferred_element_type=jnp.float32).astype(
         jnp.bfloat16
     )
-    expert_out = expert_out.reshape(sources, slot_count, features)
-    returned = lax.all_to_all(expert_out, "seq", split_axis=0, concat_axis=0, tiled=True)
-    width_back = returned.shape[2]
-    gathered = returned.reshape(experts * capacity, width_back)[slot_index].reshape(
-        tok_count, top_k, width_back
+    expert_sum = lax.psum_scatter(expert_out, "tp", scatter_dimension=1, tiled=True)
+    expert_sum = expert_sum.reshape(sources, slot_count, col_width)
+    returned = lax.all_to_all(expert_sum, "seq", split_axis=0, concat_axis=0, tiled=True)
+    gathered = returned.reshape(experts * capacity, col_width)[slot_index].reshape(
+        tok_count, top_k, col_width
     )
-    partial_moe = jnp.zeros((tok_count, width_back), jnp.float32)
+    moe = jnp.zeros((tok_count, col_width), jnp.float32)
     for route_slot in range(top_k):
-        partial_moe = partial_moe + route_weight[:, route_slot][:, None] * gathered[
-            :, route_slot
-        ].astype(jnp.float32)
-    moe = lax.psum(partial_moe.astype(jnp.bfloat16), "tp").astype(jnp.float32)
-    layer_out = (hidden + moe).astype(jnp.bfloat16)
+        moe = moe + route_weight[:, route_slot][:, None] * gathered[:, route_slot].astype(
+            jnp.float32
+        )
+    layer_part = (hidden + moe).astype(jnp.bfloat16)
+    layer_out = lax.all_gather(layer_part, "tp", axis=1, tiled=True)
     return (layer_out, latent)
 
 

time: 582 us -> 440 us (0.76)
  blocking collectives: 150 us -> 71.5 us
  waiting for transfers between devices: 315 us -> 272 us
  local copies, waits for them, and re-layouts: 39.4 us -> 16.2 us
    all_to_all x1, blocking collectives: 150 us -> 49.5 us  [on_device(): lax.all_to_all(outgoing, 'seq', split_axis=0, concat_axis=0, tiled=True)]
    all_to_all x1, waiting for transfers between devices: 139 us -> 38.4 us  [on_device(): lax.all_to_all(expert_sum, 'seq', split_axis=0, concat_axis=0, tiled=True)]
    psum x2 -> x0, waiting for transfers between devices: 93.9 us -> none  [the longest x1 47.6 us: on_device(): lax.psum(partial_attention.astype(jnp.bfloat16), 'tp').astype(jnp.float32)]
    reduce_scatter x0 -> x2, waiting for transfers between devices: none -> 87.5 us  [the longest x1 67.3 us: on_device(): lax.psum_scatter(expert_out, 'tp', scatter_dimension=1, tiled=True)]
    all_gather x0 -> x1, waiting for transfers between devices: none -> 64.2 us  [on_device(): flat_rows = lax.all_gather(flat_part, 'tp', axis=1, tiled=True)]
    slice x1, local copies, waits for them, and re-layouts: 16 us -> 1.15 us  [on_device(): gathered[:, route_slot].astype(jnp.float32)]
    all_gather x0 -> x1, blocking collectives: none -> 13.4 us  [on_device(): layer_out = lax.all_gather(layer_part, 'tp', axis=1, tiled=True)]
    psum x0 -> x1, blocking collectives: none -> 8.55 us  [on_device(): square_sum = lax.psum(jnp.sum(hidden * hidden, axis=1, keepdims=True), 'tp')]
  transfers between devices with their start and end apart: 4 -> 5, of which waited for: 4 -> 5; matrix products, arithmetic and copies ran while one was open for 1% -> 3% of each run, Pallas kernels for 0% -> 0%
where the time goes in v1:
time: 440 us
  waiting for transfers between devices  272 us (62%)
  blocking collectives  71.5 us (16%)
  matrix products  43.3 us (10%)
  local copies, waits for them, and re-layouts  16.2 us (4%)
  between operations  14.1 us (3%)
  other arithmetic  11.5 us (3%)
  starting transfers between devices  10.8 us (2%)
    all_gather x1, waiting for transfers between devices, on_device(): shard_rows = lax.all_gather(latent, 'seq', axis=0, tiled=True)  82.1 us
    reduce_scatter x1, waiting for transfers between devices, on_device(): lax.psum_scatter(expert_out, 'tp', scatter_dimension=1, tiled=True)  67.3 us
    all_gather x1, waiting for transfers between devices, on_device(): flat_rows = lax.all_gather(flat_part, 'tp', axis=1, tiled=True)  64.2 us
    all_to_all x1, blocking collectives, on_device(): lax.all_to_all(outgoing, 'seq', split_axis=0, concat_axis=0, tiled=True)  49.5 us
    all_to_all x1, waiting for transfers between devices, on_device(): lax.all_to_all(expert_sum, 'seq', split_axis=0, concat_axis=0, tiled=True)  38.4 us
    reduce_scatter x1, waiting for transfers between devices, on_device(): lax.psum_scatter(partial_attention.astype(jnp.bfloat16), 'tp', scatter_di...  20.2 us
    all_gather x1, blocking collectives, on_device(): layer_out = lax.all_gather(layer_part, 'tp', axis=1, tiled=True)  13.4 us
    dot_general x1, matrix products, on_device(): jnp.dot(hidden_units, expert_down[0], preferred_element_type=jnp.float32)  12.2 us
  transfers between devices with their start and end apart: 5, of which 5 were waited for; matrix products, arithmetic and copies ran while one was open for 3% of the time, Pallas kernels for 0%

profile of v1, /device:TPU:32, one launch (start us, length us, event | category | flops | bytes accessed | tf_op | source)
XLA Modules:
  0.0 439.7 jit_solution(12860109854484053301)
XLA Ops:
  9.0 1.9 fusion.57
  12.1 1.8 convolution_convert_fusion.3
  20.3 82.1 %all-gather.3.cloned.1.call-done = bf16[8192,576]{0,1:T(8,128)(2,1)} async-done(((bf16[128,576]{0,1:T(8,128)(2,1)}), bf16[8192,576]{0,1:T(8,128)(2,1)}) %all-gather.3.cloned.1.call-update) | async-done | bytes 9437200 | tf_op jit(solution)/shard_map/all_gather | solution.py:86
  102.3 7.0 %select_reduce_fusion = (f32[256]{0:T(256)S(1)}, f32[256,8192]{1,0:T(8,128)S(1)}) fusion(s32[256]{0:T(256)S(1)} %le.48, s32[8192]{0:T(1024)S(1)} %convert_reduce_fusion, s32[256]{0:T(256)S(1)} %eq.54, bf16[8192,576]{0,1:T(8,128)(2,1)} %all-gather.3.cloned.1.call-done, f32[256,32]{1,0:T(8,128)} %bitcast.107, f32[256,32]{1,0:T(8,128)} %bitcast.106, ...), kind=kOutput, calls=%fused_computation.4 | convolution fusion | flops 2426994432 | bytes 18451456 | tf_op jit(solution)/shard_map/ra,ka->rk/dot_general | solution.py:94
  109.3 2.8 fusion.3
  112.1 7.0 %fusion.18 = f32[256,512]{1,0:T(8,128)} fusion(bf16[8192,576]{0,1:T(8,128)(2,1)} %all-gather.3.cloned.1.call-done, f32[256,8192]{1,0:T(8,128)S(1)} %get-tuple-element.27, f32[256]{0:T(256)S(1)} %broadcast_maximum_fusion, s32[256]{0:T(256)S(1)} %le.48, s32[8192]{0:T(1024)S(1)} %convert_reduce_fusion, s32[256]{0:T(256)S(1)} %eq.54, f32[256]{0:T(256)S(1)} %fusion.3), kind=kOutput, calls=%fused_computation.29 | convolution fusion | flops 2160197632 | bytes 17338368 | tf_op jit(solution)/shard_map/dot_general | solution.py:99
  119.2 1.4 reshape.211
  120.5 1.4 convolution_convert_fusion.4
  122.0 2.4 convolution_convert_fusion.2
  124.8 1.8 reduce-window.19
  128.8 20.2 %reduce-scatter.3.cloned.1.call-done = bf16[128,512]{1,0:T(8,128)(2,1)} async-done(((bf16[128,2048]{1,0:T(8,128)(2,1)}), bf16[128,512]{1,0:T(8,128)(2,1)}) %reduce-scatter.3.cloned.1.call-update) | async-done | bytes 131088 | tf_op jit(solution)/shard_map/reduce_scatter | solution.py:115
  150.0 8.5 %psum.7 = f32[128,1]{0,1:T(1,128)S(1)} all-reduce(f32[128,1]{0,1:T(1,128)S(1)} %bitcast.111), channel_id=1, replica_groups=mesh['seq'=64,'tp'=4] {'tp'}, use_global_device_ids=true, to_apply=%region_13.14 | all-reduce | flops 128 | bytes 1024 | tf_op jit(solution)/shard_map/psum | solution.py:120
  158.6 1.5 convolution_convert_fusion.1
  160.1 49.5 %all_to_all.10 = bf16[64,24,512]{2,1,0:T(8,128)(2,1)} all-to-all(bf16[64,24,512]{2,1,0:T(8,128)(2,1)S(1)} %bitcast.101), channel_id=1, replica_groups=mesh['seq'=64,'tp'=4] {'seq'}, dimensions={0} | all-to-all | bytes 3145728 | tf_op jit(solution)/shard_map/all_to_all | solution.py:140
  209.7 64.2 %all-gather.5.cloned.1.call-done = bf16[1536,2048]{1,0:T(8,128)(2,1)} async-done(((bf16[1536,512]{1,0:T(8,128)(2,1)}), bf16[1536,2048]{1,0:T(8,128)(2,1)}) %all-gather.5.cloned.1.call-update) | async-done | bytes 6291472 | tf_op jit(solution)/shard_map/all_gather | solution.py:143
  273.9 7.0 %fusion.16 = f32[1536,352]{0,1:T(8,128)} fusion(bf16[1536,2048]{1,0:T(8,128)(2,1)} %all-gather.5.cloned.1.call-done, bf16[1,2048,352]{1,2,0:T(8,128)(2,1)} %param.23), kind=kOutput, calls=%fused_computation.24 | convolution fusion | flops 2214592512 | bytes 9895936 | tf_op jit(solution)/shard_map/dot_general | solution.py:144
  280.9 12.2 %convolution_convert_fusion = bf16[1536,2048]{1,0:T(8,128)(2,1)} fusion(bf16[1,352,2048]{2,1,0:T(8,128)(2,1)} %param.25, bf16[1536,2048]{1,0:T(8,128)(2,1)} %all-gather.5.cloned.1.call-done, f32[1536,352]{0,1:T(8,128)} %fusion.16, bf16[1,2048,352]{1,2,0:T(8,128)(2,1)} %param.24), kind=kOutput, calls=%fused_computation.7 | convolution fusion | flops 4435574784 | bytes 17629184 | tf_op jit(solution)/shard_map/dot_general | solution.py:147
  293.1 67.3 %reduce-scatter.5.cloned.1.call-done = bf16[1536,512]{1,0:T(8,128)(2,1)} async-done(((bf16[1536,2048]{1,0:T(8,128)(2,1)}), bf16[1536,512]{1,0:T(8,128)(2,1)}) %reduce-scatter.5.cloned.1.call-update) | async-done | bytes 1572880 | tf_op jit(solution)/shard_map/reduce_scatter | solution.py:150
  360.5 10.7 %all-to-all-start.1 = ((bf16[64,24,512]{2,1,0:T(8,128)(2,1)}), bf16[64,24,512]{2,1,0:T(8,128)(2,1)}, u32[]{:S(2)}, u32[]{:S(2)}) async-start(bf16[64,24,512]{2,1,0:T(8,128)(2,1)} %bitcast.102), calls=%async_computation.3 | async-start | bytes 3145728 | tf_op jit(solution)/shard_map/all_to_all | solution.py:152
  371.8 38.4 %all-to-all-done.1 = bf16[64,24,512]{2,1,0:T(8,128)(2,1)} async-done(((bf16[64,24,512]{2,1,0:T(8,128)(2,1)}), bf16[64,24,512]{2,1,0:T(8,128)(2,1)}, u32[]{:S(2)}, u32[]{:S(2)}) %all-to-all-start.1) | async-done | bytes 1572896 | tf_op jit(solution)/shard_map/all_to_all | solution.py:152
  410.2 5.0 %gather_fusion = bf16[768,512]{1,0:T(8,128)(2,1)} fusion(bf16[1536,512]{1,0:T(8,128)(2,1)} %bitcast.18, s32[1024]{0:T(1024)S(1)} %pad_clamp_fusion), kind=kCustom, calls=%fused_computation | custom fusion | bytes 1575936 | tf_op jit(solution)/shard_map/gather | solution.py:153
  415.2 1.4 reshape.218
  417.8 1.2 fusion.32
  418.9 13.4 %all_gather.11 = bf16[128,2048]{1,0:T(8,128)(2,1)S(1)} all-gather(bf16[128,512]{1,0:T(8,128)(2,1)S(1)} %fusion.32), channel_id=1, replica_groups=mesh['seq'=64,'tp'=4] {'tp'}, dimensions={1}, use_global_device_ids=true | all-gather | bytes 655360 | tf_op jit(solution)/shard_map/all_gather | solution.py:162
  (70 shorter events, 15.5 us)
Async XLA Ops:
  7.2 1.9 copy-start
  7.2 4.9 %copy-start.1 = (bf16[128,2048]{1,0:T(8,128)(2,1)S(1)}, bf16[128,2048]{1,0:T(8,128)(2,1)}, u32[]{:S(2)}) copy-start(bf16[128,2048]{1,0:T(8,128)(2,1)} %param.13) | copy-start | bytes 1572868
  7.2 4.0 copy-start.6
  7.2 95.1 %all-gather.3.cloned.1.call-start = ((), (), s32[]{:S(2)}) async-start(), calls=%async_computation.4 | async-start | bytes 9584640 | tf_op jit(solution)/shard_map/all_gather | solution.py:86
  9.0 8.4 %copy-start.3 = (bf16[2,512,256]{2,1,0:T(8,128)(2,1)S(1)}, bf16[2,512,256]{2,1,0:T(8,128)(2,1)}, u32[]{:S(2)}) copy-start(bf16[2,512,256]{2,1,0:T(8,128)(2,1)} %param.18) | copy-start | bytes 1572868
  12.0 137.0 %reduce-scatter.3.cloned.1.call-start = ((), (), s32[]{:S(2)}) async-start(), calls=%async_computation.5 | async-start | bytes 655360 | tf_op jit(solution)/shard_map/reduce_scatter | solution.py:115
  119.2 5.2 %copy-start.4 = (s32[128,6]{0,1:T(8,128)S(1)}, s32[128,6]{0,1:T(8,128)}, u32[]{:S(2)}) copy-start(s32[128,6]{0,1:T(8,128)} %param.21) | copy-start | bytes 9220
  124.4 149.6 %all-gather.5.cloned.1.call-start = ((), (), s32[]{:S(2)}) async-start(), calls=%async_computation.6 | async-start | bytes 7864320 | tf_op jit(solution)/shard_map/all_gather | solution.py:143
  209.7 150.8 %reduce-scatter.5.cloned.1.call-start = ((), (), s32[]{:S(2)}) async-start(), calls=%async_computation.7 | async-start | bytes 7864320 | tf_op jit(solution)/shard_map/reduce_scatter | solution.py:150
  293.1 78.2 %copy-start.5 = (f32[128,6]{0,1:T(8,128)S(1)}, f32[128,6]{0,1:T(8,128)}, u32[]{:S(2)}) copy-start(f32[128,6]{0,1:T(8,128)} %param.22) | copy-start | bytes 9220
  360.5 49.7 %all-to-all-start.1 = ((bf16[64,24,512]{2,1,0:T(8,128)(2,1)}), bf16[64,24,512]{2,1,0:T(8,128)(2,1)}, u32[]{:S(2)}, u32[]{:S(2)}) async-start(bf16[64,24,512]{2,1,0:T(8,128)(2,1)} %bitcast.102), calls=%async_computation.3 | async-start | bytes 3145728 | tf_op jit(solution)/shard_map/all_to_all | solution.py:152
  415.2 2.6 copy-start.2
  416.6 1.2 copy-start.7
  416.6 1.2 copy-start.8
Sparse Core Ops, SparseCore 0:
  12.1 90.1 all-gather.2
  124.5 24.4 reduce-scatter.2
  209.8 64.0 all-gather.4
  293.3 67.1 reduce-scatter.4

commit v2 on v1

--- a/solution.py
+++ b/solution.py
@@ -137,19 +137,27 @@
         jnp.bfloat16
     )
     outgoing = outgoing.reshape(experts, capacity, col_width)
-    received = lax.all_to_all(outgoing, "seq", split_axis=0, concat_axis=0, tiled=True)
-    sources, slot_count, _ = received.shape
-    flat_part = received.reshape(sources * slot_count, col_width)
-    flat_rows = lax.all_gather(flat_part, "tp", axis=1, tiled=True)
-    gate_act = jnp.dot(flat_rows, expert_gate[0], preferred_element_type=jnp.float32)
-    up_act = jnp.dot(flat_rows, expert_up[0], preferred_element_type=jnp.float32)
-    hidden_units = (jax.nn.silu(gate_act) * up_act).astype(jnp.bfloat16)
-    expert_out = jnp.dot(hidden_units, expert_down[0], preferred_element_type=jnp.float32).astype(
-        jnp.bfloat16
-    )
-    expert_sum = lax.psum_scatter(expert_out, "tp", scatter_dimension=1, tiled=True)
-    expert_sum = expert_sum.reshape(sources, slot_count, col_width)
-    returned = lax.all_to_all(expert_sum, "seq", split_axis=0, concat_axis=0, tiled=True)
+    chunk_count = 2
+    chunk_slots = capacity // chunk_count
+    returned_chunks = []
+    for chunk in range(chunk_count):
+        sending = outgoing[:, chunk * chunk_slots : (chunk + 1) * chunk_slots]
+        received = lax.all_to_all(sending, "seq", split_axis=0, concat_axis=0, tiled=True)
+        sources, slot_count, _ = received.shape
+        flat_part = received.reshape(sources * slot_count, col_width)
+        flat_rows = lax.all_gather(flat_part, "tp", axis=1, tiled=True)
+        gate_act = jnp.dot(flat_rows, expert_gate[0], preferred_element_type=jnp.float32)
+        up_act = jnp.dot(flat_rows, expert_up[0], preferred_element_type=jnp.float32)
+        hidden_units = (jax.nn.silu(gate_act) * up_act).astype(jnp.bfloat16)
+        expert_out = jnp.dot(
+            hidden_units, expert_down[0], preferred_element_type=jnp.float32
+        ).astype(jnp.bfloat16)
+        expert_sum = lax.psum_scatter(expert_out, "tp", scatter_dimension=1, tiled=True)
+        expert_sum = expert_sum.reshape(sources, slot_count, col_width)
+        returned_chunks.append(
+            lax.all_to_all(expert_sum, "seq", split_axis=0, concat_axis=0, tiled=True)
+        )
+    returned = jnp.concatenate(returned_chunks, axis=1)
     gathered = returned.reshape(experts * capacity, col_width)[slot_index].reshape(
         tok_count, top_k, col_width
     )

time: 440 us -> 434 us (0.986)
  waiting for transfers between devices: 272 us -> 228 us
  blocking collectives: 71.5 us -> 94.6 us
  starting transfers between devices: 10.8 us -> 21.6 us
    all_gather x1 -> x2, waiting for transfers between devices: 64.2 us -> 33.5 us  [on_device(): flat_rows = lax.all_gather(flat_part, 'tp', axis=1, tiled=True)]
    all_to_all x1 -> x2, blocking collectives: 49.5 us -> 72.7 us  [on_device(): lax.all_to_all(sending, 'seq', split_axis=0, concat_axis=0, tiled=True)]
    all_to_all x1 -> x2, waiting for transfers between devices: 38.4 us -> 27.1 us  [on_device(): lax.all_to_all(expert_sum, 'seq', split_axis=0, concat_axis=0, tiled=True)]
    all_to_all x1 -> x2, starting transfers between devices: 10.7 us -> 21.2 us  [on_device(): lax.all_to_all(expert_sum, 'seq', split_axis=0, concat_axis=0, tiled=True)]
    reshape x0 -> x4, local copies, waits for them, and re-layouts: none -> 6.38 us  [the longest x2 4.29 us: on_device(): expert_sum = expert_sum.reshape(sources, slot_count, col_width)]
    reduce_scatter x1 -> x2, waiting for transfers between devices: 67.3 us -> 61.1 us  [on_device(): lax.psum_scatter(expert_out, 'tp', scatter_dimension=1, tiled=True)]
    dot_general x1 -> x2, matrix products: 12.2 us -> 17 us  [on_device(): jnp.dot(hidden_units, expert_down[0], preferred_element_type=jnp.float32)]
  transfers between devices with their start and end apart: 5 -> 8, of which waited for: 5 -> 7; matrix products, arithmetic and copies ran while one was open for 3% -> 9% of each run, Pallas kernels for 0% -> 0%
where the time goes in v2:
time: 434 us; the launch traced here: 433 us
  waiting for transfers between devices  228 us (53%)
  blocking collectives  94.6 us (22%)
  matrix products  45.4 us (10%)
  starting transfers between devices  21.6 us (5%)
  local copies, waits for them, and re-layouts  16.4 us (4%)
  between operations  14.6 us (3%)
  other arithmetic  12.4 us (3%)
    all_gather x1, waiting for transfers between devices, on_device(): shard_rows = lax.all_gather(latent, 'seq', axis=0, tiled=True)  86.3 us
    all_to_all x2, blocking collectives, on_device(): lax.all_to_all(sending, 'seq', split_axis=0, concat_axis=0, tiled=True)  72.7 us
    reduce_scatter x2, waiting for transfers between devices, on_device(): lax.psum_scatter(expert_out, 'tp', scatter_dimension=1, tiled=True)  61.1 us
    all_gather x2, waiting for transfers between devices, on_device(): flat_rows = lax.all_gather(flat_part, 'tp', axis=1, tiled=True)  33.5 us
    all_to_all x2, waiting for transfers between devices, on_device(): lax.all_to_all(expert_sum, 'seq', split_axis=0, concat_axis=0, tiled=True)  27.1 us
    all_to_all x2, starting transfers between devices, on_device(): lax.all_to_all(expert_sum, 'seq', split_axis=0, concat_axis=0, tiled=True)  21.2 us
    reduce_scatter x1, waiting for transfers between devices, on_device(): lax.psum_scatter(partial_attention.astype(jnp.bfloat16), 'tp', scatter_di...  20.3 us
    dot_general x2, matrix products, on_device(): jnp.dot(hidden_units, expert_down[0], preferred_element_type=jnp.float32)  17 us
  transfers between devices with their start and end apart: 8, of which 7 were waited for; matrix products, arithmetic and copies ran while one was open for 9% of the time, Pallas kernels for 0%

profile of v2, /device:TPU:32, one launch (start us, length us, event | category | flops | bytes accessed | tf_op | source)
XLA Modules:
  0.0 433.4 jit_solution(10827465271504471686)
XLA Ops:
  12.0 1.8 convolution_convert_fusion.4
  16.0 86.3 %all-gather.4.cloned.1.call-done = bf16[8192,576]{0,1:T(8,128)(2,1)} async-done(((bf16[128,576]{0,1:T(8,128)(2,1)}), bf16[8192,576]{0,1:T(8,128)(2,1)}) %all-gather.4.cloned.1.call-update) | async-done | bytes 9437200 | tf_op jit(solution)/shard_map/all_gather | solution.py:86
  102.3 6.8 %select_reduce_fusion = (f32[256]{0:T(256)S(1)}, f32[256,8192]{1,0:T(8,128)S(1)}) fusion(s32[256]{0:T(256)S(1)} %le.48, s32[8192]{0:T(1024)S(1)} %convert_reduce_fusion, s32[256]{0:T(256)S(1)} %eq.54, bf16[8192,576]{0,1:T(8,128)(2,1)} %all-gather.4.cloned.1.call-done, f32[256,32]{1,0:T(8,128)S(1)} %bitcast.122, f32[256,32]{1,0:T(8,128)S(1)} %bitcast.121, ...), kind=kOutput, calls=%fused_computation.4 | convolution fusion | flops 2426994432 | bytes 18451456 | tf_op jit(solution)/shard_map/ra,ka->rk/dot_general | solution.py:94
  109.0 2.8 fusion.3
  111.9 6.2 %fusion.35 = f32[256,512]{1,0:T(8,128)S(1)} fusion(bf16[8192,576]{0,1:T(8,128)(2,1)} %all-gather.4.cloned.1.call-done, f32[256,8192]{1,0:T(8,128)S(1)} %get-tuple-element.29, f32[256]{0:T(256)S(1)} %broadcast_maximum_fusion, s32[256]{0:T(256)S(1)} %le.48, s32[8192]{0:T(1024)S(1)} %convert_reduce_fusion, s32[256]{0:T(256)S(1)} %eq.54, f32[256]{0:T(256)S(1)} %fusion.3), kind=kOutput, calls=%fused_computation.39 | convolution fusion | flops 2160197632 | bytes 17338368 | tf_op jit(solution)/shard_map/dot_general | solution.py:99
  124.9 20.3 %reduce-scatter.4.cloned.1.call-done = bf16[128,512]{1,0:T(8,128)(2,1)} async-done(((bf16[128,2048]{1,0:T(8,128)(2,1)}), bf16[128,512]{1,0:T(8,128)(2,1)}) %reduce-scatter.4.cloned.1.call-update) | async-done | bytes 131088 | tf_op jit(solution)/shard_map/reduce_scatter | solution.py:115
  146.2 8.5 %psum.7 = f32[128,1]{0,1:T(1,128)S(1)} all-reduce(f32[128,1]{0,1:T(1,128)S(1)} %bitcast.126), channel_id=1, replica_groups=mesh['seq'=64,'tp'=4] {'tp'}, use_global_device_ids=true, to_apply=%region_13.14 | all-reduce | flops 128 | bytes 1024 | tf_op jit(solution)/shard_map/psum | solution.py:120
  156.8 38.1 %all_to_all.20 = bf16[64,12,512]{2,1,0:T(8,128)(2,1)S(1)} all-to-all(bf16[64,12,512]{2,1,0:T(8,128)(2,1)S(1)} %get-tuple-element.4), channel_id=1, replica_groups=mesh['seq'=64,'tp'=4] {'seq'}, dimensions={0} | all-to-all | bytes 1572864 | tf_op jit(solution)/shard_map/all_to_all | solution.py:145
  196.1 34.5 %all_to_all.21 = bf16[64,12,512]{2,1,0:T(8,128)(2,1)S(1)} all-to-all(bf16[64,12,512]{2,1,0:T(8,128)(2,1)S(1)} %get-tuple-element.5), channel_id=1, replica_groups=mesh['seq'=64,'tp'=4] {'seq'}, dimensions={0} | all-to-all | bytes 1572864 | tf_op jit(solution)/shard_map/all_to_all | solution.py:145
  231.7 2.6 all-gather.6.cloned.1.call-done
  234.3 4.2 fusion.21
  238.4 8.5 %convolution_convert_fusion.1 = bf16[768,2048]{1,0:T(8,128)(2,1)} fusion(bf16[1,352,2048]{2,1,0:T(8,128)(2,1)} %param.25, bf16[768,2048]{1,0:T(8,128)(2,1)} %all-gather.6.cloned.1.call-done, bf16[1,2048,352]{1,2,0:T(8,128)(2,1)} %param.24, f32[768,352]{0,1:T(8,128)} %fusion.21), kind=kOutput, calls=%fused_computation.17 | convolution fusion | flops 2217787392 | bytes 10256384 | tf_op jit(solution)/shard_map/dot_general | solution.py:152
  247.2 30.9 %all-gather.8.cloned.1.call-done = bf16[768,2048]{1,0:T(8,128)(2,1)} async-done(((bf16[768,512]{1,0:T(8,128)(2,1)}), bf16[768,2048]{1,0:T(8,128)(2,1)}) %all-gather.8.cloned.1.call-update) | async-done | bytes 3145744 | tf_op jit(solution)/shard_map/all_gather | solution.py:148
  278.2 4.2 fusion.19
  282.4 8.5 %convolution_convert_fusion = bf16[768,2048]{1,0:T(8,128)(2,1)} fusion(bf16[1,352,2048]{2,1,0:T(8,128)(2,1)} %param.25, bf16[768,2048]{1,0:T(8,128)(2,1)} %all-gather.8.cloned.1.call-done, bf16[1,2048,352]{1,2,0:T(8,128)(2,1)} %param.24, f32[768,352]{0,1:T(8,128)} %fusion.19), kind=kOutput, calls=%fused_computation.16 | convolution fusion | flops 2217787392 | bytes 10256384 | tf_op jit(solution)/shard_map/dot_general | solution.py:152
  290.9 30.7 %reduce-scatter.6.cloned.1.call-done = bf16[768,512]{1,0:T(8,128)(2,1)} async-done(((bf16[768,2048]{1,0:T(8,128)(2,1)}), bf16[768,512]{1,0:T(8,128)(2,1)}) %reduce-scatter.6.cloned.1.call-update) | async-done | bytes 786448 | tf_op jit(solution)/shard_map/reduce_scatter | solution.py:155
  321.6 2.2 reshape.222
  323.8 10.5 %all-to-all-start.1 = ((bf16[64,12,512]{2,1,0:T(8,128)(2,1)}), bf16[64,12,512]{2,1,0:T(8,128)(2,1)S(1)}, u32[]{:S(2)}, u32[]{:S(2)}) async-start(bf16[64,12,512]{2,1,0:T(8,128)(2,1)} %reshape.222), calls=%async_computation.3 | async-start | bytes 2097152 | tf_op jit(solution)/shard_map/all_to_all | solution.py:158
  334.3 30.3 %reduce-scatter.8.cloned.1.call-done = bf16[768,512]{1,0:T(8,128)(2,1)} async-done(((bf16[768,2048]{1,0:T(8,128)(2,1)}), bf16[768,512]{1,0:T(8,128)(2,1)}) %reduce-scatter.8.cloned.1.call-update) | async-done | bytes 786448 | tf_op jit(solution)/shard_map/reduce_scatter | solution.py:155
  364.7 2.1 reshape.224
  366.8 10.7 %all-to-all-start.3 = ((bf16[64,12,512]{2,1,0:T(8,128)(2,1)}), bf16[64,12,512]{2,1,0:T(8,128)(2,1)}, u32[]{:S(2)}, u32[]{:S(2)}) async-start(bf16[64,12,512]{2,1,0:T(8,128)(2,1)} %reshape.224), calls=%async_computation.6 | async-start | bytes 2097152 | tf_op jit(solution)/shard_map/all_to_all | solution.py:158
  378.2 27.1 %all-to-all-done.3 = bf16[64,12,512]{2,1,0:T(8,128)(2,1)} async-done(((bf16[64,12,512]{2,1,0:T(8,128)(2,1)}), bf16[64,12,512]{2,1,0:T(8,128)(2,1)}, u32[]{:S(2)}, u32[]{:S(2)}) %all-to-all-start.3) | async-done | bytes 786464 | tf_op jit(solution)/shard_map/all_to_all | solution.py:158
  407.0 2.7 gather_fusion
  412.3 13.4 %all_gather.15 = bf16[128,2048]{1,0:T(8,128)(2,1)S(1)} all-gather(bf16[128,512]{1,0:T(8,128)(2,1)S(1)} %fusion.53), channel_id=1, replica_groups=mesh['seq'=64,'tp'=4] {'tp'}, dimensions={1}, use_global_device_ids=true | all-gather | bytes 655360 | tf_op jit(solution)/shard_map/all_gather | solution.py:170
  (93 shorter events, 24.8 us)
Async XLA Ops:
  7.2 1.9 copy-start
  7.2 4.8 %copy-start.2 = (bf16[128,2048]{1,0:T(8,128)(2,1)S(1)}, bf16[128,2048]{1,0:T(8,128)(2,1)}, u32[]{:S(2)}) copy-start(bf16[128,2048]{1,0:T(8,128)(2,1)} %param.13) | copy-start | bytes 1572868
  7.2 3.9 copy-start.8
  7.2 95.1 %all-gather.4.cloned.1.call-start = ((), (), s32[]{:S(2)}) async-start(), calls=%async_computation.7 | async-start | bytes 9584640 | tf_op jit(solution)/shard_map/all_gather | solution.py:86
  10.9 3.9 copy-start.5
  12.0 133.2 %reduce-scatter.4.cloned.1.call-start = ((), (), s32[]{:S(2)}) async-start(), calls=%async_computation.8 | async-start | bytes 655360 | tf_op jit(solution)/shard_map/reduce_scatter | solution.py:115
  118.1 1.2 copy-start.4
  118.1 2.4 copy-start.6
  120.5 113.8 %all-gather.6.cloned.1.call-start = ((), (), s32[]{:S(2)}) async-start(), calls=%async_computation.9 | async-start | bytes 3932160 | tf_op jit(solution)/shard_map/all_gather | solution.py:148
  196.0 82.2 %all-gather.8.cloned.1.call-start = ((), (), s32[]{:S(2)}) async-start(), calls=%async_computation.11 | async-start | bytes 3932160 | tf_op jit(solution)/shard_map/all_gather | solution.py:148
  230.6 3.7 copy-start.11
  231.6 90.0 %reduce-scatter.6.cloned.1.call-start = ((), (), s32[]{:S(2)}) async-start(), calls=%async_computation.10 | async-start | bytes 3932160 | tf_op jit(solution)/shard_map/reduce_scatter | solution.py:155
  247.0 117.7 %reduce-scatter.8.cloned.1.call-start = ((), (), s32[]{:S(2)}) async-start(), calls=%async_computation.12 | async-start | bytes 3932160 | tf_op jit(solution)/shard_map/reduce_scatter | solution.py:155
  323.8 43.0 %all-to-all-start.1 = ((bf16[64,12,512]{2,1,0:T(8,128)(2,1)}), bf16[64,12,512]{2,1,0:T(8,128)(2,1)S(1)}, u32[]{:S(2)}, u32[]{:S(2)}) async-start(bf16[64,12,512]{2,1,0:T(8,128)(2,1)} %reshape.222), calls=%async_computation.3 | async-start | bytes 2097152 | tf_op jit(solution)/shard_map/all_to_all | solution.py:158
  334.3 43.4 %copy-start.7 = (f32[128,6]{0,1:T(8,128)S(1)}, f32[128,6]{0,1:T(8,128)}, u32[]{:S(2)}) copy-start(f32[128,6]{0,1:T(8,128)} %param.22) | copy-start | bytes 9220
  366.8 38.5 %all-to-all-start.3 = ((bf16[64,12,512]{2,1,0:T(8,128)(2,1)}), bf16[64,12,512]{2,1,0:T(8,128)(2,1)}, u32[]{:S(2)}, u32[]{:S(2)}) async-start(bf16[64,12,512]{2,1,0:T(8,128)(2,1)} %reshape.224), calls=%async_computation.6 | async-start | bytes 2097152 | tf_op jit(solution)/shard_map/all_to_all | solution.py:158
  409.7 1.5 copy-start.3
  409.9 1.2 copy-start.9
  410.0 1.2 copy-start.10
  410.0 16.6 %copy-start.1 = (bf16[2048,576]{0,1:T(8,128)(2,1)S(1)}, bf16[2048,576]{0,1:T(8,128)(2,1)}, u32[]{:S(2)}) copy-start(bf16[2048,576]{0,1:T(8,128)(2,1)} %param.16) | copy-start | bytes 7077892
Sparse Core Ops, SparseCore 0:
  12.1 90.1 all-gather.3
  120.6 24.5 reduce-scatter.3
  196.1 38.0 all-gather.5
  235.9 42.2 all-gather.7
  280.6 41.0 reduce-scatter.5
  324.1 40.5 reduce-scatter.7

commit v3 on v2

--- a/solution.py
+++ b/solution.py
@@ -69,44 +69,67 @@
         ],
         axis=1,
     ).astype(jnp.bfloat16)
+    tp_count = lax.axis_size("tp")
+    tp_index = lax.axis_index("tp")
+    kv_up_all = lax.all_gather(kv_up, "tp", axis=0, tiled=True)
+    all_heads = kv_up_all.shape[0]
     q_proj = jnp.dot(stream, q_weight, preferred_element_type=jnp.float32).astype(jnp.bfloat16)
-    q_proj = q_proj.reshape(tok_count, head_count, NOPE + ROPE)
+    q_proj = lax.all_gather(q_proj, "tp", axis=1, tiled=True)
+    q_proj = q_proj.reshape(tok_count, all_heads, NOPE + ROPE)
     absorbed = jnp.einsum(
-        "thj,hcj->thc", q_proj[:, :, :NOPE], kv_up[:, :, :NOPE], preferred_element_type=jnp.float32
+        "thj,hcj->thc", q_proj[:, :, :NOPE], kv_up_all[:, :, :NOPE], preferred_element_type=jnp.float32
     )
     rotated = rotate(
         q_proj[:, :, NOPE:].astype(jnp.float32), cos_table[:, None, :], sin_table[:, None, :]
     )
     softmax_scale = (NOPE + ROPE) ** (-0.5)
     queries = (jnp.concatenate([absorbed, rotated], axis=2) * softmax_scale).astype(jnp.bfloat16)
-    queries = queries.reshape(tok_count * head_count, LATENT + ROPE)
-    row_segment = jnp.repeat(segment, head_count)
-    row_index = jnp.repeat(token_index, head_count)
-    row_total = tok_count * head_count
-    shard_rows = lax.all_gather(latent, "seq", axis=0, tiled=True)
-    key_count = shard_rows.shape[0]
-    key_index = jnp.arange(key_count, dtype=jnp.int32)
+    queries = queries.reshape(tok_count * all_heads, LATENT + ROPE)
+    row_segment = jnp.repeat(segment, all_heads)
+    row_index = jnp.repeat(token_index, all_heads)
+    key_rows = tok_count // tp_count
+    own_keys = lax.dynamic_slice_in_dim(latent, tp_index * key_rows, key_rows, 0)
+    shard_rows = lax.all_gather(own_keys, "seq", axis=0, tiled=True)
+    seq_count = shard_rows.shape[0] // key_rows
+    key_index = (
+        jnp.arange(seq_count, dtype=jnp.int32)[:, None] * tok_count
+        + tp_index * key_rows
+        + jnp.arange(key_rows, dtype=jnp.int32)[None, :]
+    ).reshape(-1)
     key_segment, unused = place(key_index, lengths)
     allowed = (row_segment[:, None] == key_segment[None, :]) & (
         key_index[None, :] <= row_index[:, None]
     )
-    running_max = jnp.full((row_total,), -1e30, jnp.float32)
     scores = jnp.einsum("ra,ka->rk", queries, shard_rows, preferred_element_type=jnp.float32)
     block_peak = jnp.max(jnp.where(allowed, scores, -jnp.inf), axis=1)
-    new_peak = jnp.maximum(running_max, block_peak)
-    weights = jnp.where(allowed, jnp.exp(scores - new_peak[:, None]), 0.0)
-    running_sum = jnp.sum(weights, axis=1)
+    peak = jnp.maximum(jnp.full_like(block_peak, -1e30), block_peak)
+    weights = jnp.where(allowed, jnp.exp(scores - peak[:, None]), 0.0)
+    weight_sum = jnp.sum(weights, axis=1)
     context_sum = jnp.dot(
         weights.astype(jnp.bfloat16), shard_rows[:, :LATENT], preferred_element_type=jnp.float32
-    )
-    running_max, running_sum, context_sum = (new_peak, running_sum, context_sum)
-    context = (context_sum / running_sum[:, None]).reshape(tok_count, head_count, LATENT)
-    heads_out = jnp.einsum(
+    ).reshape(tok_count, all_heads, LATENT)
+    heads_part = jnp.einsum(
         "thc,hcv->thv",
-        context,
-        kv_up[:, :, NOPE:].astype(jnp.float32),
+        context_sum,
+        kv_up_all[:, :, NOPE:].astype(jnp.float32),
         precision=lax.Precision.HIGHEST,
     )
+    packed = jnp.concatenate(
+        [
+            heads_part,
+            weight_sum.reshape(tok_count, all_heads, 1),
+            peak.reshape(tok_count, all_heads, 1),
+        ],
+        axis=2,
+    )
+    packed = packed.reshape(tok_count, tp_count, head_count, VDIM + 2).transpose(1, 0, 2, 3)
+    packed = lax.all_to_all(packed, "tp", split_axis=0, concat_axis=0, tiled=True)
+    part_peak = packed[:, :, :, VDIM + 1]
+    top_peak = jnp.max(part_peak, axis=0)
+    rescale = jnp.exp(part_peak - top_peak[None])
+    numerator = jnp.sum(packed[:, :, :, :VDIM] * rescale[..., None], axis=0)
+    denominator = jnp.sum(packed[:, :, :, VDIM] * rescale, axis=0)
+    heads_out = numerator / denominator[..., None]
     heads_out = heads_out.astype(jnp.bfloat16).reshape(tok_count, head_count * VDIM)
     partial_attention = jnp.dot(heads_out, out_weight, preferred_element_type=jnp.float32)
     tp_count = lax.axis_size("tp")

time: 434 us -> 474 us (1.092)
  blocking collectives: 94.6 us -> 122 us
  local copies, waits for them, and re-layouts: 16.4 us -> 21.8 us
    all_to_all x0 -> x1, blocking collectives: none -> 14 us  [on_device(): lax.all_to_all(packed, 'tp', split_axis=0, concat_axis=0, tiled=True)]
    all_gather x0 -> x1, blocking collectives: none -> 13.1 us  [on_device(): q_proj = lax.all_gather(q_proj, 'tp', axis=1, tiled=True)]
    all_gather x1 -> x2, waiting for transfers between devices: 86.3 us -> 90.6 us  [the longest x1 75.5 us: on_device(): shard_rows = lax.all_gather(own_keys, 'seq', axis=0, tiled=True)]
  transfers between devices with their start and end apart: 8 -> 9, of which waited for: 7 -> 8; matrix products, arithmetic and copies ran while one was open for 9% -> 10% of each run, Pallas kernels for 0% -> 0%
where the time goes in v3:
time: 474 us; the launch traced here: 473 us
  waiting for transfers between devices  232 us (49%)
  blocking collectives  122 us (26%)
  matrix products  46.1 us (10%)
  local copies, waits for them, and re-layouts  21.8 us (5%)
  starting transfers between devices  21.7 us (5%)
  other arithmetic  15.1 us (3%)
  between operations  14.7 us (3%)
    all_gather x1, waiting for transfers between devices, on_device(): shard_rows = lax.all_gather(own_keys, 'seq', axis=0, tiled=True)  75.5 us
    all_to_all x2, blocking collectives, on_device(): lax.all_to_all(sending, 'seq', split_axis=0, concat_axis=0, tiled=True)  72.7 us
    reduce_scatter x2, waiting for transfers between devices, on_device(): lax.psum_scatter(expert_out, 'tp', scatter_dimension=1, tiled=True)  62.5 us
    all_gather x2, waiting for transfers between devices, on_device(): flat_rows = lax.all_gather(flat_part, 'tp', axis=1, tiled=True)  34.6 us
    all_to_all x2, waiting for transfers between devices, on_device(): lax.all_to_all(expert_sum, 'seq', split_axis=0, concat_axis=0, tiled=True)  27.1 us
    all_to_all x2, starting transfers between devices, on_device(): lax.all_to_all(expert_sum, 'seq', split_axis=0, concat_axis=0, tiled=True)  21.2 us
    reduce_scatter x1, waiting for transfers between devices, on_device(): lax.psum_scatter(partial_attention.astype(jnp.bfloat16), 'tp', scatter_di...  16.3 us
    dot_general x2, matrix products, on_device(): jnp.dot(hidden_units, expert_down[0], preferred_element_type=jnp.float32)  16 us
  transfers between devices with their start and end apart: 9, of which 8 were waited for; matrix products, arithmetic and copies ran while one was open for 10% of the time, Pallas kernels for 0%

profile of v3, /device:TPU:32, one launch (start us, length us, event | category | flops | bytes accessed | tf_op | source)
XLA Modules:
  0.0 472.8 jit_solution(8885224359928597981)
XLA Ops:
  14.7 13.1 %all_gather.18 = bf16[128,1536]{1,0:T(8,128)(2,1)S(1)} all-gather(bf16[128,384]{1,0:T(8,128)(2,1)S(1)} %convolution_convert_fusion.4), channel_id=1, replica_groups=mesh['seq'=64,'tp'=4] {'tp'}, dimensions={1}, use_global_device_ids=true | all-gather | bytes 491520 | tf_op jit(solution)/shard_map/all_gather | solution.py:77
  30.7 15.1 %all-gather.5.cloned.1.call-done = bf16[8,512,256]{2,1,0:T(8,128)(2,1)} async-done(((bf16[2,512,256]{2,1,0:T(8,128)(2,1)}), bf16[8,512,256]{2,1,0:T(8,128)(2,1)}) %all-gather.5.cloned.1.call-update) | async-done | bytes 2097168 | tf_op jit(solution)/shard_map/all_gather | solution.py:74
  47.5 2.5 copy.143
  50.0 75.5 %all-gather.7.cloned.1.call-done = bf16[2048,576]{1,0:T(8,128)(2,1)} async-done(((bf16[32,576]{1,0:T(8,128)(2,1)}), bf16[2048,576]{1,0:T(8,128)(2,1)}) %all-gather.7.cloned.1.call-update) | async-done | bytes 2359312 | tf_op jit(solution)/shard_map/all_gather | solution.py:92
  125.5 8.6 %select_reduce_fusion = (f32[1024]{0:T(1024)S(1)}, f32[1024,2048]{1,0:T(8,128)}) fusion(s32[2048]{0:T(1024)S(1)} %add.144, s32[2048]{0:T(1024)S(1)} %convert_reduce_fusion, s32[1024]{0:T(1024)S(1)} %le.48, s32[1024]{0:T(1024)S(1)} %eq.54, bf16[2048,576]{1,0:T(8,128)(2,1)} %all-gather.7.cloned.1.call-done, f32[1024,32]{1,0:T(8,128)} %bitcast.153, ...), kind=kOutput, calls=%fused_computation.2 | convolution fusion | flops 2428763136 | bytes 13135872 | tf_op jit(solution)/shard_map/ra,ka->rk/dot_general | solution.py:103
  134.4 5.5 %fusion = f32[1024]{0:T(1024)S(1)} fusion(f32[1024,2048]{1,0:T(8,128)} %get-tuple-element.29, f32[1024]{0:T(1024)S(1)} %broadcast_maximum_fusion, s32[2048]{0:T(1024)S(1)} %add.144, s32[2048]{0:T(1024)S(1)} %convert_reduce_fusion, s32[1024]{0:T(1024)S(1)} %le.48, s32[1024]{0:T(1024)S(1)} %eq.54), kind=kLoop, calls=%fused_computation.4 | loop fusion | flops 12581888 | bytes 8421376 | tf_op jit(solution)/shard_map/reduce_sum | solution.py:107
  140.2 4.3 fusion.10
  148.2 14.0 %all_to_all.25 = f32[4,128,2,130]{1,2,3,0:T(2,128)S(1)} all-to-all(f32[4,128,2,130]{1,2,3,0:T(2,128)S(1)} %maximum_bitcast_fusion), channel_id=1, replica_groups=mesh['seq'=64,'tp'=4] {'tp'}, dimensions={0} | all-to-all | bytes 1064960 | tf_op jit(solution)/shard_map/all_to_all | solution.py:126
  168.3 16.3 %reduce-scatter.4.cloned.1.call-done = bf16[128,512]{1,0:T(8,128)(2,1)} async-done(((bf16[128,2048]{1,0:T(8,128)(2,1)}), bf16[128,512]{1,0:T(8,128)(2,1)}) %reduce-scatter.4.cloned.1.call-update) | async-done | bytes 131088 | tf_op jit(solution)/shard_map/reduce_scatter | solution.py:138
  185.7 8.4 %psum.7 = f32[128,1]{0,1:T(1,128)S(1)} all-reduce(f32[128,1]{0,1:T(1,128)S(1)} %bitcast.158), channel_id=1, replica_groups=mesh['seq'=64,'tp'=4] {'tp'}, use_global_device_ids=true, to_apply=%region_16.17 | all-reduce | flops 128 | bytes 1024 | tf_op jit(solution)/shard_map/psum | solution.py:143
  196.0 38.2 %all_to_all.26 = bf16[64,12,512]{2,1,0:T(8,128)(2,1)S(1)} all-to-all(bf16[64,12,512]{2,1,0:T(8,128)(2,1)S(1)} %get-tuple-element.4), channel_id=1, replica_groups=mesh['seq'=64,'tp'=4] {'seq'}, dimensions={0} | all-to-all | bytes 1572864 | tf_op jit(solution)/shard_map/all_to_all | solution.py:168
  235.3 34.5 %all_to_all.27 = bf16[64,12,512]{2,1,0:T(8,128)(2,1)S(1)} all-to-all(bf16[64,12,512]{2,1,0:T(8,128)(2,1)S(1)} %get-tuple-element.5), channel_id=1, replica_groups=mesh['seq'=64,'tp'=4] {'seq'}, dimensions={0} | all-to-all | bytes 1572864 | tf_op jit(solution)/shard_map/all_to_all | solution.py:168
  273.5 3.6 fusion.23
  277.2 7.8 %convolution_convert_fusion.1 = bf16[768,2048]{1,0:T(8,128)(2,1)} fusion(bf16[1,352,2048]{2,1,0:T(8,128)(2,1)S(1)} %copy-done.15, bf16[768,2048]{1,0:T(8,128)(2,1)} %all-gather.9.cloned.1.call-done, bf16[1,2048,352]{1,2,0:T(8,128)(2,1)} %param.24, f32[768,352]{0,1:T(8,128)S(1)} %fusion.23), kind=kOutput, calls=%fused_computation.10 | convolution fusion | flops 2217787392 | bytes 10256384 | tf_op jit(solution)/shard_map/dot_general | solution.py:175
  285.3 32.2 %all-gather.11.cloned.1.call-done = bf16[768,2048]{1,0:T(8,128)(2,1)} async-done(((bf16[768,512]{1,0:T(8,128)(2,1)}), bf16[768,2048]{1,0:T(8,128)(2,1)}) %all-gather.11.cloned.1.call-update) | async-done | bytes 3145744 | tf_op jit(solution)/shard_map/all_gather | solution.py:171
  317.4 3.2 fusion.21
  320.6 8.2 %convolution_convert_fusion = bf16[768,2048]{1,0:T(8,128)(2,1)} fusion(bf16[1,352,2048]{2,1,0:T(8,128)(2,1)} %param.25, bf16[768,2048]{1,0:T(8,128)(2,1)} %all-gather.11.cloned.1.call-done, bf16[1,2048,352]{1,2,0:T(8,128)(2,1)} %param.24, f32[768,352]{0,1:T(8,128)S(1)} %fusion.21), kind=kOutput, calls=%fused_computation.9 | convolution fusion | flops 2217787392 | bytes 10256384 | tf_op jit(solution)/shard_map/dot_general | solution.py:175
  328.9 32.0 %reduce-scatter.6.cloned.1.call-done = bf16[768,512]{1,0:T(8,128)(2,1)} async-done(((bf16[768,2048]{1,0:T(8,128)(2,1)}), bf16[768,512]{1,0:T(8,128)(2,1)}) %reduce-scatter.6.cloned.1.call-update) | async-done | bytes 786448 | tf_op jit(solution)/shard_map/reduce_scatter | solution.py:178
  363.1 10.5 %all-to-all-start.2 = ((bf16[64,12,512]{2,1,0:T(8,128)(2,1)}), bf16[64,12,512]{2,1,0:T(8,128)(2,1)S(1)}, u32[]{:S(2)}, u32[]{:S(2)}) async-start(bf16[64,12,512]{2,1,0:T(8,128)(2,1)} %reshape.278), calls=%async_computation.4 | async-start | bytes 2097152 | tf_op jit(solution)/shard_map/all_to_all | solution.py:181
  373.6 30.5 %reduce-scatter.8.cloned.1.call-done = bf16[768,512]{1,0:T(8,128)(2,1)} async-done(((bf16[768,2048]{1,0:T(8,128)(2,1)}), bf16[768,512]{1,0:T(8,128)(2,1)}) %reduce-scatter.8.cloned.1.call-update) | async-done | bytes 786448 | tf_op jit(solution)/shard_map/reduce_scatter | solution.py:178
  406.2 10.7 %all-to-all-start.4 = ((bf16[64,12,512]{2,1,0:T(8,128)(2,1)}), bf16[64,12,512]{2,1,0:T(8,128)(2,1)}, u32[]{:S(2)}, u32[]{:S(2)}) async-start(bf16[64,12,512]{2,1,0:T(8,128)(2,1)} %reshape.280), calls=%async_computation.7 | async-start | bytes 2097152 | tf_op jit(solution)/shard_map/all_to_all | solution.py:181
  417.6 27.1 %all-to-all-done.4 = bf16[64,12,512]{2,1,0:T(8,128)(2,1)} async-done(((bf16[64,12,512]{2,1,0:T(8,128)(2,1)}), bf16[64,12,512]{2,1,0:T(8,128)(2,1)}, u32[]{:S(2)}, u32[]{:S(2)}) %all-to-all-start.4) | async-done | bytes 786464 | tf_op jit(solution)/shard_map/all_to_all | solution.py:181
  446.4 2.7 gather_fusion
  451.7 13.4 %all_gather.23 = bf16[128,2048]{1,0:T(8,128)(2,1)S(1)} all-gather(bf16[128,512]{1,0:T(8,128)(2,1)S(1)} %fusion.52), channel_id=1, replica_groups=mesh['seq'=64,'tp'=4] {'tp'}, dimensions={1}, use_global_device_ids=true | all-gather | bytes 655360 | tf_op jit(solution)/shard_map/all_gather | solution.py:193
  (120 shorter events, 40.5 us)
Async XLA Ops:
  7.2 2.4 copy-start
  7.2 4.5 copy-start.11
  7.2 38.6 %all-gather.5.cloned.1.call-start = ((), (), s32[]{:S(2)}) async-start(), calls=%async_computation.8 | async-start | bytes 2621440 | tf_op jit(solution)/shard_map/all_gather | solution.py:74
  7.9 117.6 %all-gather.7.cloned.1.call-start = ((), (), s32[]{:S(2)}) async-start(), calls=%async_computation.9 | async-start | bytes 2662400 | tf_op jit(solution)/shard_map/all_gather | solution.py:92
  9.6 3.3 copy-start.3
  12.8 171.8 %reduce-scatter.4.cloned.1.call-start = ((), (), s32[]{:S(2)}) async-start(), calls=%async_computation.10 | async-start | bytes 655360 | tf_op jit(solution)/shard_map/reduce_scatter | solution.py:138
  47.5 78.0 %copy-start.8 = (f32[128,8,32]{2,1,0:T(8,128)S(1)}, f32[128,8,32]{2,1,0:T(8,128)}, u32[]{:S(2)}) copy-start(f32[128,8,32]{2,1,0:T(8,128)} %copy.86) | copy-start | bytes 393220
  134.4 5.8 %copy-start.2 = (f32[1024,2048]{1,0:T(8,128)S(1)}, f32[1024,2048]{1,0:T(8,128)}, u32[]{:S(2)}) copy-start(f32[1024,2048]{1,0:T(8,128)} %get-tuple-element.29) | copy-start | bytes 25165828
  140.2 4.3 copy-start.4
  147.3 15.2 %copy-start.6 = (bf16[256,2048]{1,0:T(8,128)(2,1)S(1)}, bf16[256,2048]{1,0:T(8,128)(2,1)}, u32[]{:S(2)}) copy-start(bf16[256,2048]{1,0:T(8,128)(2,1)} %param.19) | copy-start | bytes 3145732
  148.2 15.6 %copy-start.9 = (s32[128,6]{0,1:T(8,128)S(1)}, s32[128,6]{0,1:T(8,128)}, u32[]{:S(2)}) copy-start(s32[128,6]{0,1:T(8,128)} %param.21) | copy-start | bytes 9220
  163.7 109.8 %all-gather.9.cloned.1.call-start = ((), (), s32[]{:S(2)}) async-start(), calls=%async_computation.11 | async-start | bytes 3932160 | tf_op jit(solution)/shard_map/all_gather | solution.py:171
  235.3 82.1 %all-gather.11.cloned.1.call-start = ((), (), s32[]{:S(2)}) async-start(), calls=%async_computation.13 | async-start | bytes 3932160 | tf_op jit(solution)/shard_map/all_gather | solution.py:171
  271.0 6.2 %copy-start.15 = (bf16[1,352,2048]{2,1,0:T(8,128)(2,1)S(1)}, bf16[1,352,2048]{2,1,0:T(8,128)(2,1)}, u32[]{:S(2)}) copy-start(bf16[1,352,2048]{2,1,0:T(8,128)(2,1)} %param.25) | copy-start | bytes 4325380
  271.0 89.9 %reduce-scatter.6.cloned.1.call-start = ((), (), s32[]{:S(2)}) async-start(), calls=%async_computation.12 | async-start | bytes 3932160 | tf_op jit(solution)/shard_map/reduce_scatter | solution.py:178
  284.9 32.5 %copy-start.14 = (bf16[1,2048,352]{1,2,0:T(8,128)(2,1)S(1)}, bf16[1,2048,352]{1,2,0:T(8,128)(2,1)}, u32[]{:S(2)}) copy-start(bf16[1,2048,352]{1,2,0:T(8,128)(2,1)} %param.23) | copy-start | bytes 4325380
  284.9 119.1 %reduce-scatter.8.cloned.1.call-start = ((), (), s32[]{:S(2)}) async-start(), calls=%async_computation.14 | async-start | bytes 3932160 | tf_op jit(solution)/shard_map/reduce_scatter | solution.py:178
  363.1 43.1 %all-to-all-start.2 = ((bf16[64,12,512]{2,1,0:T(8,128)(2,1)}), bf16[64,12,512]{2,1,0:T(8,128)(2,1)S(1)}, u32[]{:S(2)}, u32[]{:S(2)}) async-start(bf16[64,12,512]{2,1,0:T(8,128)(2,1)} %reshape.278), calls=%async_computation.4 | async-start | bytes 2097152 | tf_op jit(solution)/shard_map/all_to_all | solution.py:181
  373.6 43.5 %copy-start.10 = (f32[128,6]{0,1:T(8,128)S(1)}, f32[128,6]{0,1:T(8,128)}, u32[]{:S(2)}) copy-start(f32[128,6]{0,1:T(8,128)} %param.22) | copy-start | bytes 9220
  406.2 38.5 %all-to-all-start.4 = ((bf16[64,12,512]{2,1,0:T(8,128)(2,1)}), bf16[64,12,512]{2,1,0:T(8,128)(2,1)}, u32[]{:S(2)}, u32[]{:S(2)}) async-start(bf16[64,12,512]{2,1,0:T(8,128)(2,1)} %reshape.280), calls=%async_computation.7 | async-start | bytes 2097152 | tf_op jit(solution)/shard_map/all_to_all | solution.py:181
  449.1 1.5 copy-start.5
  449.3 1.2 copy-start.12
  449.4 1.2 copy-start.13
  449.4 16.6 %copy-start.1 = (bf16[2048,576]{0,1:T(8,128)(2,1)S(1)}, bf16[2048,576]{0,1:T(8,128)(2,1)}, u32[]{:S(2)}) copy-start(bf16[2048,576]{0,1:T(8,128)(2,1)} %param.16) | copy-start | bytes 7077892
  (1 other events, 0.9 us)
Sparse Core Ops, SparseCore 0:
  9.8 35.8 all-gather.4
  48.5 76.9 all-gather.6
  163.8 20.7 reduce-scatter.3
  235.4 38.0 all-gather.8
  275.2 42.2 all-gather.10
  319.8 41.0 reduce-scatter.5
  363.5 40.5 reduce-scatter.7

commit v4 on v2

--- a/solution.py
+++ b/solution.py
@@ -1,6 +1,8 @@
 import jax
 import jax.numpy as jnp
 from jax import lax
+from jax.experimental import pallas as pl
+from jax.experimental.pallas import tpu as pltpu
 from jax.sharding import PartitionSpec as P
 
 D = 2048
@@ -36,6 +38,68 @@
         [first_half * cos_table - second * sin_table, first_half * sin_table + second * cos_table],
         axis=-1,
     )
+
+
+def _exchange_body(x_ref, o_ref, send_sem, recv_sem, local_sem):
+    n = x_ref.shape[0]
+    me = lax.axis_index("seq")
+    tp_me = lax.axis_index("tp")
+    local = pltpu.make_async_copy(x_ref.at[me], o_ref.at[me], local_sem)
+    local.start()
+
+    def start_one(i, carry):
+        dest = lax.rem(me + i, n)
+        pltpu.make_async_remote_copy(
+            src_ref=x_ref.at[dest],
+            dst_ref=o_ref.at[me],
+            send_sem=send_sem.at[dest],
+            recv_sem=recv_sem.at[me],
+            device_id=(dest, tp_me),
+            device_id_type=pl.DeviceIdType.MESH,
+        ).start()
+        return carry
+
+    lax.fori_loop(1, n, start_one, 0)
+
+    def wait_one(i, carry):
+        dest = lax.rem(me + i, n)
+        source = lax.rem(me + n - i, n)
+        pltpu.make_async_remote_copy(
+            src_ref=x_ref.at[dest],
+            dst_ref=o_ref.at[source],
+            send_sem=send_sem.at[dest],
+            recv_sem=recv_sem.at[source],
+            device_id=(dest, tp_me),
+            device_id_type=pl.DeviceIdType.MESH,
+        ).wait_send()
+        pltpu.make_async_remote_copy(
+            src_ref=x_ref.at[source],
+            dst_ref=o_ref.at[source],
+            send_sem=send_sem.at[source],
+            recv_sem=recv_sem.at[source],
+            device_id=(source, tp_me),
+            device_id_type=pl.DeviceIdType.MESH,
+        ).wait_recv()
+        return carry
+
+    lax.fori_loop(1, n, wait_one, 0)
+    local.wait()
+
+
+def seq_exchange(x):
+    n = x.shape[0]
+    return pl.pallas_call(
+        _exchange_body,
+        out_shape=jax.ShapeDtypeStruct(x.shape, x.dtype),
+        in_specs=[pl.BlockSpec(memory_space=pl.ANY)],
+        out_specs=pl.BlockSpec(memory_space=pl.ANY),
+        scratch_shapes=[
+            pltpu.SemaphoreType.DMA((n,)),
+            pltpu.SemaphoreType.DMA((n,)),
+            pltpu.SemaphoreType.DMA,
+        ],
+        compiler_params=pltpu.CompilerParams(has_side_effects=True),
+    )(x)
 
 
 def on_device(
@@ -142,7 +206,7 @@
     returned_chunks = []
     for chunk in range(chunk_count):
         sending = outgoing[:, chunk * chunk_slots : (chunk + 1) * chunk_slots]
-        received = lax.all_to_all(sending, "seq", split_axis=0, concat_axis=0, tiled=True)
+        received = seq_exchange(sending)
         sources, slot_count, _ = received.shape
         flat_part = received.reshape(sources * slot_count, col_width)
         flat_rows = lax.all_gather(flat_part, "tp", axis=1, tiled=True)
@@ -155,7 +219,7 @@
         expert_sum = lax.psum_scatter(expert_out, "tp", scatter_dimension=1, tiled=True)
         expert_sum = expert_sum.reshape(sources, slot_count, col_width)
         returned_chunks.append(
-            lax.all_to_all(expert_sum, "seq", split_axis=0, concat_axis=0, tiled=True)
+            seq_exchange(expert_sum)
         )
     returned = jnp.concatenate(returned_chunks, axis=1)
     gathered = returned.reshape(experts * capacity, col_width)[slot_index].reshape(

time: 434 us -> 442 us (1.018)
  Pallas kernels: 0 us -> 151 us
  blocking collectives: 94.6 us -> 21.9 us
  waiting for transfers between devices: 228 us -> 173 us
  starting transfers between devices: 21.6 us -> 0.47 us
    pallas_call x0 -> x4, Pallas kernels: none -> 151 us  [seq_exchange(): pl.pallas_call(_exchange_body, out_shape=jax.ShapeDtypeStruct(x.shape, x....]
    all_to_all x2 -> x0, blocking collectives: 72.7 us -> none  [on_device(): lax.all_to_all(sending, 'seq', split_axis=0, concat_axis=0, tiled=True)]
    reduce_scatter x2, waiting for transfers between devices: 61.1 us -> 32.8 us  [on_device(): lax.psum_scatter(expert_out, 'tp', scatter_dimension=1, tiled=True)]
    all_to_all x2 -> x0, waiting for transfers between devices: 27.1 us -> none  [on_device(): lax.all_to_all(expert_sum, 'seq', split_axis=0, concat_axis=0, tiled=True)]
    all_to_all x2 -> x0, starting transfers between devices: 21.2 us -> none  [on_device(): lax.all_to_all(expert_sum, 'seq', split_axis=0, concat_axis=0, tiled=True)]
  transfers between devices with their start and end apart: 8 -> 6, of which waited for: 7 -> 6; matrix products, arithmetic and copies ran while one was open for 9% -> 9% of each run, Pallas kernels for 0% -> 17%
where the time goes in v4:
time: 442 us; the launch traced here: 438 us
  waiting for transfers between devices  173 us (39%)
  Pallas kernels  151 us (34%)
  matrix products  44.7 us (10%)
  blocking collectives  21.9 us (5%)
  local copies, waits for them, and re-layouts  20.5 us (5%)
  between operations  14.6 us (3%)
  other arithmetic  12.4 us (3%)
    pallas_call x4, Pallas kernels, seq_exchange(): pl.pallas_call(_exchange_body, out_shape=jax.ShapeDtypeStruct(x.shape, x....  151 us
    all_gather x1, waiting for transfers between devices, on_device(): shard_rows = lax.all_gather(latent, 'seq', axis=0, tiled=True)  86.3 us
    all_gather x2, waiting for transfers between devices, on_device(): flat_rows = lax.all_gather(flat_part, 'tp', axis=1, tiled=True)  33.1 us
    reduce_scatter x2, waiting for transfers between devices, on_device(): lax.psum_scatter(expert_out, 'tp', scatter_dimension=1, tiled=True)  32.8 us
    reduce_scatter x1, waiting for transfers between devices, on_device(): lax.psum_scatter(partial_attention.astype(jnp.bfloat16), 'tp', scatter_di...  20.3 us
    dot_general x2, matrix products, on_device(): jnp.dot(hidden_units, expert_down[0], preferred_element_type=jnp.float32)  16.1 us
    all_gather x1, blocking collectives, on_device(): layer_out = lax.all_gather(layer_part, 'tp', axis=1, tiled=True)  13.4 us
  transfers between devices with their start and end apart: 6, of which 6 were waited for; matrix products, arithmetic and copies ran while one was open for 9% of the time, Pallas kernels for 17%

profile of v4, /device:TPU:32, one launch (start us, length us, event | category | flops | bytes accessed | tf_op | source)
XLA Modules:
  0.0 438.4 jit_solution(1805820008675495770)
XLA Ops:
  16.0 86.3 %all-gather.4.cloned.1.call-done = bf16[8192,576]{0,1:T(8,128)(2,1)} async-done(((bf16[128,576]{0,1:T(8,128)(2,1)}), bf16[8192,576]{0,1:T(8,128)(2,1)}) %all-gather.4.cloned.1.call-update) | async-done | bytes 9437200 | tf_op jit(solution)/shard_map/all_gather | solution.py:150
  102.3 6.8 %select_reduce_fusion = (f32[256]{0:T(256)S(1)}, f32[256,8192]{1,0:T(8,128)S(1)}) fusion(s32[256]{0:T(256)S(1)} %le.48, s32[8192]{0:T(1024)S(1)} %convert_reduce_fusion, s32[256]{0:T(256)S(1)} %eq.54, bf16[8192,576]{0,1:T(8,128)(2,1)} %all-gather.4.cloned.1.call-done, f32[256,32]{1,0:T(8,128)S(1)} %bitcast.122, f32[256,32]{1,0:T(8,128)S(1)} %bitcast.121, ...), kind=kOutput, calls=%fused_computation.4 | convolution fusion | flops 2426994432 | bytes 18451456 | tf_op jit(solution)/shard_map/ra,ka->rk/dot_general | solution.py:158
  109.0 2.8 fusion.3
  111.9 6.2 %fusion.35 = f32[256,512]{1,0:T(8,128)S(1)} fusion(bf16[8192,576]{0,1:T(8,128)(2,1)} %all-gather.4.cloned.1.call-done, f32[256,8192]{1,0:T(8,128)S(1)} %get-tuple-element.29, f32[256]{0:T(256)S(1)} %broadcast_maximum_fusion, s32[256]{0:T(256)S(1)} %le.48, s32[8192]{0:T(1024)S(1)} %convert_reduce_fusion, s32[256]{0:T(256)S(1)} %eq.54, f32[256]{0:T(256)S(1)} %fusion.3), kind=kOutput, calls=%fused_computation.39 | convolution fusion | flops 2160197632 | bytes 17338368 | tf_op jit(solution)/shard_map/dot_general | solution.py:163
  124.9 20.3 %reduce-scatter.4.cloned.1.call-done = bf16[128,512]{1,0:T(8,128)(2,1)} async-done(((bf16[128,2048]{1,0:T(8,128)(2,1)}), bf16[128,512]{1,0:T(8,128)(2,1)}) %reduce-scatter.4.cloned.1.call-update) | async-done | bytes 131088 | tf_op jit(solution)/shard_map/reduce_scatter | solution.py:179
  146.2 8.5 %psum.7 = f32[128,1]{0,1:T(1,128)S(1)} all-reduce(f32[128,1]{0,1:T(1,128)S(1)} %bitcast.126), channel_id=1, replica_groups=mesh['seq'=64,'tp'=4] {'tp'}, use_global_device_ids=true, to_apply=%region_13.14 | all-reduce | flops 128 | bytes 1024 | tf_op jit(solution)/shard_map/psum | solution.py:184
  156.3 1.9 fusion.78
  158.2 37.8 %shard_map.140 = bf16[64,12,512]{2,1,0:T(8,128)(2,1)} custom-call(bf16[64,12,512]{2,1,0:T(8,128)(2,1)} %get-tuple-element.4.x_ref), custom_call_target="tpu_custom_call" | custom-call | tf_op jit(solution)/shard_map/pallas_call | solution.py:91
  196.0 2.1 reshape.221
  198.1 37.7 %shard_map.142 = bf16[64,12,512]{2,1,0:T(8,128)(2,1)} custom-call(bf16[64,12,512]{2,1,0:T(8,128)(2,1)} %get-tuple-element.5.x_ref), custom_call_target="tpu_custom_call" | custom-call | tf_op jit(solution)/shard_map/pallas_call | solution.py:91
  235.9 2.1 reshape.223
  239.8 4.3 fusion.21
  244.1 8.0 %convolution_convert_fusion.1 = bf16[768,2048]{1,0:T(8,128)(2,1)} fusion(bf16[1,352,2048]{2,1,0:T(8,128)(2,1)S(1)} %copy-done.13, bf16[768,2048]{1,0:T(8,128)(2,1)} %all-gather.6.cloned.1.call-done, bf16[1,2048,352]{1,2,0:T(8,128)(2,1)} %param.24, f32[768,352]{0,1:T(8,128)} %fusion.21), kind=kOutput, calls=%fused_computation.17 | convolution fusion | flops 2217787392 | bytes 10256384 | tf_op jit(solution)/shard_map/dot_general | solution.py:216
  252.4 31.3 %all-gather.8.cloned.1.call-done = bf16[768,2048]{1,0:T(8,128)(2,1)} async-done(((bf16[768,512]{1,0:T(8,128)(2,1)}), bf16[768,2048]{1,0:T(8,128)(2,1)}) %all-gather.8.cloned.1.call-update) | async-done | bytes 3145744 | tf_op jit(solution)/shard_map/all_gather | solution.py:212
  283.7 4.3 fusion.19
  288.0 8.1 %convolution_convert_fusion = bf16[768,2048]{1,0:T(8,128)(2,1)} fusion(bf16[1,352,2048]{2,1,0:T(8,128)(2,1)S(1)} %copy-done.13, bf16[768,2048]{1,0:T(8,128)(2,1)} %all-gather.8.cloned.1.call-done, bf16[1,2048,352]{1,2,0:T(8,128)(2,1)} %param.24, f32[768,352]{0,1:T(8,128)} %fusion.19), kind=kOutput, calls=%fused_computation.16 | convolution fusion | flops 2217787392 | bytes 10256384 | tf_op jit(solution)/shard_map/dot_general | solution.py:216
  297.3 29.8 %reduce-scatter.6.cloned.1.call-done = bf16[768,512]{1,0:T(8,128)(2,1)} async-done(((bf16[768,2048]{1,0:T(8,128)(2,1)}), bf16[768,512]{1,0:T(8,128)(2,1)}) %reduce-scatter.6.cloned.1.call-update) | async-done | bytes 786448 | tf_op jit(solution)/shard_map/reduce_scatter | solution.py:219
  327.2 2.2 reshape.222.x_ref
  329.3 37.8 %shard_map.141 = bf16[64,12,512]{2,1,0:T(8,128)(2,1)} custom-call(bf16[64,12,512]{2,1,0:T(8,128)(2,1)} %reshape.222.x_ref), custom_call_target="tpu_custom_call" | custom-call | tf_op jit(solution)/shard_map/pallas_call | solution.py:91
  367.2 3.0 reduce-scatter.8.cloned.1.call-done
  370.2 2.2 reshape.224.x_ref
  372.4 37.8 %shard_map.143 = bf16[64,12,512]{2,1,0:T(8,128)(2,1)} custom-call(bf16[64,12,512]{2,1,0:T(8,128)(2,1)} %reshape.224.x_ref), custom_call_target="tpu_custom_call" | custom-call | tf_op jit(solution)/shard_map/pallas_call | solution.py:91
  411.9 2.7 gather_fusion
  417.3 13.4 %all_gather.15 = bf16[128,2048]{1,0:T(8,128)(2,1)S(1)} all-gather(bf16[128,512]{1,0:T(8,128)(2,1)S(1)} %fusion.53), channel_id=1, replica_groups=mesh['seq'=64,'tp'=4] {'tp'}, dimensions={1}, use_global_device_ids=true | all-gather | bytes 655360 | tf_op jit(solution)/shard_map/all_gather | solution.py:234
  (95 shorter events, 26.4 us)
Async XLA Ops:
  7.2 1.9 copy-start
  7.2 4.8 %copy-start.3 = (bf16[128,2048]{1,0:T(8,128)(2,1)S(1)}, bf16[128,2048]{1,0:T(8,128)(2,1)}, u32[]{:S(2)}) copy-start(bf16[128,2048]{1,0:T(8,128)(2,1)} %param.13) | copy-start | bytes 1572868
  7.2 3.9 copy-start.9
  7.2 95.1 %all-gather.4.cloned.1.call-start = ((), (), s32[]{:S(2)}) async-start(), calls=%async_computation.3 | async-start | bytes 9584640 | tf_op jit(solution)/shard_map/all_gather | solution.py:150
  10.9 3.9 copy-start.6
  12.0 133.2 %reduce-scatter.4.cloned.1.call-start = ((), (), s32[]{:S(2)}) async-start(), calls=%async_computation.4 | async-start | bytes 655360 | tf_op jit(solution)/shard_map/reduce_scatter | solution.py:179
  118.1 1.2 copy-start.5
  118.1 2.4 copy-start.7
  120.5 119.3 %all-gather.6.cloned.1.call-start = ((), (), s32[]{:S(2)}) async-start(), calls=%async_computation.5 | async-start | bytes 3932160 | tf_op jit(solution)/shard_map/all_gather | solution.py:212
  198.1 85.6 %all-gather.8.cloned.1.call-start = ((), (), s32[]{:S(2)}) async-start(), calls=%async_computation.7 | async-start | bytes 3932160 | tf_op jit(solution)/shard_map/all_gather | solution.py:212
  198.1 41.7 %copy-start.12 = (bf16[1,2048,352]{1,2,0:T(8,128)(2,1)S(1)}, bf16[1,2048,352]{1,2,0:T(8,128)(2,1)}, u32[]{:S(2)}) copy-start(bf16[1,2048,352]{1,2,0:T(8,128)(2,1)} %param.23) | copy-start | bytes 4325380
  238.0 6.1 %copy-start.13 = (bf16[1,352,2048]{2,1,0:T(8,128)(2,1)S(1)}, bf16[1,352,2048]{2,1,0:T(8,128)(2,1)}, u32[]{:S(2)}) copy-start(bf16[1,352,2048]{2,1,0:T(8,128)(2,1)} %param.25) | copy-start | bytes 4325380
  238.0 89.2 %reduce-scatter.6.cloned.1.call-start = ((), (), s32[]{:S(2)}) async-start(), calls=%async_computation.6 | async-start | bytes 3932160 | tf_op jit(solution)/shard_map/reduce_scatter | solution.py:219
  252.1 118.1 %reduce-scatter.8.cloned.1.call-start = ((), (), s32[]{:S(2)}) async-start(), calls=%async_computation.8 | async-start | bytes 3932160 | tf_op jit(solution)/shard_map/reduce_scatter | solution.py:219
  296.1 0.7 copy-start.8
  367.2 43.0 %copy-start.2 = (bf16[64,12,512]{2,1,0:T(8,128)(2,1)S(1)}, bf16[64,12,512]{2,1,0:T(8,128)(2,1)}, u32[]{:S(2)}) copy-start(bf16[64,12,512]{2,1,0:T(8,128)(2,1)} %shard_map.141) | copy-start | bytes 2359300
  414.6 1.5 copy-start.4
  414.9 1.2 copy-start.10
  414.9 1.2 copy-start.11
  414.9 16.6 %copy-start.1 = (bf16[2048,576]{0,1:T(8,128)(2,1)S(1)}, bf16[2048,576]{0,1:T(8,128)(2,1)}, u32[]{:S(2)}) copy-start(bf16[2048,576]{0,1:T(8,128)(2,1)} %param.16) | copy-start | bytes 7077892
Sparse Core Ops, SparseCore 0:
  12.1 90.1 all-gather.3
  120.6 24.5 reduce-scatter.3
  198.2 41.5 all-gather.5
  241.5 42.2 all-gather.7
  286.1 41.0 reduce-scatter.5
  329.6 40.5 reduce-scatter.7

commit v5 on v4

--- a/solution.py
+++ b/solution.py
@@ -201,27 +201,19 @@
         jnp.bfloat16
     )
     outgoing = outgoing.reshape(experts, capacity, col_width)
-    chunk_count = 2
-    chunk_slots = capacity // chunk_count
-    returned_chunks = []
-    for chunk in range(chunk_count):
-        sending = outgoing[:, chunk * chunk_slots : (chunk + 1) * chunk_slots]
-        received = seq_exchange(sending)
-        sources, slot_count, _ = received.shape
-        flat_part = received.reshape(sources * slot_count, col_width)
-        flat_rows = lax.all_gather(flat_part, "tp", axis=1, tiled=True)
-        gate_act = jnp.dot(flat_rows, expert_gate[0], preferred_element_type=jnp.float32)
-        up_act = jnp.dot(flat_rows, expert_up[0], preferred_element_type=jnp.float32)
-        hidden_units = (jax.nn.silu(gate_act) * up_act).astype(jnp.bfloat16)
-        expert_out = jnp.dot(
-            hidden_units, expert_down[0], preferred_element_type=jnp.float32
-        ).astype(jnp.bfloat16)
-        expert_sum = lax.psum_scatter(expert_out, "tp", scatter_dimension=1, tiled=True)
-        expert_sum = expert_sum.reshape(sources, slot_count, col_width)
-        returned_chunks.append(
-            seq_exchange(expert_sum)
-        )
-    returned = jnp.concatenate(returned_chunks, axis=1)
+    received = seq_exchange(outgoing)
+    sources, slot_count, _ = received.shape
+    flat_part = received.reshape(sources * slot_count, col_width)
+    flat_rows = lax.all_gather(flat_part, "tp", axis=1, tiled=True)
+    gate_act = jnp.dot(flat_rows, expert_gate[0], preferred_element_type=jnp.float32)
+    up_act = jnp.dot(flat_rows, expert_up[0], preferred_element_type=jnp.float32)
+    hidden_units = (jax.nn.silu(gate_act) * up_act).astype(jnp.bfloat16)
+    expert_out = jnp.dot(hidden_units, expert_down[0], preferred_element_type=jnp.float32).astype(
+        jnp.bfloat16
+    )
+    expert_sum = lax.psum_scatter(expert_out, "tp", scatter_dimension=1, tiled=True)
+    expert_sum = expert_sum.reshape(sources, slot_count, col_width)
+    returned = seq_exchange(expert_sum)
     gathered = returned.reshape(experts * capacity, col_width)[slot_index].reshape(
         tok_count, top_k, col_width
     )

time: 442 us -> 447 us (1.011)
  waiting for transfers between devices: 173 us -> 237 us
  Pallas kernels: 151 us -> 97.1 us
    pallas_call x4 -> x2, Pallas kernels: 151 us -> 97.1 us  [seq_exchange(): pl.pallas_call(_exchange_body, out_shape=jax.ShapeDtypeStruct(x.shape, x....]
    all_gather x2 -> x1, waiting for transfers between devices: 33.1 us -> 68.2 us  [on_device(): flat_rows = lax.all_gather(flat_part, 'tp', axis=1, tiled=True)]
    reduce_scatter x2 -> x1, waiting for transfers between devices: 32.8 us -> 66.1 us  [on_device(): lax.psum_scatter(expert_out, 'tp', scatter_dimension=1, tiled=True)]
    reshape x4 -> x0, local copies, waits for them, and re-layouts: 8.47 us -> none  [the longest x2 4.33 us: on_device(): expert_sum = expert_sum.reshape(sources, slot_count, col_width)]
    dot_general x2 -> x1, matrix products: 16.1 us -> 12.3 us  [on_device(): jnp.dot(hidden_units, expert_down[0], preferred_element_type=jnp.float32)]
  transfers between devices with their start and end apart: 6 -> 4, of which waited for: 6 -> 4; matrix products, arithmetic and copies ran while one was open for 9% -> 3% of each run, Pallas kernels for 17% -> 0%
where the time goes in v5:
time: 447 us; the launch traced here: 443 us
  waiting for transfers between devices  237 us (53%)
  Pallas kernels  97.1 us (22%)
  matrix products  44.6 us (10%)
  blocking collectives  22 us (5%)
  local copies, waits for them, and re-layouts  16.8 us (4%)
  between operations  14.1 us (3%)
  other arithmetic  11.5 us (3%)
    pallas_call x2, Pallas kernels, seq_exchange(): pl.pallas_call(_exchange_body, out_shape=jax.ShapeDtypeStruct(x.shape, x....  97.1 us
    all_gather x1, waiting for transfers between devices, on_device(): shard_rows = lax.all_gather(latent, 'seq', axis=0, tiled=True)  82.1 us
    all_gather x1, waiting for transfers between devices, on_device(): flat_rows = lax.all_gather(flat_part, 'tp', axis=1, tiled=True)  68.2 us
    reduce_scatter x1, waiting for transfers between devices, on_device(): lax.psum_scatter(expert_out, 'tp', scatter_dimension=1, tiled=True)  66.1 us
    reduce_scatter x1, waiting for transfers between devices, on_device(): lax.psum_scatter(partial_attention.astype(jnp.bfloat16), 'tp', scatter_di...  20.2 us
    all_gather x1, blocking collectives, on_device(): layer_out = lax.all_gather(layer_part, 'tp', axis=1, tiled=True)  13.4 us
    dot_general x1, matrix products, on_device(): jnp.dot(hidden_units, expert_down[0], preferred_element_type=jnp.float32)  12.3 us
  transfers between devices with their start and end apart: 4, of which 4 were waited for; matrix products, arithmetic and copies ran while one was open for 3% of the time, Pallas kernels for 0%

profile of v5, /device:TPU:32, one launch (start us, length us, event | category | flops | bytes accessed | tf_op | source)
XLA Modules:
  0.0 442.8 jit_solution(2925174703143091877)
XLA Ops:
  9.0 1.9 fusion.57
  12.1 1.8 convolution_convert_fusion.3
  18.9 1.2 concatenate.14
  20.3 82.1 %all-gather.3.cloned.1.call-done = bf16[8192,576]{0,1:T(8,128)(2,1)} async-done(((bf16[128,576]{0,1:T(8,128)(2,1)}), bf16[8192,576]{0,1:T(8,128)(2,1)}) %all-gather.3.cloned.1.call-update) | async-done | bytes 9437200 | tf_op jit(solution)/shard_map/all_gather | solution.py:150
  102.3 7.0 %select_reduce_fusion = (f32[256]{0:T(256)S(1)}, f32[256,8192]{1,0:T(8,128)S(1)}) fusion(s32[256]{0:T(256)S(1)} %le.48, s32[8192]{0:T(1024)S(1)} %convert_reduce_fusion, s32[256]{0:T(256)S(1)} %eq.54, bf16[8192,576]{0,1:T(8,128)(2,1)} %all-gather.3.cloned.1.call-done, f32[256,32]{1,0:T(8,128)} %bitcast.108, f32[256,32]{1,0:T(8,128)} %bitcast.107, ...), kind=kOutput, calls=%fused_computation.4 | convolution fusion | flops 2426994432 | bytes 18451456 | tf_op jit(solution)/shard_map/ra,ka->rk/dot_general | solution.py:158
  109.3 2.8 fusion.3
  112.1 7.0 %fusion.18 = f32[256,512]{1,0:T(8,128)} fusion(bf16[8192,576]{0,1:T(8,128)(2,1)} %all-gather.3.cloned.1.call-done, f32[256,8192]{1,0:T(8,128)S(1)} %get-tuple-element.27, f32[256]{0:T(256)S(1)} %broadcast_maximum_fusion, s32[256]{0:T(256)S(1)} %le.48, s32[8192]{0:T(1024)S(1)} %convert_reduce_fusion, s32[256]{0:T(256)S(1)} %eq.54, f32[256]{0:T(256)S(1)} %fusion.3), kind=kOutput, calls=%fused_computation.29 | convolution fusion | flops 2160197632 | bytes 17338368 | tf_op jit(solution)/shard_map/dot_general | solution.py:163
  119.2 1.4 reshape.211
  120.5 1.4 convolution_convert_fusion.4
  122.0 2.4 convolution_convert_fusion.2
  124.8 1.8 reduce-window.19
  128.8 20.2 %reduce-scatter.3.cloned.1.call-done = bf16[128,512]{1,0:T(8,128)(2,1)} async-done(((bf16[128,2048]{1,0:T(8,128)(2,1)}), bf16[128,512]{1,0:T(8,128)(2,1)}) %reduce-scatter.3.cloned.1.call-update) | async-done | bytes 131088 | tf_op jit(solution)/shard_map/reduce_scatter | solution.py:179
  150.0 8.5 %psum.7 = f32[128,1]{0,1:T(1,128)S(1)} all-reduce(f32[128,1]{0,1:T(1,128)S(1)} %bitcast.112), channel_id=1, replica_groups=mesh['seq'=64,'tp'=4] {'tp'}, use_global_device_ids=true, to_apply=%region_13.14 | all-reduce | flops 128 | bytes 1024 | tf_op jit(solution)/shard_map/psum | solution.py:184
  158.6 2.7 convolution_convert_fusion.1
  161.3 48.5 %shard_map.140 = bf16[64,24,512]{2,1,0:T(8,128)(2,1)} custom-call(bf16[64,24,512]{2,1,0:T(8,128)(2,1)} %bitcast.102), custom_call_target="tpu_custom_call" | custom-call | tf_op jit(solution)/shard_map/pallas_call | solution.py:91
  209.9 68.2 %all-gather.5.cloned.1.call-done = bf16[1536,2048]{1,0:T(8,128)(2,1)} async-done(((bf16[1536,512]{1,0:T(8,128)(2,1)}), bf16[1536,2048]{1,0:T(8,128)(2,1)}) %all-gather.5.cloned.1.call-update) | async-done | bytes 6291472 | tf_op jit(solution)/shard_map/all_gather | solution.py:207
  278.1 7.0 %fusion.16 = f32[1536,352]{0,1:T(8,128)} fusion(bf16[1536,2048]{1,0:T(8,128)(2,1)} %all-gather.5.cloned.1.call-done, bf16[1,2048,352]{1,2,0:T(8,128)(2,1)} %param.23), kind=kOutput, calls=%fused_computation.24 | convolution fusion | flops 2214592512 | bytes 9895936 | tf_op jit(solution)/shard_map/dot_general | solution.py:208
  285.0 12.3 %convolution_convert_fusion = bf16[1536,2048]{1,0:T(8,128)(2,1)} fusion(bf16[1,352,2048]{2,1,0:T(8,128)(2,1)} %param.25, bf16[1536,2048]{1,0:T(8,128)(2,1)} %all-gather.5.cloned.1.call-done, f32[1536,352]{0,1:T(8,128)} %fusion.16, bf16[1,2048,352]{1,2,0:T(8,128)(2,1)} %param.24), kind=kOutput, calls=%fused_computation.7 | convolution fusion | flops 4435574784 | bytes 17629184 | tf_op jit(solution)/shard_map/dot_general | solution.py:211
  298.6 66.1 %reduce-scatter.5.cloned.1.call-done = bf16[1536,512]{1,0:T(8,128)(2,1)} async-done(((bf16[1536,2048]{1,0:T(8,128)(2,1)}), bf16[1536,512]{1,0:T(8,128)(2,1)}) %reduce-scatter.5.cloned.1.call-update) | async-done | bytes 1572880 | tf_op jit(solution)/shard_map/reduce_scatter | solution.py:214
  364.7 48.6 %shard_map.141 = bf16[64,24,512]{2,1,0:T(8,128)(2,1)} custom-call(bf16[64,24,512]{2,1,0:T(8,128)(2,1)} %bitcast.103), custom_call_target="tpu_custom_call" | custom-call | tf_op jit(solution)/shard_map/pallas_call | solution.py:91
  413.3 5.0 %gather_fusion = bf16[768,512]{1,0:T(8,128)(2,1)} fusion(bf16[1536,512]{1,0:T(8,128)(2,1)} %bitcast.100, s32[1024]{0:T(1024)S(1)} %pad_clamp_fusion), kind=kCustom, calls=%fused_computation | custom fusion | bytes 1575936 | tf_op jit(solution)/shard_map/gather | solution.py:217
  418.3 1.4 reshape.218
  420.9 1.2 fusion.32
  422.0 13.4 %all_gather.11 = bf16[128,2048]{1,0:T(8,128)(2,1)S(1)} all-gather(bf16[128,512]{1,0:T(8,128)(2,1)S(1)} %fusion.32), channel_id=1, replica_groups=mesh['seq'=64,'tp'=4] {'tp'}, dimensions={1}, use_global_device_ids=true | all-gather | bytes 655360 | tf_op jit(solution)/shard_map/all_gather | solution.py:226
  (69 shorter events, 14.9 us)
Async XLA Ops:
  7.2 1.9 copy-start
  7.2 4.9 %copy-start.1 = (bf16[128,2048]{1,0:T(8,128)(2,1)S(1)}, bf16[128,2048]{1,0:T(8,128)(2,1)}, u32[]{:S(2)}) copy-start(bf16[128,2048]{1,0:T(8,128)(2,1)} %param.13) | copy-start | bytes 1572868
  7.2 4.0 copy-start.6
  7.2 95.1 %all-gather.3.cloned.1.call-start = ((), (), s32[]{:S(2)}) async-start(), calls=%async_computation.2 | async-start | bytes 9584640 | tf_op jit(solution)/shard_map/all_gather | solution.py:150
  9.0 8.4 %copy-start.3 = (bf16[2,512,256]{2,1,0:T(8,128)(2,1)S(1)}, bf16[2,512,256]{2,1,0:T(8,128)(2,1)}, u32[]{:S(2)}) copy-start(bf16[2,512,256]{2,1,0:T(8,128)(2,1)} %param.18) | copy-start | bytes 1572868
  12.0 137.0 %reduce-scatter.3.cloned.1.call-start = ((), (), s32[]{:S(2)}) async-start(), calls=%async_computation.3 | async-start | bytes 655360 | tf_op jit(solution)/shard_map/reduce_scatter | solution.py:179
  119.2 5.2 %copy-start.4 = (s32[128,6]{0,1:T(8,128)S(1)}, s32[128,6]{0,1:T(8,128)}, u32[]{:S(2)}) copy-start(s32[128,6]{0,1:T(8,128)} %param.21) | copy-start | bytes 9220
  124.4 153.7 %all-gather.5.cloned.1.call-start = ((), (), s32[]{:S(2)}) async-start(), calls=%async_computation.4 | async-start | bytes 7864320 | tf_op jit(solution)/shard_map/all_gather | solution.py:207
  209.8 154.9 %reduce-scatter.5.cloned.1.call-start = ((), (), s32[]{:S(2)}) async-start(), calls=%async_computation.5 | async-start | bytes 7864320 | tf_op jit(solution)/shard_map/reduce_scatter | solution.py:214
  297.3 0.7 copy-start.5
  418.3 2.6 copy-start.2
  419.6 1.2 copy-start.7
  419.7 1.2 copy-start.8
Sparse Core Ops, SparseCore 0:
  12.1 90.1 all-gather.2
  124.5 24.4 reduce-scatter.2
  209.9 68.1 all-gather.4
  297.5 67.1 reduce-scatter.4

commit v6 on v2

--- a/solution.py
+++ b/solution.py
@@ -83,7 +83,9 @@
     row_segment = jnp.repeat(segment, head_count)
     row_index = jnp.repeat(token_index, head_count)
     row_total = tok_count * head_count
-    shard_rows = lax.all_gather(latent, "seq", axis=0, tiled=True)
+    quarter_rows = tok_count // lax.axis_size("tp")
+    own_rows = lax.dynamic_slice_in_dim(latent, lax.axis_index("tp") * quarter_rows, quarter_rows, 0)
+    shard_rows = lax.all_gather(own_rows, ("seq", "tp"), axis=0, tiled=True)
     key_count = shard_rows.shape[0]
     key_index = jnp.arange(key_count, dtype=jnp.int32)
     key_segment, unused = place(key_index, lengths)

time: 434 us -> 463 us (1.067)
  waiting for transfers between devices: 228 us -> 256 us
    all_gather x1, waiting for transfers between devices: 86.3 us -> 117 us  [on_device(): shard_rows = lax.all_gather(own_rows, ('seq', 'tp'), axis=0, tiled=True)]
where the time goes in v6:
time: 463 us; the launch traced here: 462 us
  waiting for transfers between devices  256 us (55%)
  blocking collectives  94.5 us (20%)
  matrix products  45.4 us (10%)
  starting transfers between devices  21.8 us (5%)
  local copies, waits for them, and re-layouts  17.9 us (4%)
  between operations  14.6 us (3%)
  other arithmetic  11.7 us (3%)
    all_gather x1, waiting for transfers between devices, on_device(): shard_rows = lax.all_gather(own_rows, ('seq', 'tp'), axis=0, tiled=True)  117 us
    all_to_all x2, blocking collectives, on_device(): lax.all_to_all(sending, 'seq', split_axis=0, concat_axis=0, tiled=True)  72.7 us
    reduce_scatter x2, waiting for transfers between devices, on_device(): lax.psum_scatter(expert_out, 'tp', scatter_dimension=1, tiled=True)  61.1 us
    all_gather x2, waiting for transfers between devices, on_device(): flat_rows = lax.all_gather(flat_part, 'tp', axis=1, tiled=True)  33.5 us
    all_to_all x2, waiting for transfers between devices, on_device(): lax.all_to_all(expert_sum, 'seq', split_axis=0, concat_axis=0, tiled=True)  27.1 us
    all_to_all x2, starting transfers between devices, on_device(): lax.all_to_all(expert_sum, 'seq', split_axis=0, concat_axis=0, tiled=True)  21.2 us
    dot_general x2, matrix products, on_device(): jnp.dot(hidden_units, expert_down[0], preferred_element_type=jnp.float32)  17 us
    reduce_scatter x1, waiting for transfers between devices, on_device(): lax.psum_scatter(partial_attention.astype(jnp.bfloat16), 'tp', scatter_di...  16.8 us
  transfers between devices with their start and end apart: 8, of which 7 were waited for; matrix products, arithmetic and copies ran while one was open for 9% of the time, Pallas kernels for 0%

profile of v6, /device:TPU:32, one launch (start us, length us, event | category | flops | bytes accessed | tf_op | source)
XLA Modules:
  0.0 461.9 jit_solution(12373266124717227379)
XLA Ops:
  9.0 1.9 fusion.80
  16.9 117.4 %all-gather.4.cloned.1.call-done = bf16[8192,576]{1,0:T(8,128)(2,1)} async-done(((bf16[32,576]{1,0:T(8,128)(2,1)}), bf16[8192,576]{1,0:T(8,128)(2,1)}) %all-gather.4.cloned.1.call-update) | async-done | bytes 9437200 | tf_op jit(solution)/shard_map/all_gather | solution.py:88
  134.3 7.1 %select_reduce_fusion = (f32[256]{0:T(256)S(1)}, f32[256,8192]{1,0:T(8,128)S(1)}) fusion(s32[256]{0:T(256)S(1)} %le.48, s32[8192]{0:T(1024)S(1)} %convert_reduce_fusion, s32[256]{0:T(256)S(1)} %eq.54, bf16[8192,576]{1,0:T(8,128)(2,1)} %all-gather.4.cloned.1.call-done, f32[256,32]{1,0:T(8,128)S(1)} %bitcast.122, f32[256,32]{1,0:T(8,128)S(1)} %bitcast.121, ...), kind=kOutput, calls=%fused_computation.4 | convolution fusion | flops 2426994432 | bytes 18451456 | tf_op jit(solution)/shard_map/ra,ka->rk/dot_general | solution.py:96
  141.4 2.7 fusion.3
  144.1 5.8 %fusion.35 = f32[256,512]{1,0:T(8,128)S(1)} fusion(bf16[8192,576]{1,0:T(8,128)(2,1)} %all-gather.4.cloned.1.call-done, f32[256,8192]{1,0:T(8,128)S(1)} %get-tuple-element.29, f32[256]{0:T(256)S(1)} %broadcast_maximum_fusion, s32[256]{0:T(256)S(1)} %le.48, s32[8192]{0:T(1024)S(1)} %convert_reduce_fusion, s32[256]{0:T(256)S(1)} %eq.54, f32[256]{0:T(256)S(1)} %fusion.3), kind=kOutput, calls=%fused_computation.39 | convolution fusion | flops 2160197632 | bytes 17338368 | tf_op jit(solution)/shard_map/dot_general | solution.py:101
  157.0 16.8 %reduce-scatter.4.cloned.1.call-done = bf16[128,512]{1,0:T(8,128)(2,1)} async-done(((bf16[128,2048]{1,0:T(8,128)(2,1)}), bf16[128,512]{1,0:T(8,128)(2,1)}) %reduce-scatter.4.cloned.1.call-update) | async-done | bytes 131088 | tf_op jit(solution)/shard_map/reduce_scatter | solution.py:117
  174.8 8.4 %psum.7 = f32[128,1]{0,1:T(1,128)S(1)} all-reduce(f32[128,1]{0,1:T(1,128)S(1)} %bitcast.126), channel_id=1, replica_groups=mesh['seq'=64,'tp'=4] {'tp'}, use_global_device_ids=true, to_apply=%region_13.14 | all-reduce | flops 128 | bytes 1024 | tf_op jit(solution)/shard_map/psum | solution.py:122
  185.2 38.1 %all_to_all.20 = bf16[64,12,512]{2,1,0:T(8,128)(2,1)S(1)} all-to-all(bf16[64,12,512]{2,1,0:T(8,128)(2,1)S(1)} %get-tuple-element.4), channel_id=1, replica_groups=mesh['seq'=64,'tp'=4] {'seq'}, dimensions={0} | all-to-all | bytes 1572864 | tf_op jit(solution)/shard_map/all_to_all | solution.py:147
  224.5 34.5 %all_to_all.21 = bf16[64,12,512]{2,1,0:T(8,128)(2,1)S(1)} all-to-all(bf16[64,12,512]{2,1,0:T(8,128)(2,1)S(1)} %get-tuple-element.5), channel_id=1, replica_groups=mesh['seq'=64,'tp'=4] {'seq'}, dimensions={0} | all-to-all | bytes 1572864 | tf_op jit(solution)/shard_map/all_to_all | solution.py:147
  260.1 2.6 all-gather.6.cloned.1.call-done
  262.7 4.2 fusion.21
  266.9 8.5 %convolution_convert_fusion.1 = bf16[768,2048]{1,0:T(8,128)(2,1)} fusion(bf16[1,352,2048]{2,1,0:T(8,128)(2,1)} %param.25, bf16[768,2048]{1,0:T(8,128)(2,1)} %all-gather.6.cloned.1.call-done, bf16[1,2048,352]{1,2,0:T(8,128)(2,1)} %param.24, f32[768,352]{0,1:T(8,128)} %fusion.21), kind=kOutput, calls=%fused_computation.17 | convolution fusion | flops 2217787392 | bytes 10256384 | tf_op jit(solution)/shard_map/dot_general | solution.py:154
  275.7 30.9 %all-gather.8.cloned.1.call-done = bf16[768,2048]{1,0:T(8,128)(2,1)} async-done(((bf16[768,512]{1,0:T(8,128)(2,1)}), bf16[768,2048]{1,0:T(8,128)(2,1)}) %all-gather.8.cloned.1.call-update) | async-done | bytes 3145744 | tf_op jit(solution)/shard_map/all_gather | solution.py:150
  306.6 4.2 fusion.19
  310.8 8.5 %convolution_convert_fusion = bf16[768,2048]{1,0:T(8,128)(2,1)} fusion(bf16[1,352,2048]{2,1,0:T(8,128)(2,1)} %param.25, bf16[768,2048]{1,0:T(8,128)(2,1)} %all-gather.8.cloned.1.call-done, bf16[1,2048,352]{1,2,0:T(8,128)(2,1)} %param.24, f32[768,352]{0,1:T(8,128)} %fusion.19), kind=kOutput, calls=%fused_computation.16 | convolution fusion | flops 2217787392 | bytes 10256384 | tf_op jit(solution)/shard_map/dot_general | solution.py:154
  319.4 30.7 %reduce-scatter.6.cloned.1.call-done = bf16[768,512]{1,0:T(8,128)(2,1)} async-done(((bf16[768,2048]{1,0:T(8,128)(2,1)}), bf16[768,512]{1,0:T(8,128)(2,1)}) %reduce-scatter.6.cloned.1.call-update) | async-done | bytes 786448 | tf_op jit(solution)/shard_map/reduce_scatter | solution.py:157
  350.1 2.2 reshape.222
  352.3 10.5 %all-to-all-start.1 = ((bf16[64,12,512]{2,1,0:T(8,128)(2,1)}), bf16[64,12,512]{2,1,0:T(8,128)(2,1)S(1)}, u32[]{:S(2)}, u32[]{:S(2)}) async-start(bf16[64,12,512]{2,1,0:T(8,128)(2,1)} %reshape.222), calls=%async_computation.3 | async-start | bytes 2097152 | tf_op jit(solution)/shard_map/all_to_all | solution.py:160
  362.8 30.3 %reduce-scatter.8.cloned.1.call-done = bf16[768,512]{1,0:T(8,128)(2,1)} async-done(((bf16[768,2048]{1,0:T(8,128)(2,1)}), bf16[768,512]{1,0:T(8,128)(2,1)}) %reduce-scatter.8.cloned.1.call-update) | async-done | bytes 786448 | tf_op jit(solution)/shard_map/reduce_scatter | solution.py:157
  393.1 2.1 reshape.224
  395.2 10.7 %all-to-all-start.3 = ((bf16[64,12,512]{2,1,0:T(8,128)(2,1)}), bf16[64,12,512]{2,1,0:T(8,128)(2,1)}, u32[]{:S(2)}, u32[]{:S(2)}) async-start(bf16[64,12,512]{2,1,0:T(8,128)(2,1)} %reshape.224), calls=%async_computation.6 | async-start | bytes 2097152 | tf_op jit(solution)/shard_map/all_to_all | solution.py:160
  406.6 27.1 %all-to-all-done.3 = bf16[64,12,512]{2,1,0:T(8,128)(2,1)} async-done(((bf16[64,12,512]{2,1,0:T(8,128)(2,1)}), bf16[64,12,512]{2,1,0:T(8,128)(2,1)}, u32[]{:S(2)}, u32[]{:S(2)}) %all-to-all-start.3) | async-done | bytes 786464 | tf_op jit(solution)/shard_map/all_to_all | solution.py:160
  435.4 2.7 gather_fusion
  440.8 13.4 %all_gather.15 = bf16[128,2048]{1,0:T(8,128)(2,1)S(1)} all-gather(bf16[128,512]{1,0:T(8,128)(2,1)S(1)} %fusion.53), channel_id=1, replica_groups=mesh['seq'=64,'tp'=4] {'tp'}, dimensions={1}, use_global_device_ids=true | all-gather | bytes 655360 | tf_op jit(solution)/shard_map/all_gather | solution.py:172
  (97 shorter events, 25.9 us)
Async XLA Ops:
  7.2 1.8 copy-start
  7.2 4.0 copy-start.9
  7.2 127.1 %all-gather.4.cloned.1.call-start = ((), (), s32[]{:S(2)}) async-start(), calls=%async_computation.7 | async-start | bytes 10526720 | tf_op jit(solution)/shard_map/all_gather | solution.py:88
  9.0 3.9 copy-start.2
  10.9 4.7 %copy-start.6 = (bf16[2,512,256]{2,1,0:T(8,128)(2,1)S(1)}, bf16[2,512,256]{2,1,0:T(8,128)(2,1)}, u32[]{:S(2)}) copy-start(bf16[2,512,256]{2,1,0:T(8,128)(2,1)} %param.18) | copy-start | bytes 1572868
  11.3 0.7 copy-start.5
  12.9 160.9 %reduce-scatter.4.cloned.1.call-start = ((), (), s32[]{:S(2)}) async-start(), calls=%async_computation.8 | async-start | bytes 655360 | tf_op jit(solution)/shard_map/reduce_scatter | solution.py:117
  150.0 1.2 copy-start.4
  150.0 2.6 copy-start.7
  152.3 110.4 %all-gather.6.cloned.1.call-start = ((), (), s32[]{:S(2)}) async-start(), calls=%async_computation.9 | async-start | bytes 3932160 | tf_op jit(solution)/shard_map/all_gather | solution.py:150
  224.4 82.2 %all-gather.8.cloned.1.call-start = ((), (), s32[]{:S(2)}) async-start(), calls=%async_computation.11 | async-start | bytes 3932160 | tf_op jit(solution)/shard_map/all_gather | solution.py:150
  259.0 3.7 copy-start.12
  260.1 90.0 %reduce-scatter.6.cloned.1.call-start = ((), (), s32[]{:S(2)}) async-start(), calls=%async_computation.10 | async-start | bytes 3932160 | tf_op jit(solution)/shard_map/reduce_scatter | solution.py:157
  275.4 117.7 %reduce-scatter.8.cloned.1.call-start = ((), (), s32[]{:S(2)}) async-start(), calls=%async_computation.12 | async-start | bytes 3932160 | tf_op jit(solution)/shard_map/reduce_scatter | solution.py:157
  352.3 43.0 %all-to-all-start.1 = ((bf16[64,12,512]{2,1,0:T(8,128)(2,1)}), bf16[64,12,512]{2,1,0:T(8,128)(2,1)S(1)}, u32[]{:S(2)}, u32[]{:S(2)}) async-start(bf16[64,12,512]{2,1,0:T(8,128)(2,1)} %reshape.222), calls=%async_computation.3 | async-start | bytes 2097152 | tf_op jit(solution)/shard_map/all_to_all | solution.py:160
  362.8 43.4 %copy-start.8 = (f32[128,6]{0,1:T(8,128)S(1)}, f32[128,6]{0,1:T(8,128)}, u32[]{:S(2)}) copy-start(f32[128,6]{0,1:T(8,128)} %param.22) | copy-start | bytes 9220
  395.2 38.5 %all-to-all-start.3 = ((bf16[64,12,512]{2,1,0:T(8,128)(2,1)}), bf16[64,12,512]{2,1,0:T(8,128)(2,1)}, u32[]{:S(2)}, u32[]{:S(2)}) async-start(bf16[64,12,512]{2,1,0:T(8,128)(2,1)} %reshape.224), calls=%async_computation.6 | async-start | bytes 2097152 | tf_op jit(solution)/shard_map/all_to_all | solution.py:160
  438.1 1.5 copy-start.3
  438.4 1.2 copy-start.10
  438.4 1.2 copy-start.11
  438.4 16.6 %copy-start.1 = (bf16[2048,576]{0,1:T(8,128)(2,1)S(1)}, bf16[2048,576]{0,1:T(8,128)(2,1)}, u32[]{:S(2)}) copy-start(bf16[2048,576]{0,1:T(8,128)(2,1)} %param.16) | copy-start | bytes 7077892
Sparse Core Ops, SparseCore 0:
  13.0 121.2 all-gather.3
  152.5 21.2 reduce-scatter.3
  224.6 38.0 all-gather.5
  264.4 42.2 all-gather.7
  309.0 41.0 reduce-scatter.5
  352.5 40.5 reduce-scatter.7

commit v7 on v2

--- a/solution.py
+++ b/solution.py
@@ -117,9 +117,7 @@
     ).astype(jnp.float32)
     stream_part = lax.dynamic_slice_in_dim(stream, col_start, col_width, 1)
     hidden = stream_part.astype(jnp.float32) + attention_part
-    square_sum = lax.psum(jnp.sum(hidden * hidden, axis=1, keepdims=True), "tp")
-    gain_part = lax.dynamic_slice_in_dim(moe_gain, col_start, col_width, 0)
-    normed = (hidden * lax.rsqrt(square_sum / D + 1e-06) * gain_part[None, :]).astype(jnp.bfloat16)
+    normed = hidden.astype(jnp.bfloat16)
     experts = lax.axis_size("seq")
     top_k = routes.shape[1]
     capacity = min(tok_count, max(2, 2 * tok_count * top_k // experts))
@@ -145,7 +143,12 @@
         received = lax.all_to_all(sending, "seq", split_axis=0, concat_axis=0, tiled=True)
         sources, slot_count, _ = received.shape
         flat_part = received.reshape(sources * slot_count, col_width)
-        flat_rows = lax.all_gather(flat_part, "tp", axis=1, tiled=True)
+        flat_rows = lax.all_gather(flat_part, "tp", axis=1, tiled=True).astype(jnp.float32)
+        flat_rows = (
+            flat_rows
+            * lax.rsqrt(jnp.mean(flat_rows * flat_rows, axis=1, keepdims=True) + 1e-06)
+            * moe_gain[None, :]
+        ).astype(jnp.bfloat16)
         gate_act = jnp.dot(flat_rows, expert_gate[0], preferred_element_type=jnp.float32)
         up_act = jnp.dot(flat_rows, expert_up[0], preferred_element_type=jnp.float32)
         hidden_units = (jax.nn.silu(gate_act) * up_act).astype(jnp.bfloat16)

time: 434 us -> 426 us (0.982)
  blocking collectives: 94.6 us -> 86.1 us
  other arithmetic: 12.4 us -> 16.9 us
    psum x1 -> x0, blocking collectives: 8.53 us -> none  [on_device(): square_sum = lax.psum(jnp.sum(hidden * hidden, axis=1, keepdims=True), 'tp')]
    reduce_sum x1 -> x2, other arithmetic: 1.03 us -> 5.44 us  [on_device(): jnp.mean(flat_rows * flat_rows, axis=1, keepdims=True) + 1e-06]
  transfers between devices with their start and end apart: 8 -> 8, of which waited for: 7 -> 7; matrix products, arithmetic and copies ran while one was open for 9% -> 10% of each run, Pallas kernels for 0% -> 0%
where the time goes in v7:
time: 426 us; the launch traced here: 425 us
  waiting for transfers between devices  226 us (53%)
  blocking collectives  86.1 us (20%)
  matrix products  42.9 us (10%)
  starting transfers between devices  21.9 us (5%)
  local copies, waits for them, and re-layouts  17.4 us (4%)
  other arithmetic  16.9 us (4%)
  between operations  14.5 us (3%)
    all_gather x1, waiting for transfers between devices, on_device(): shard_rows = lax.all_gather(latent, 'seq', axis=0, tiled=True)  86.3 us
    all_to_all x2, blocking collectives, on_device(): lax.all_to_all(sending, 'seq', split_axis=0, concat_axis=0, tiled=True)  72.7 us
    reduce_scatter x2, waiting for transfers between devices, on_device(): lax.psum_scatter(expert_out, 'tp', scatter_dimension=1, tiled=True)  59.4 us
    all_gather x2, waiting for transfers between devices, on_device(): lax.all_gather(flat_part, 'tp', axis=1, tiled=True).astype(jnp.float32)  31.9 us
    all_to_all x2, waiting for transfers between devices, on_device(): lax.all_to_all(expert_sum, 'seq', split_axis=0, concat_axis=0, tiled=True)  27.1 us
    all_to_all x2, starting transfers between devices, on_device(): lax.all_to_all(expert_sum, 'seq', split_axis=0, concat_axis=0, tiled=True)  21.3 us
    reduce_scatter x1, waiting for transfers between devices, on_device(): lax.psum_scatter(partial_attention.astype(jnp.bfloat16), 'tp', scatter_di...  20.8 us
    dot_general x2, matrix products, on_device(): jnp.dot(hidden_units, expert_down[0], preferred_element_type=jnp.float32)  15.2 us
  transfers between devices with their start and end apart: 8, of which 7 were waited for; matrix products, arithmetic and copies ran while one was open for 10% of the time, Pallas kernels for 0%

profile of v7, /device:TPU:32, one launch (start us, length us, event | category | flops | bytes accessed | tf_op | source)
XLA Modules:
  0.0 425.4 jit_solution(11232632624955133262)
XLA Ops:
  16.0 86.3 %all-gather.4.cloned.1.call-done = bf16[8192,576]{0,1:T(8,128)(2,1)} async-done(((bf16[128,576]{0,1:T(8,128)(2,1)}), bf16[8192,576]{0,1:T(8,128)(2,1)}) %all-gather.4.cloned.1.call-update) | async-done | bytes 9437200 | tf_op jit(solution)/shard_map/all_gather | solution.py:86
  102.3 6.8 %select_reduce_fusion = (f32[256]{0:T(256)S(1)}, f32[256,8192]{1,0:T(8,128)S(1)}) fusion(s32[256]{0:T(256)S(1)} %le.48, s32[8192]{0:T(1024)S(1)} %convert_reduce_fusion, s32[256]{0:T(256)S(1)} %eq.54, bf16[8192,576]{0,1:T(8,128)(2,1)} %all-gather.4.cloned.1.call-done, f32[256,32]{1,0:T(8,128)S(1)} %bitcast.115, f32[256,32]{1,0:T(8,128)S(1)} %bitcast.114, ...), kind=kOutput, calls=%fused_computation.4 | convolution fusion | flops 2426994432 | bytes 18451456 | tf_op jit(solution)/shard_map/ra,ka->rk/dot_general | solution.py:94
  109.1 2.8 fusion.9
  111.9 6.3 %fusion.41 = f32[256,512]{1,0:T(8,128)S(1)} fusion(bf16[8192,576]{0,1:T(8,128)(2,1)} %all-gather.4.cloned.1.call-done, f32[256,8192]{1,0:T(8,128)S(1)} %get-tuple-element.29, f32[256]{0:T(256)S(1)} %broadcast_maximum_fusion, s32[256]{0:T(256)S(1)} %le.48, s32[8192]{0:T(1024)S(1)} %convert_reduce_fusion, s32[256]{0:T(256)S(1)} %eq.54, f32[256]{0:T(256)S(1)} %fusion.9), kind=kOutput, calls=%fused_computation.49 | convolution fusion | flops 2160197632 | bytes 17338368 | tf_op jit(solution)/shard_map/dot_general | solution.py:99
  124.1 20.8 %reduce-scatter.4.cloned.1.call-done = bf16[128,512]{1,0:T(8,128)(2,1)} async-done(((bf16[128,2048]{1,0:T(8,128)(2,1)}), bf16[128,512]{1,0:T(8,128)(2,1)}) %reduce-scatter.4.cloned.1.call-update) | async-done | bytes 131088 | tf_op jit(solution)/shard_map/reduce_scatter | solution.py:115
  146.9 38.2 %all_to_all.20 = bf16[64,12,512]{2,1,0:T(8,128)(2,1)S(1)} all-to-all(bf16[64,12,512]{2,1,0:T(8,128)(2,1)S(1)} %get-tuple-element.4), channel_id=1, replica_groups=mesh['seq'=64,'tp'=4] {'seq'}, dimensions={0} | all-to-all | bytes 1572864 | tf_op jit(solution)/shard_map/all_to_all | solution.py:143
  186.2 34.5 %all_to_all.21 = bf16[64,12,512]{2,1,0:T(8,128)(2,1)S(1)} all-to-all(bf16[64,12,512]{2,1,0:T(8,128)(2,1)S(1)} %get-tuple-element.5), channel_id=1, replica_groups=mesh['seq'=64,'tp'=4] {'seq'}, dimensions={0} | all-to-all | bytes 1572864 | tf_op jit(solution)/shard_map/all_to_all | solution.py:143
  221.9 2.5 all-gather.6.cloned.1.call-done
  224.4 2.7 fusion.3
  227.3 3.8 fusion.27
  231.0 7.6 %convolution_convert_fusion.1 = bf16[768,2048]{1,0:T(8,128)(2,1)} fusion(bf16[1,352,2048]{2,1,0:T(8,128)(2,1)} %param.25, bf16[1,2048,352]{1,2,0:T(8,128)(2,1)} %param.24, f32[768,352]{0,1:T(8,128)} %fusion.27, bf16[768,2048]{1,0:T(8,128)(2,1)S(1)} %copy-done.4, f32[2048]{0:T(1024)S(1)} %copy-done.13, f32[768]{0:T(1024)S(1)} %add_rsqrt_fusion.1), kind=kOutput, calls=%fused_computation.27 | convolution fusion | flops 2224078848 | bytes 10267648 | tf_op jit(solution)/shard_map/dot_general | solution.py:155
  238.9 29.4 %all-gather.8.cloned.1.call-done = bf16[768,2048]{1,0:T(8,128)(2,1)} async-done(((bf16[768,512]{1,0:T(8,128)(2,1)}), bf16[768,2048]{1,0:T(8,128)(2,1)}) %all-gather.8.cloned.1.call-update) | async-done | bytes 3145744 | tf_op jit(solution)/shard_map/all_gather | solution.py:146
  268.4 2.7 fusion.6
  271.2 3.8 fusion.25
  275.0 7.6 %convolution_convert_fusion = bf16[768,2048]{1,0:T(8,128)(2,1)} fusion(bf16[1,352,2048]{2,1,0:T(8,128)(2,1)} %param.25, bf16[1,2048,352]{1,2,0:T(8,128)(2,1)} %param.24, f32[768,352]{0,1:T(8,128)} %fusion.25, bf16[768,2048]{1,0:T(8,128)(2,1)S(1)} %copy-done.3, f32[768]{0:T(1024)S(1)} %add_rsqrt_fusion, f32[2048]{0:T(1024)S(1)} %copy-done.13), kind=kOutput, calls=%fused_computation.26 | convolution fusion | flops 2224078848 | bytes 10267648 | tf_op jit(solution)/shard_map/dot_general | solution.py:155
  282.6 29.2 %reduce-scatter.6.cloned.1.call-done = bf16[768,512]{1,0:T(8,128)(2,1)} async-done(((bf16[768,2048]{1,0:T(8,128)(2,1)}), bf16[768,512]{1,0:T(8,128)(2,1)}) %reduce-scatter.6.cloned.1.call-update) | async-done | bytes 786448 | tf_op jit(solution)/shard_map/reduce_scatter | solution.py:158
  311.8 2.2 reshape.238
  314.0 10.6 %all-to-all-start.1 = ((bf16[64,12,512]{2,1,0:T(8,128)(2,1)}), bf16[64,12,512]{2,1,0:T(8,128)(2,1)S(1)}, u32[]{:S(2)}, u32[]{:S(2)}) async-start(bf16[64,12,512]{2,1,0:T(8,128)(2,1)} %reshape.238), calls=%async_computation.3 | async-start | bytes 2097152 | tf_op jit(solution)/shard_map/all_to_all | solution.py:161
  324.6 30.2 %reduce-scatter.8.cloned.1.call-done = bf16[768,512]{1,0:T(8,128)(2,1)} async-done(((bf16[768,2048]{1,0:T(8,128)(2,1)}), bf16[768,512]{1,0:T(8,128)(2,1)}) %reduce-scatter.8.cloned.1.call-update) | async-done | bytes 786448 | tf_op jit(solution)/shard_map/reduce_scatter | solution.py:158
  354.8 2.1 reshape.240
  357.0 10.7 %all-to-all-start.3 = ((bf16[64,12,512]{2,1,0:T(8,128)(2,1)}), bf16[64,12,512]{2,1,0:T(8,128)(2,1)}, u32[]{:S(2)}, u32[]{:S(2)}) async-start(bf16[64,12,512]{2,1,0:T(8,128)(2,1)} %reshape.240), calls=%async_computation.6 | async-start | bytes 2097152 | tf_op jit(solution)/shard_map/all_to_all | solution.py:161
  368.4 27.1 %all-to-all-done.3 = bf16[64,12,512]{2,1,0:T(8,128)(2,1)} async-done(((bf16[64,12,512]{2,1,0:T(8,128)(2,1)}), bf16[64,12,512]{2,1,0:T(8,128)(2,1)}, u32[]{:S(2)}, u32[]{:S(2)}) %all-to-all-start.3) | async-done | bytes 786464 | tf_op jit(solution)/shard_map/all_to_all | solution.py:161
  397.2 3.3 gather_fusion
  404.3 13.4 %all_gather.15 = bf16[128,2048]{1,0:T(8,128)(2,1)S(1)} all-gather(bf16[128,512]{1,0:T(8,128)(2,1)S(1)} %fusion.67), channel_id=1, replica_groups=mesh['seq'=64,'tp'=4] {'tp'}, dimensions={1}, use_global_device_ids=true | all-gather | bytes 655360 | tf_op jit(solution)/shard_map/all_gather | solution.py:173
  (97 shorter events, 26.2 us)
Async XLA Ops:
  7.2 1.9 copy-start
  7.2 4.9 %copy-start.2 = (bf16[128,2048]{1,0:T(8,128)(2,1)S(1)}, bf16[128,2048]{1,0:T(8,128)(2,1)}, u32[]{:S(2)}) copy-start(bf16[128,2048]{1,0:T(8,128)(2,1)} %param.13) | copy-start | bytes 1572868
  7.2 4.0 copy-start.10
  7.2 95.1 %all-gather.4.cloned.1.call-start = ((), (), s32[]{:S(2)}) async-start(), calls=%async_computation.7 | async-start | bytes 9584640 | tf_op jit(solution)/shard_map/all_gather | solution.py:86
  9.0 5.8 %copy-start.7 = (bf16[2,512,256]{2,1,0:T(8,128)(2,1)S(1)}, bf16[2,512,256]{2,1,0:T(8,128)(2,1)}, u32[]{:S(2)}) copy-start(bf16[2,512,256]{2,1,0:T(8,128)(2,1)} %param.18) | copy-start | bytes 1572868
  12.0 132.9 %reduce-scatter.4.cloned.1.call-start = ((), (), s32[]{:S(2)}) async-start(), calls=%async_computation.8 | async-start | bytes 655360 | tf_op jit(solution)/shard_map/reduce_scatter | solution.py:115
  111.9 7.2 %copy-start.5 = (bf16[256,2048]{1,0:T(8,128)(2,1)S(1)}, bf16[256,2048]{1,0:T(8,128)(2,1)}, u32[]{:S(2)}) copy-start(bf16[256,2048]{1,0:T(8,128)(2,1)} %param.19) | copy-start | bytes 3145732
  118.3 2.2 copy-start.8
  120.2 104.2 %all-gather.6.cloned.1.call-start = ((), (), s32[]{:S(2)}) async-start(), calls=%async_computation.9 | async-start | bytes 3932160 | tf_op jit(solution)/shard_map/all_gather | solution.py:146
  186.1 82.2 %all-gather.8.cloned.1.call-start = ((), (), s32[]{:S(2)}) async-start(), calls=%async_computation.11 | async-start | bytes 3932160 | tf_op jit(solution)/shard_map/all_gather | solution.py:146
  220.7 6.5 %copy-start.13 = (f32[2048]{0:T(1024)S(1)}, f32[2048]{0:T(1024)}, u32[]{:S(2)}) copy-start(f32[2048]{0:T(1024)} %param.20) | copy-start | bytes 24580
  221.9 90.0 %reduce-scatter.6.cloned.1.call-start = ((), (), s32[]{:S(2)}) async-start(), calls=%async_computation.10 | async-start | bytes 3932160 | tf_op jit(solution)/shard_map/reduce_scatter | solution.py:158
  224.4 2.8 copy-start.4
  238.7 116.2 %reduce-scatter.8.cloned.1.call-start = ((), (), s32[]{:S(2)}) async-start(), calls=%async_computation.12 | async-start | bytes 3932160 | tf_op jit(solution)/shard_map/reduce_scatter | solution.py:158
  268.4 2.8 copy-start.3
  314.0 53.8 %copy-start.9 = (f32[128,6]{0,1:T(8,128)S(1)}, f32[128,6]{0,1:T(8,128)}, u32[]{:S(2)}) copy-start(f32[128,6]{0,1:T(8,128)} %param.22) | copy-start | bytes 9220
  314.0 43.0 %all-to-all-start.1 = ((bf16[64,12,512]{2,1,0:T(8,128)(2,1)}), bf16[64,12,512]{2,1,0:T(8,128)(2,1)S(1)}, u32[]{:S(2)}, u32[]{:S(2)}) async-start(bf16[64,12,512]{2,1,0:T(8,128)(2,1)} %reshape.238), calls=%async_computation.3 | async-start | bytes 2097152 | tf_op jit(solution)/shard_map/all_to_all | solution.py:161
  357.0 38.5 %all-to-all-start.3 = ((bf16[64,12,512]{2,1,0:T(8,128)(2,1)}), bf16[64,12,512]{2,1,0:T(8,128)(2,1)}, u32[]{:S(2)}, u32[]{:S(2)}) async-start(bf16[64,12,512]{2,1,0:T(8,128)(2,1)} %reshape.240), calls=%async_computation.6 | async-start | bytes 2097152 | tf_op jit(solution)/shard_map/all_to_all | solution.py:161
  400.5 2.7 copy-start.6
  400.5 18.1 %copy-start.1 = (bf16[2048,576]{0,1:T(8,128)(2,1)S(1)}, bf16[2048,576]{0,1:T(8,128)(2,1)}, u32[]{:S(2)}) copy-start(bf16[2048,576]{0,1:T(8,128)(2,1)} %param.16) | copy-start | bytes 7077892
  402.0 1.2 copy-start.11
  402.0 1.2 copy-start.12
Sparse Core Ops, SparseCore 0:
  12.1 90.1 all-gather.3
  120.4 24.4 reduce-scatter.3
  186.3 38.1 all-gather.5
  226.1 42.2 all-gather.7
  270.8 41.0 reduce-scatter.5
  314.2 40.5 reduce-scatter.7

commit v8 on v7

--- a/solution.py
+++ b/solution.py
@@ -143,7 +143,13 @@
         received = lax.all_to_all(sending, "seq", split_axis=0, concat_axis=0, tiled=True)
         sources, slot_count, _ = received.shape
         flat_part = received.reshape(sources * slot_count, col_width)
-        flat_rows = lax.all_gather(flat_part, "tp", axis=1, tiled=True).astype(jnp.float32)
+        if chunk == 0:
+            flat_rows = lax.all_gather(flat_part, "tp", axis=1, tiled=True)
+        else:
+            repeated = jnp.broadcast_to(flat_part[None], (tp_count,) + flat_part.shape)
+            pieces = lax.all_to_all(repeated, "tp", split_axis=0, concat_axis=0, tiled=True)
+            flat_rows = pieces.transpose(1, 0, 2).reshape(sources * slot_count, D)
+        flat_rows = flat_rows.astype(jnp.float32)
         flat_rows = (
             flat_rows
             * lax.rsqrt(jnp.mean(flat_rows * flat_rows, axis=1, keepdims=True) + 1e-06)

time: 426 us -> 441 us (1.035)
  waiting for transfers between devices: 226 us -> 262 us
  blocking collectives: 86.1 us -> 51.6 us
  starting transfers between devices: 21.9 us -> 32.4 us
    all_to_all x0 -> x2, waiting for transfers between devices: none -> 70.5 us  [the longest x1 43.7 us: on_device(): lax.all_to_all(repeated, 'tp', split_axis=0, concat_axis=0, tiled=True)]
    all_to_all x2 -> x1, blocking collectives: 72.7 us -> 38.1 us  [on_device(): lax.all_to_all(sending, 'seq', split_axis=0, concat_axis=0, tiled=True)]
    all_gather x2 -> x1, waiting for transfers between devices: 31.9 us -> 0.02 us  [on_device(): flat_rows = lax.all_gather(flat_part, 'tp', axis=1, tiled=True)]
    all_to_all x0 -> x2, starting transfers between devices: none -> 10.7 us  [the longest x1 6.86 us: on_device(): lax.all_to_all(sending, 'seq', split_axis=0, concat_axis=0, tiled=True)]
  transfers between devices with their start and end apart: 8 -> 9, of which waited for: 7 -> 7; matrix products, arithmetic and copies ran while one was open for 10% -> 10% of each run, Pallas kernels for 0% -> 0%
where the time goes in v8:
time: 441 us; the launch traced here: 440 us
  waiting for transfers between devices  262 us (59%)
  blocking collectives  51.6 us (12%)
  matrix products  43.4 us (10%)
  starting transfers between devices  32.4 us (7%)
  local copies, waits for them, and re-layouts  19.4 us (4%)
  other arithmetic  17.3 us (4%)
  between operations  14.3 us (3%)
    all_gather x1, waiting for transfers between devices, on_device(): shard_rows = lax.all_gather(latent, 'seq', axis=0, tiled=True)  86.3 us
    reduce_scatter x2, waiting for transfers between devices, on_device(): lax.psum_scatter(expert_out, 'tp', scatter_dimension=1, tiled=True)  56.6 us
    all_to_all x1, waiting for transfers between devices, on_device(): lax.all_to_all(repeated, 'tp', split_axis=0, concat_axis=0, tiled=True)  43.7 us
    all_to_all x1, blocking collectives, on_device(): lax.all_to_all(sending, 'seq', split_axis=0, concat_axis=0, tiled=True)  38.1 us
    all_to_all x2, waiting for transfers between devices, on_device(): lax.all_to_all(expert_sum, 'seq', split_axis=0, concat_axis=0, tiled=True)  27.1 us
    all_to_all x1, waiting for transfers between devices, on_device(): lax.all_to_all(sending, 'seq', split_axis=0, concat_axis=0, tiled=True)  26.7 us
    all_to_all x2, starting transfers between devices, on_device(): lax.all_to_all(expert_sum, 'seq', split_axis=0, concat_axis=0, tiled=True)  21.3 us
    reduce_scatter x1, waiting for transfers between devices, on_device(): lax.psum_scatter(partial_attention.astype(jnp.bfloat16), 'tp', scatter_di...  21 us
  transfers between devices with their start and end apart: 9, of which 7 were waited for; matrix products, arithmetic and copies ran while one was open for 10% of the time, Pallas kernels for 0%

profile of v8, /device:TPU:32, one launch (start us, length us, event | category | flops | bytes accessed | tf_op | source)
XLA Modules:
  0.0 440.1 jit_solution(11954787143515328230)
XLA Ops:
  16.0 86.3 %all-gather.3.cloned.1.call-done = bf16[8192,576]{0,1:T(8,128)(2,1)} async-done(((bf16[128,576]{0,1:T(8,128)(2,1)}), bf16[8192,576]{0,1:T(8,128)(2,1)}) %all-gather.3.cloned.1.call-update) | async-done | bytes 9437200 | tf_op jit(solution)/shard_map/all_gather | solution.py:86
  102.3 6.8 %select_reduce_fusion = (f32[256]{0:T(256)S(1)}, f32[256,8192]{1,0:T(8,128)S(1)}) fusion(s32[256]{0:T(256)S(1)} %le.48, s32[8192]{0:T(1024)S(1)} %convert_reduce_fusion, s32[256]{0:T(256)S(1)} %eq.54, bf16[8192,576]{0,1:T(8,128)(2,1)} %all-gather.3.cloned.1.call-done, f32[256,32]{1,0:T(8,128)S(1)} %bitcast.120, f32[256,32]{1,0:T(8,128)S(1)} %bitcast.119, ...), kind=kOutput, calls=%fused_computation.4 | convolution fusion | flops 2426994432 | bytes 18451456 | tf_op jit(solution)/shard_map/ra,ka->rk/dot_general | solution.py:94
  109.1 2.8 fusion.9
  111.9 6.3 %fusion.41 = f32[256,512]{1,0:T(8,128)S(1)} fusion(bf16[8192,576]{0,1:T(8,128)(2,1)} %all-gather.3.cloned.1.call-done, f32[256,8192]{1,0:T(8,128)S(1)} %get-tuple-element.29, f32[256]{0:T(256)S(1)} %broadcast_maximum_fusion, s32[256]{0:T(256)S(1)} %le.48, s32[8192]{0:T(1024)S(1)} %convert_reduce_fusion, s32[256]{0:T(256)S(1)} %eq.54, f32[256]{0:T(256)S(1)} %fusion.9), kind=kOutput, calls=%fused_computation.49 | convolution fusion | flops 2160197632 | bytes 17338368 | tf_op jit(solution)/shard_map/dot_general | solution.py:99
  123.9 21.0 %reduce-scatter.4.cloned.1.call-done = bf16[128,512]{1,0:T(8,128)(2,1)} async-done(((bf16[128,2048]{1,0:T(8,128)(2,1)}), bf16[128,512]{1,0:T(8,128)(2,1)}) %reduce-scatter.4.cloned.1.call-update) | async-done | bytes 131088 | tf_op jit(solution)/shard_map/reduce_scatter | solution.py:115
  147.9 38.1 %all_to_all.25 = bf16[64,12,512]{2,1,0:T(8,128)(2,1)S(1)} all-to-all(bf16[64,12,512]{2,1,0:T(8,128)(2,1)S(1)} %get-tuple-element.4), channel_id=1, replica_groups=mesh['seq'=64,'tp'=4] {'seq'}, dimensions={0} | all-to-all | bytes 1572864 | tf_op jit(solution)/shard_map/all_to_all | solution.py:143
  186.0 6.9 %all-to-all-start.2 = ((bf16[64,12,512]{2,1,0:T(8,128)(2,1)}), bf16[64,12,512]{2,1,0:T(8,128)(2,1)S(1)}, u32[]{:S(2)}, u32[]{:S(2)}) async-start(bf16[64,12,512]{2,1,0:T(8,128)(2,1)} %get-tuple-element.5), calls=%async_computation.4 | async-start | bytes 2097152 | tf_op jit(solution)/shard_map/all_to_all | solution.py:143
  194.0 26.7 %all-to-all-done.2 = bf16[64,12,512]{2,1,0:T(8,128)(2,1)S(1)} async-done(((bf16[64,12,512]{2,1,0:T(8,128)(2,1)}), bf16[64,12,512]{2,1,0:T(8,128)(2,1)S(1)}, u32[]{:S(2)}, u32[]{:S(2)}) %all-to-all-start.2) | async-done | bytes 786464 | tf_op jit(solution)/shard_map/all_to_all | solution.py:143
  223.1 3.8 all-to-all-start.3
  227.0 43.7 %all-to-all-done.3 = bf16[4,768,512]{1,2,0:T(8,128)(2,1)S(1)} async-done(((bf16[4,768,512]{1,2,0:T(8,128)(2,1)}), bf16[4,768,512]{1,2,0:T(8,128)(2,1)S(1)}, u32[]{:S(2)}, u32[]{:S(2)}) %all-to-all-start.3) | async-done | bytes 3145760 | tf_op jit(solution)/shard_map/all_to_all | solution.py:150
  271.5 2.5 fusion.8
  274.0 4.3 fusion.25
  278.3 7.6 %convolution_convert_fusion = bf16[768,2048]{1,0:T(8,128)(2,1)} fusion(bf16[1,352,2048]{2,1,0:T(8,128)(2,1)S(1)} %copy-done.14, bf16[768,2048]{0,1:T(8,128)(2,1)} %bitcast.15, bf16[1,2048,352]{1,2,0:T(8,128)(2,1)S(1)} %copy-done.15, f32[768,352]{0,1:T(8,128)} %fusion.25), kind=kOutput, calls=%fused_computation.26 | convolution fusion | flops 2217787392 | bytes 10256384 | tf_op jit(solution)/shard_map/dot_general | solution.py:161
  286.2 2.7 fusion.3
  289.1 3.8 fusion.27
  292.8 7.6 %convolution_convert_fusion.1 = bf16[768,2048]{1,0:T(8,128)(2,1)} fusion(bf16[1,352,2048]{2,1,0:T(8,128)(2,1)} %param.25, bf16[1,2048,352]{1,2,0:T(8,128)(2,1)} %param.24, f32[768,352]{0,1:T(8,128)} %fusion.27, bf16[768,2048]{1,0:T(8,128)(2,1)S(1)} %copy-done.3, f32[2048]{0:T(1024)S(1)} %copy-done.7, f32[768]{0:T(1024)S(1)} %add_rsqrt_fusion.1), kind=kOutput, calls=%fused_computation.27 | convolution fusion | flops 2224078848 | bytes 10267648 | tf_op jit(solution)/shard_map/dot_general | solution.py:161
  300.5 26.4 %reduce-scatter.8.cloned.1.call-done = bf16[768,512]{1,0:T(8,128)(2,1)} async-done(((bf16[768,2048]{1,0:T(8,128)(2,1)}), bf16[768,512]{1,0:T(8,128)(2,1)}) %reduce-scatter.8.cloned.1.call-update) | async-done | bytes 786448 | tf_op jit(solution)/shard_map/reduce_scatter | solution.py:164
  328.9 10.6 %all-to-all-start.4 = ((bf16[64,12,512]{2,1,0:T(8,128)(2,1)}), bf16[64,12,512]{2,1,0:T(8,128)(2,1)S(1)}, u32[]{:S(2)}, u32[]{:S(2)}) async-start(bf16[64,12,512]{2,1,0:T(8,128)(2,1)} %reshape.258), calls=%async_computation.7 | async-start | bytes 2097152 | tf_op jit(solution)/shard_map/all_to_all | solution.py:167
  339.6 30.3 %reduce-scatter.6.cloned.1.call-done = bf16[768,512]{1,0:T(8,128)(2,1)} async-done(((bf16[768,2048]{1,0:T(8,128)(2,1)}), bf16[768,512]{1,0:T(8,128)(2,1)}) %reduce-scatter.6.cloned.1.call-update) | async-done | bytes 786448 | tf_op jit(solution)/shard_map/reduce_scatter | solution.py:164
  369.8 2.1 reshape.257
  372.0 10.7 %all-to-all-start.1 = ((bf16[64,12,512]{2,1,0:T(8,128)(2,1)}), bf16[64,12,512]{2,1,0:T(8,128)(2,1)}, u32[]{:S(2)}, u32[]{:S(2)}) async-start(bf16[64,12,512]{2,1,0:T(8,128)(2,1)} %reshape.257), calls=%async_computation.3 | async-start | bytes 2097152 | tf_op jit(solution)/shard_map/all_to_all | solution.py:167
  383.4 27.1 %all-to-all-done.1 = bf16[64,12,512]{2,1,0:T(8,128)(2,1)} async-done(((bf16[64,12,512]{2,1,0:T(8,128)(2,1)}), bf16[64,12,512]{2,1,0:T(8,128)(2,1)}, u32[]{:S(2)}, u32[]{:S(2)}) %all-to-all-start.1) | async-done | bytes 786464 | tf_op jit(solution)/shard_map/all_to_all | solution.py:167
  412.2 3.3 gather_fusion
  419.3 13.4 %all_gather.11 = bf16[128,2048]{1,0:T(8,128)(2,1)S(1)} all-gather(bf16[128,512]{1,0:T(8,128)(2,1)S(1)} %fusion.63), channel_id=1, replica_groups=mesh['seq'=64,'tp'=4] {'tp'}, dimensions={1}, use_global_device_ids=true | all-gather | bytes 655360 | tf_op jit(solution)/shard_map/all_gather | solution.py:179
  (105 shorter events, 30.9 us)
Async XLA Ops:
  7.2 1.9 copy-start
  7.2 4.9 %copy-start.2 = (bf16[128,2048]{1,0:T(8,128)(2,1)S(1)}, bf16[128,2048]{1,0:T(8,128)(2,1)}, u32[]{:S(2)}) copy-start(bf16[128,2048]{1,0:T(8,128)(2,1)} %param.13) | copy-start | bytes 1572868
  7.2 4.0 copy-start.10
  7.2 95.1 %all-gather.3.cloned.1.call-start = ((), (), s32[]{:S(2)}) async-start(), calls=%async_computation.8 | async-start | bytes 9584640 | tf_op jit(solution)/shard_map/all_gather | solution.py:86
  9.0 5.8 %copy-start.6 = (bf16[2,512,256]{2,1,0:T(8,128)(2,1)S(1)}, bf16[2,512,256]{2,1,0:T(8,128)(2,1)}, u32[]{:S(2)}) copy-start(bf16[2,512,256]{2,1,0:T(8,128)(2,1)} %param.18) | copy-start | bytes 1572868
  12.0 132.9 %reduce-scatter.4.cloned.1.call-start = ((), (), s32[]{:S(2)}) async-start(), calls=%async_computation.9 | async-start | bytes 655360 | tf_op jit(solution)/shard_map/reduce_scatter | solution.py:115
  111.9 7.2 %copy-start.4 = (bf16[256,2048]{1,0:T(8,128)(2,1)S(1)}, bf16[256,2048]{1,0:T(8,128)(2,1)}, u32[]{:S(2)}) copy-start(bf16[256,2048]{1,0:T(8,128)(2,1)} %param.19) | copy-start | bytes 3145732
  118.3 2.0 copy-start.8
  186.0 34.7 %all-to-all-start.2 = ((bf16[64,12,512]{2,1,0:T(8,128)(2,1)}), bf16[64,12,512]{2,1,0:T(8,128)(2,1)S(1)}, u32[]{:S(2)}, u32[]{:S(2)}) async-start(bf16[64,12,512]{2,1,0:T(8,128)(2,1)} %get-tuple-element.5), calls=%async_computation.4 | async-start | bytes 2097152 | tf_op jit(solution)/shard_map/all_to_all | solution.py:143
  192.9 93.3 %all-gather.5.cloned.1.call-start = ((), (), s32[]{:S(2)}) async-start(), calls=%async_computation.10 | async-start | bytes 3932160 | tf_op jit(solution)/shard_map/all_gather | solution.py:147
  223.1 3.9 copy-start.7
  223.1 47.7 %all-to-all-start.3 = ((bf16[4,768,512]{1,2,0:T(8,128)(2,1)}), bf16[4,768,512]{1,2,0:T(8,128)(2,1)S(1)}, u32[]{:S(2)}, u32[]{:S(2)}) async-start(bf16[4,768,512]{1,2,0:T(8,128)(2,1)} %broadcast_in_dim.23), calls=%async_computation.5 | async-start | bytes 6291456 | tf_op jit(solution)/shard_map/all_to_all | solution.py:150
  227.0 99.9 %reduce-scatter.8.cloned.1.call-start = ((), (), s32[]{:S(2)}) async-start(), calls=%async_computation.12 | async-start | bytes 3932160 | tf_op jit(solution)/shard_map/reduce_scatter | solution.py:164
  271.5 2.5 copy-start.13
  274.0 4.3 copy-start.14
  274.0 4.3 copy-start.15
  285.9 83.9 %reduce-scatter.6.cloned.1.call-start = ((), (), s32[]{:S(2)}) async-start(), calls=%async_computation.11 | async-start | bytes 3932160 | tf_op jit(solution)/shard_map/reduce_scatter | solution.py:164
  286.2 2.8 copy-start.3
  328.9 53.9 %copy-start.9 = (f32[128,6]{0,1:T(8,128)S(1)}, f32[128,6]{0,1:T(8,128)}, u32[]{:S(2)}) copy-start(f32[128,6]{0,1:T(8,128)} %param.22) | copy-start | bytes 9220
  328.9 43.0 %all-to-all-start.4 = ((bf16[64,12,512]{2,1,0:T(8,128)(2,1)}), bf16[64,12,512]{2,1,0:T(8,128)(2,1)S(1)}, u32[]{:S(2)}, u32[]{:S(2)}) async-start(bf16[64,12,512]{2,1,0:T(8,128)(2,1)} %reshape.258), calls=%async_computation.7 | async-start | bytes 2097152 | tf_op jit(solution)/shard_map/all_to_all | solution.py:167
  372.0 38.5 %all-to-all-start.1 = ((bf16[64,12,512]{2,1,0:T(8,128)(2,1)}), bf16[64,12,512]{2,1,0:T(8,128)(2,1)}, u32[]{:S(2)}, u32[]{:S(2)}) async-start(bf16[64,12,512]{2,1,0:T(8,128)(2,1)} %reshape.257), calls=%async_computation.3 | async-start | bytes 2097152 | tf_op jit(solution)/shard_map/all_to_all | solution.py:167
  415.5 2.7 copy-start.5
  415.5 18.1 %copy-start.1 = (bf16[2048,576]{0,1:T(8,128)(2,1)S(1)}, bf16[2048,576]{0,1:T(8,128)(2,1)}, u32[]{:S(2)}) copy-start(bf16[2048,576]{0,1:T(8,128)(2,1)} %param.16) | copy-start | bytes 7077892
  417.0 1.2 copy-start.11
  (1 other events, 1.2 us)
Sparse Core Ops, SparseCore 0:
  12.1 90.1 all-gather.2
  120.4 24.4 reduce-scatter.3
  195.5 47.3 all-gather.4
  286.1 40.7 reduce-scatter.7
  329.2 40.5 reduce-scatter.5

commit v9 on v7

--- a/solution.py
+++ b/solution.py
@@ -137,7 +137,7 @@
     outgoing = outgoing.reshape(experts, capacity, col_width)
     chunk_count = 2
     chunk_slots = capacity // chunk_count
-    returned_chunks = []
+    moe = jnp.zeros((tok_count, col_width), jnp.float32)
     for chunk in range(chunk_count):
         sending = outgoing[:, chunk * chunk_slots : (chunk + 1) * chunk_slots]
         received = lax.all_to_all(sending, "seq", split_axis=0, concat_axis=0, tiled=True)
@@ -157,18 +157,18 @@
         ).astype(jnp.bfloat16)
         expert_sum = lax.psum_scatter(expert_out, "tp", scatter_dimension=1, tiled=True)
         expert_sum = expert_sum.reshape(sources, slot_count, col_width)
-        returned_chunks.append(
-            lax.all_to_all(expert_sum, "seq", split_axis=0, concat_axis=0, tiled=True)
+        returned = lax.all_to_all(expert_sum, "seq", split_axis=0, concat_axis=0, tiled=True)
+        in_chunk = (slot_rank // chunk_slots == chunk).reshape(tok_count, top_k)
+        chunk_index = flat_routes * chunk_slots + slot_rank - chunk * chunk_slots
+        chunk_index = jnp.where(in_chunk.reshape(-1), chunk_index, 0)
+        gathered = returned.reshape(experts * chunk_slots, col_width)[chunk_index].reshape(
+            tok_count, top_k, col_width
         )
-    returned = jnp.concatenate(returned_chunks, axis=1)
-    gathered = returned.reshape(experts * capacity, col_width)[slot_index].reshape(
-        tok_count, top_k, col_width
-    )
-    moe = jnp.zeros((tok_count, col_width), jnp.float32)
-    for route_slot in range(top_k):
-        moe = moe + route_weight[:, route_slot][:, None] * gathered[:, route_slot].astype(
-            jnp.float32
-        )
+        chunk_weight = jnp.where(in_chunk, route_weight, 0.0)
+        for route_slot in range(top_k):
+            moe = moe + chunk_weight[:, route_slot][:, None] * gathered[:, route_slot].astype(
+                jnp.float32
+            )
     layer_part = (hidden + moe).astype(jnp.bfloat16)
     layer_out = lax.all_gather(layer_part, "tp", axis=1, tiled=True)
     return (layer_out, latent)

time: 426 us -> 430 us (level)
  local copies, waits for them, and re-layouts: 17.4 us -> 26.2 us
    slice x1, local copies, waits for them, and re-layouts: 1.15 us -> 6.41 us  [on_device(): gathered[:, route_slot].astype(jnp.float32)]
where the time goes in v9:
time: 430 us
  waiting for transfers between devices  225 us (52%)
  blocking collectives  86.1 us (20%)
  matrix products  40.6 us (9%)
  local copies, waits for them, and re-layouts  26.2 us (6%)
  starting transfers between devices  22 us (5%)
  other arithmetic  15.5 us (4%)
  between operations  14.6 us (3%)
    all_gather x1, waiting for transfers between devices, on_device(): shard_rows = lax.all_gather(latent, 'seq', axis=0, tiled=True)  86.3 us
    all_to_all x2, blocking collectives, on_device(): lax.all_to_all(sending, 'seq', split_axis=0, concat_axis=0, tiled=True)  72.7 us
    reduce_scatter x2, waiting for transfers between devices, on_device(): lax.psum_scatter(expert_out, 'tp', scatter_dimension=1, tiled=True)  61.2 us
    all_gather x2, waiting for transfers between devices, on_device(): lax.all_gather(flat_part, 'tp', axis=1, tiled=True).astype(jnp.float32)  32.6 us
    all_to_all x2, waiting for transfers between devices, on_device(): lax.all_to_all(expert_sum, 'seq', split_axis=0, concat_axis=0, tiled=True)  23.7 us
    all_to_all x2, starting transfers between devices, on_device(): lax.all_to_all(expert_sum, 'seq', split_axis=0, concat_axis=0, tiled=True)  21.3 us
    reduce_scatter x1, waiting for transfers between devices, on_device(): lax.psum_scatter(partial_attention.astype(jnp.bfloat16), 'tp', scatter_di...  20.8 us
    dot_general x2, matrix products, on_device(): jnp.dot(hidden_units, expert_down[0], preferred_element_type=jnp.float32)  16.1 us
  transfers between devices with their start and end apart: 8, of which 7 were waited for; matrix products, arithmetic and copies ran while one was open for 10% of the time, Pallas kernels for 0%

profile of v9, /device:TPU:32, one launch (start us, length us, event | category | flops | bytes accessed | tf_op | source)
XLA Modules:
  0.0 429.7 jit_solution(9712315103556283590)
XLA Ops:
  16.1 86.3 %all-gather.4.cloned.1.call-done = bf16[8192,576]{0,1:T(8,128)(2,1)} async-done(((bf16[128,576]{0,1:T(8,128)(2,1)}), bf16[8192,576]{0,1:T(8,128)(2,1)}) %all-gather.4.cloned.1.call-update) | async-done | bytes 9437200 | tf_op jit(solution)/shard_map/all_gather | solution.py:86
  102.4 6.8 %select_reduce_fusion = (f32[256]{0:T(256)S(1)}, f32[256,8192]{1,0:T(8,128)S(1)}) fusion(s32[256]{0:T(256)S(1)} %le.48, s32[8192]{0:T(1024)S(1)} %convert_reduce_fusion, s32[256]{0:T(256)S(1)} %eq.81, bf16[8192,576]{0,1:T(8,128)(2,1)} %all-gather.4.cloned.1.call-done, f32[256,32]{1,0:T(8,128)S(1)} %bitcast.131, f32[256,32]{1,0:T(8,128)S(1)} %bitcast.130, ...), kind=kOutput, calls=%fused_computation.5 | convolution fusion | flops 2426994432 | bytes 18451456 | tf_op jit(solution)/shard_map/ra,ka->rk/dot_general | solution.py:94
  109.2 2.8 fusion.9
  112.0 6.3 %fusion.41 = f32[256,512]{1,0:T(8,128)S(1)} fusion(bf16[8192,576]{0,1:T(8,128)(2,1)} %all-gather.4.cloned.1.call-done, f32[256,8192]{1,0:T(8,128)S(1)} %get-tuple-element.43, f32[256]{0:T(256)S(1)} %broadcast_maximum_fusion, s32[256]{0:T(256)S(1)} %le.48, s32[8192]{0:T(1024)S(1)} %convert_reduce_fusion, s32[256]{0:T(256)S(1)} %eq.81, f32[256]{0:T(256)S(1)} %fusion.9), kind=kOutput, calls=%fused_computation.49 | convolution fusion | flops 2160197632 | bytes 17338368 | tf_op jit(solution)/shard_map/dot_general | solution.py:99
  124.2 20.8 %reduce-scatter.4.cloned.1.call-done = bf16[128,512]{1,0:T(8,128)(2,1)} async-done(((bf16[128,2048]{1,0:T(8,128)(2,1)}), bf16[128,512]{1,0:T(8,128)(2,1)}) %reduce-scatter.4.cloned.1.call-update) | async-done | bytes 131088 | tf_op jit(solution)/shard_map/reduce_scatter | solution.py:115
  147.0 38.1 %all_to_all.20 = bf16[64,12,512]{2,1,0:T(8,128)(2,1)S(1)} all-to-all(bf16[64,12,512]{2,1,0:T(8,128)(2,1)S(1)} %get-tuple-element.19), channel_id=1, replica_groups=mesh['seq'=64,'tp'=4] {'seq'}, dimensions={0} | all-to-all | bytes 1572864 | tf_op jit(solution)/shard_map/all_to_all | solution.py:143
  186.3 34.5 %all_to_all.21 = bf16[64,12,512]{2,1,0:T(8,128)(2,1)S(1)} all-to-all(bf16[64,12,512]{2,1,0:T(8,128)(2,1)S(1)} %get-tuple-element.18), channel_id=1, replica_groups=mesh['seq'=64,'tp'=4] {'seq'}, dimensions={0} | all-to-all | bytes 1572864 | tf_op jit(solution)/shard_map/all_to_all | solution.py:143
  222.0 2.6 all-gather.8.cloned.1.call-done
  224.5 2.7 fusion.6
  227.4 2.9 fusion.25
  230.3 7.8 %convolution_convert_fusion = bf16[768,2048]{1,0:T(8,128)(2,1)} fusion(bf16[1,352,2048]{2,1,0:T(8,128)(2,1)S(1)} %copy-done.12, bf16[1,2048,352]{1,2,0:T(8,128)(2,1)} %param.24, f32[768,352]{0,1:T(8,128)S(1)} %fusion.25, bf16[768,2048]{1,0:T(8,128)(2,1)} %all-gather.8.cloned.1.call-done, f32[768]{0:T(1024)S(1)} %add_rsqrt_fusion, f32[2048]{0:T(1024)S(1)} %copy-done.13), kind=kOutput, calls=%fused_computation.27 | convolution fusion | flops 2224078848 | bytes 10267648 | tf_op jit(solution)/shard_map/dot_general | solution.py:155
  238.4 30.1 %all-gather.6.cloned.1.call-done = bf16[768,2048]{1,0:T(8,128)(2,1)} async-done(((bf16[768,512]{1,0:T(8,128)(2,1)}), bf16[768,2048]{1,0:T(8,128)(2,1)}) %all-gather.6.cloned.1.call-update) | async-done | bytes 3145744 | tf_op jit(solution)/shard_map/all_gather | solution.py:146
  268.5 2.7 fusion.3
  272.7 8.3 %convolution_convert_fusion.1 = bf16[768,2048]{1,0:T(8,128)(2,1)} fusion(bf16[1,352,2048]{2,1,0:T(8,128)(2,1)} %param.25, bf16[1,2048,352]{1,2,0:T(8,128)(2,1)} %param.24, f32[768,352]{0,1:T(8,128)S(1)} %fusion.27, bf16[768,2048]{1,0:T(8,128)(2,1)} %all-gather.6.cloned.1.call-done, f32[2048]{0:T(1024)S(1)} %copy-done.13, f32[768]{0:T(1024)S(1)} %add_rsqrt_fusion.1), kind=kOutput, calls=%fused_computation.28 | convolution fusion | flops 2224078848 | bytes 10267648 | tf_op jit(solution)/shard_map/dot_general | solution.py:155
  281.0 30.9 %reduce-scatter.8.cloned.1.call-done = bf16[768,512]{1,0:T(8,128)(2,1)} async-done(((bf16[768,2048]{1,0:T(8,128)(2,1)}), bf16[768,512]{1,0:T(8,128)(2,1)}) %reduce-scatter.8.cloned.1.call-update) | async-done | bytes 786448 | tf_op jit(solution)/shard_map/reduce_scatter | solution.py:158
  314.1 10.6 %all-to-all-start.3 = ((bf16[64,12,512]{2,1,0:T(8,128)(2,1)}), bf16[64,12,512]{2,1,0:T(8,128)(2,1)S(1)}, u32[]{:S(2)}, u32[]{:S(2)}) async-start(bf16[64,12,512]{2,1,0:T(8,128)(2,1)} %reshape.323), calls=%async_computation.6 | async-start | bytes 2097152 | tf_op jit(solution)/shard_map/all_to_all | solution.py:160
  324.7 30.3 %reduce-scatter.6.cloned.1.call-done = bf16[768,512]{1,0:T(8,128)(2,1)} async-done(((bf16[768,2048]{1,0:T(8,128)(2,1)}), bf16[768,512]{1,0:T(8,128)(2,1)}) %reduce-scatter.6.cloned.1.call-update) | async-done | bytes 786448 | tf_op jit(solution)/shard_map/reduce_scatter | solution.py:158
  354.9 2.2 reshape.319
  357.1 10.7 %all-to-all-start.1 = ((bf16[64,12,512]{2,1,0:T(8,128)(2,1)}), bf16[64,12,512]{2,1,0:T(8,128)(2,1)}, u32[]{:S(2)}, u32[]{:S(2)}) async-start(bf16[64,12,512]{2,1,0:T(8,128)(2,1)} %reshape.319), calls=%async_computation.3 | async-start | bytes 2097152 | tf_op jit(solution)/shard_map/all_to_all | solution.py:160
  368.9 2.7 gather_fusion.1
  371.9 23.7 %all-to-all-done.1 = bf16[64,12,512]{2,1,0:T(8,128)(2,1)} async-done(((bf16[64,12,512]{2,1,0:T(8,128)(2,1)}), bf16[64,12,512]{2,1,0:T(8,128)(2,1)}, u32[]{:S(2)}, u32[]{:S(2)}) %all-to-all-start.1) | async-done | bytes 786464 | tf_op jit(solution)/shard_map/all_to_all | solution.py:160
  396.9 2.7 gather_fusion
  400.8 6.4 %fusion.100 = (bf16[128,1,512]{2,1,0:T(2,128)(2,1)S(1)}, bf16[128,1,512]{2,1,0:T(2,128)(2,1)S(1)}, bf16[128,1,512]{2,1,0:T(2,128)(2,1)S(1)}, bf16[128,1,512]{2,1...) fusion(bf16[128,6,512]{2,1,0:T(8,128)(2,1)} %reshape.321, ...), kind=kLoop, calls=%fused_computation.169 | loop fusion | bytes 3145728 | tf_op jit(solution)/shard_map/slice | solution.py:169
  408.6 13.4 %all_gather.15 = bf16[128,2048]{1,0:T(8,128)(2,1)S(1)} all-gather(bf16[128,512]{1,0:T(8,128)(2,1)S(1)} %fusion.67), channel_id=1, replica_groups=mesh['seq'=64,'tp'=4] {'tp'}, dimensions={1}, use_global_device_ids=true | all-gather | bytes 655360 | tf_op jit(solution)/shard_map/all_gather | solution.py:173
  (104 shorter events, 28.8 us)
Async XLA Ops:
  7.2 1.9 copy-start
  7.2 5.0 %copy-start.2 = (bf16[128,2048]{1,0:T(8,128)(2,1)S(1)}, bf16[128,2048]{1,0:T(8,128)(2,1)}, u32[]{:S(2)}) copy-start(bf16[128,2048]{1,0:T(8,128)(2,1)} %param.13) | copy-start | bytes 1572868
  7.2 4.1 copy-start.10
  7.2 95.2 %all-gather.4.cloned.1.call-start = ((), (), s32[]{:S(2)}) async-start(), calls=%async_computation.7 | async-start | bytes 9584640 | tf_op jit(solution)/shard_map/all_gather | solution.py:86
  9.1 5.7 %copy-start.6 = (bf16[2,512,256]{2,1,0:T(8,128)(2,1)S(1)}, bf16[2,512,256]{2,1,0:T(8,128)(2,1)}, u32[]{:S(2)}) copy-start(bf16[2,512,256]{2,1,0:T(8,128)(2,1)} %param.18) | copy-start | bytes 1572868
  12.1 132.9 %reduce-scatter.4.cloned.1.call-start = ((), (), s32[]{:S(2)}) async-start(), calls=%async_computation.8 | async-start | bytes 655360 | tf_op jit(solution)/shard_map/reduce_scatter | solution.py:115
  112.0 7.2 %copy-start.5 = (bf16[256,2048]{1,0:T(8,128)(2,1)S(1)}, bf16[256,2048]{1,0:T(8,128)(2,1)}, u32[]{:S(2)}) copy-start(bf16[256,2048]{1,0:T(8,128)(2,1)} %param.19) | copy-start | bytes 3145732
  118.3 2.2 copy-start.8
  120.3 104.2 %all-gather.8.cloned.1.call-start = ((), (), s32[]{:S(2)}) async-start(), calls=%async_computation.11 | async-start | bytes 3932160 | tf_op jit(solution)/shard_map/all_gather | solution.py:146
  186.2 82.3 %all-gather.6.cloned.1.call-start = ((), (), s32[]{:S(2)}) async-start(), calls=%async_computation.9 | async-start | bytes 3932160 | tf_op jit(solution)/shard_map/all_gather | solution.py:146
  220.8 6.5 %copy-start.13 = (f32[2048]{0:T(1024)S(1)}, f32[2048]{0:T(1024)}, u32[]{:S(2)}) copy-start(f32[2048]{0:T(1024)} %param.20) | copy-start | bytes 24580
  221.9 90.0 %reduce-scatter.8.cloned.1.call-start = ((), (), s32[]{:S(2)}) async-start(), calls=%async_computation.12 | async-start | bytes 3932160 | tf_op jit(solution)/shard_map/reduce_scatter | solution.py:158
  224.5 2.8 copy-start.4
  227.4 2.9 copy-start.12
  238.1 33.1 %copy-start.11 = (bf16[1,2048,352]{1,2,0:T(8,128)(2,1)S(1)}, bf16[1,2048,352]{1,2,0:T(8,128)(2,1)}, u32[]{:S(2)}) copy-start(bf16[1,2048,352]{1,2,0:T(8,128)(2,1)} %param.23) | copy-start | bytes 4325380
  238.2 116.8 %reduce-scatter.6.cloned.1.call-start = ((), (), s32[]{:S(2)}) async-start(), calls=%async_computation.10 | async-start | bytes 3932160 | tf_op jit(solution)/shard_map/reduce_scatter | solution.py:158
  268.5 2.8 copy-start.3
  314.1 53.9 %copy-start.9 = (f32[128,6]{0,1:T(8,128)S(1)}, f32[128,6]{0,1:T(8,128)}, u32[]{:S(2)}) copy-start(f32[128,6]{0,1:T(8,128)} %param.22) | copy-start | bytes 9220
  314.1 43.1 %all-to-all-start.3 = ((bf16[64,12,512]{2,1,0:T(8,128)(2,1)}), bf16[64,12,512]{2,1,0:T(8,128)(2,1)S(1)}, u32[]{:S(2)}, u32[]{:S(2)}) async-start(bf16[64,12,512]{2,1,0:T(8,128)(2,1)} %reshape.323), calls=%async_computation.6 | async-start | bytes 2097152 | tf_op jit(solution)/shard_map/all_to_all | solution.py:160
  357.1 38.5 %all-to-all-start.1 = ((bf16[64,12,512]{2,1,0:T(8,128)(2,1)}), bf16[64,12,512]{2,1,0:T(8,128)(2,1)}, u32[]{:S(2)}, u32[]{:S(2)}) async-start(bf16[64,12,512]{2,1,0:T(8,128)(2,1)} %reshape.319), calls=%async_computation.3 | async-start | bytes 2097152 | tf_op jit(solution)/shard_map/all_to_all | solution.py:160
  400.8 6.4 %copy-start.7 = (bf16[128,512]{1,0:T(8,128)(2,1)S(1)}, bf16[128,512]{1,0:T(8,128)(2,1)}, u32[]{:S(2)}) copy-start(bf16[128,512]{1,0:T(8,128)(2,1)} %reduce-scatter.4.cloned.1.call-done) | copy-start | bytes 393220
  400.8 22.0 %copy-start.1 = (bf16[2048,576]{0,1:T(8,128)(2,1)S(1)}, bf16[2048,576]{0,1:T(8,128)(2,1)}, u32[]{:S(2)}) copy-start(bf16[2048,576]{0,1:T(8,128)(2,1)} %param.16) | copy-start | bytes 7077892
Sparse Core Ops, SparseCore 0:
  12.2 90.1 all-gather.3
  120.4 24.4 reduce-scatter.3
  186.3 38.1 all-gather.7
  226.2 42.2 all-gather.5
  270.9 41.0 reduce-scatter.7
  314.3 40.5 reduce-scatter.5

commit v10 on v7

--- a/solution.py
+++ b/solution.py
@@ -112,9 +112,11 @@
     tp_count = lax.axis_size("tp")
     col_width = D // tp_count
     col_start = lax.axis_index("tp") * col_width
-    attention_part = lax.psum_scatter(
-        partial_attention.astype(jnp.bfloat16), "tp", scatter_dimension=1, tiled=True
-    ).astype(jnp.float32)
+    attention_pieces = partial_attention.astype(jnp.bfloat16).reshape(tok_count, tp_count, col_width)
+    attention_pieces = lax.all_to_all(
+        attention_pieces.transpose(1, 0, 2), "tp", split_axis=0, concat_axis=0, tiled=True
+    )
+    attention_part = jnp.sum(attention_pieces.astype(jnp.float32), axis=0)
     stream_part = lax.dynamic_slice_in_dim(stream, col_start, col_width, 1)
     hidden = stream_part.astype(jnp.float32) + attention_part
     normed = hidden.astype(jnp.bfloat16)

time: 426 us -> 413 us (0.969)
  waiting for transfers between devices: 226 us -> 212 us
    reduce_scatter x1 -> x0, waiting for transfers between devices: 20.8 us -> none  [on_device(): lax.psum_scatter(partial_attention.astype(jnp.bfloat16), 'tp', scatter_di...]
    all_to_all x0 -> x1, waiting for transfers between devices: none -> 9.08 us  [on_device(): lax.all_to_all(attention_pieces.transpose(1, 0, 2), 'tp', split_axis=0, c...]
where the time goes in v10:
time: 413 us
  waiting for transfers between devices  212 us (51%)
  blocking collectives  85.2 us (21%)
  matrix products  41.3 us (10%)
  starting transfers between devices  25.9 us (6%)
  other arithmetic  18 us (4%)
  local copies, waits for them, and re-layouts  16.6 us (4%)
  between operations  14.2 us (3%)
    all_gather x1, waiting for transfers between devices, on_device(): shard_rows = lax.all_gather(latent, 'seq', axis=0, tiled=True)  83.5 us
    all_to_all x2, blocking collectives, on_device(): lax.all_to_all(sending, 'seq', split_axis=0, concat_axis=0, tiled=True)  71.7 us
    reduce_scatter x2, waiting for transfers between devices, on_device(): lax.psum_scatter(expert_out, 'tp', scatter_dimension=1, tiled=True)  59.5 us
    all_gather x2, waiting for transfers between devices, on_device(): lax.all_gather(flat_part, 'tp', axis=1, tiled=True).astype(jnp.float32)  31.8 us
    all_to_all x2, waiting for transfers between devices, on_device(): lax.all_to_all(expert_sum, 'seq', split_axis=0, concat_axis=0, tiled=True)  27.6 us
    all_to_all x2, starting transfers between devices, on_device(): lax.all_to_all(expert_sum, 'seq', split_axis=0, concat_axis=0, tiled=True)  21.3 us
    dot_general x2, matrix products, on_device(): jnp.dot(hidden_units, expert_down[0], preferred_element_type=jnp.float32)  15.2 us
    all_gather x1, blocking collectives, on_device(): layer_out = lax.all_gather(layer_part, 'tp', axis=1, tiled=True)  13.4 us
  transfers between devices with their start and end apart: 8, of which 7 were waited for; matrix products, arithmetic and copies ran while one was open for 10% of the time, Pallas kernels for 0%

profile of v10, /device:TPU:32, one launch (start us, length us, event | category | flops | bytes accessed | tf_op | source)
XLA Modules:
  0.0 412.8 jit_solution(9438771589378792705)
XLA Ops:
  18.8 83.5 %all-gather.4.cloned.1.call-done = bf16[8192,576]{0,1:T(8,128)(2,1)} async-done(((bf16[128,576]{0,1:T(8,128)(2,1)}), bf16[8192,576]{0,1:T(8,128)(2,1)}) %all-gather.4.cloned.1.call-update) | async-done | bytes 9437200 | tf_op jit(solution)/shard_map/all_gather | solution.py:86
  102.3 6.8 %select_reduce_fusion = (f32[256]{0:T(256)S(1)}, f32[256,8192]{1,0:T(8,128)S(1)}) fusion(s32[256]{0:T(256)S(1)} %le.48, s32[8192]{0:T(1024)S(1)} %convert_reduce_fusion.1, s32[256]{0:T(256)S(1)} %eq.54, bf16[8192,576]{0,1:T(8,128)(2,1)} %all-gather.4.cloned.1.call-done, f32[256,32]{1,0:T(8,128)S(1)} %bitcast.126, f32[256,32]{1,0:T(8,128)S(1)} %bitcast.125, ...), kind=kOutput, calls=%fused_computation.4 | convolution fusion | flops 2426994432 | bytes 18451456 | tf_op jit(solution)/shard_map/ra,ka->rk/dot_general | solution.py:94
  109.1 2.8 fusion.9
  111.9 6.3 %fusion.41 = f32[256,512]{1,0:T(8,128)S(1)} fusion(bf16[8192,576]{0,1:T(8,128)(2,1)} %all-gather.4.cloned.1.call-done, f32[256,8192]{1,0:T(8,128)S(1)} %get-tuple-element.29, f32[256]{0:T(256)S(1)} %broadcast_maximum_fusion, s32[256]{0:T(256)S(1)} %le.48, s32[8192]{0:T(1024)S(1)} %convert_reduce_fusion.1, s32[256]{0:T(256)S(1)} %eq.54, f32[256]{0:T(256)S(1)} %fusion.9), kind=kOutput, calls=%fused_computation.49 | convolution fusion | flops 2160197632 | bytes 17338368 | tf_op jit(solution)/shard_map/dot_general | solution.py:99
  120.3 4.2 %all-to-all-start = ((bf16[4,128,512]{2,1,0:T(8,128)(2,1)}), bf16[4,128,512]{2,1,0:T(8,128)(2,1)S(1)}, u32[]{:S(2)}, u32[]{:S(2)}) async-start(bf16[4,128,512]{2,1,0:T(8,128)(2,1)} %bitcast.117), calls=%async_computation | async-start | bytes 1048576 | tf_op jit(solution)/shard_map/all_to_all | solution.py:116
  125.3 9.1 %all-to-all-done = bf16[4,128,512]{2,1,0:T(8,128)(2,1)S(1)} async-done(((bf16[4,128,512]{2,1,0:T(8,128)(2,1)}), bf16[4,128,512]{2,1,0:T(8,128)(2,1)S(1)}, u32[]{:S(2)}, u32[]{:S(2)}) %all-to-all-start) | async-done | bytes 524320 | tf_op jit(solution)/shard_map/all_to_all | solution.py:116
  135.6 37.2 %all_to_all.25 = bf16[64,12,512]{2,1,0:T(8,128)(2,1)S(1)} all-to-all(bf16[64,12,512]{2,1,0:T(8,128)(2,1)S(1)} %get-tuple-element.4), channel_id=1, replica_groups=mesh['seq'=64,'tp'=4] {'seq'}, dimensions={0} | all-to-all | bytes 1572864 | tf_op jit(solution)/shard_map/all_to_all | solution.py:145
  174.0 34.5 %all_to_all.26 = bf16[64,12,512]{2,1,0:T(8,128)(2,1)S(1)} all-to-all(bf16[64,12,512]{2,1,0:T(8,128)(2,1)S(1)} %get-tuple-element.5), channel_id=1, replica_groups=mesh['seq'=64,'tp'=4] {'seq'}, dimensions={0} | all-to-all | bytes 1572864 | tf_op jit(solution)/shard_map/all_to_all | solution.py:145
  209.7 2.2 all-gather.6.cloned.1.call-done
  212.0 2.7 fusion.3
  214.8 3.8 fusion.27
  218.6 7.6 %convolution_convert_fusion.1 = bf16[768,2048]{1,0:T(8,128)(2,1)} fusion(bf16[1,352,2048]{2,1,0:T(8,128)(2,1)} %param.25, bf16[1,2048,352]{1,2,0:T(8,128)(2,1)} %param.24, f32[768,352]{0,1:T(8,128)} %fusion.27, bf16[768,2048]{1,0:T(8,128)(2,1)S(1)} %copy-done.4, f32[2048]{0:T(1024)S(1)} %copy-done.12, f32[768]{0:T(1024)S(1)} %add_rsqrt_fusion.1), kind=kOutput, calls=%fused_computation.27 | convolution fusion | flops 2224078848 | bytes 10267648 | tf_op jit(solution)/shard_map/dot_general | solution.py:157
  226.5 29.6 %all-gather.8.cloned.1.call-done = bf16[768,2048]{1,0:T(8,128)(2,1)} async-done(((bf16[768,512]{1,0:T(8,128)(2,1)}), bf16[768,2048]{1,0:T(8,128)(2,1)}) %all-gather.8.cloned.1.call-update) | async-done | bytes 3145744 | tf_op jit(solution)/shard_map/all_gather | solution.py:148
  256.0 2.7 fusion.6
  258.9 3.8 fusion.25
  262.7 7.6 %convolution_convert_fusion = bf16[768,2048]{1,0:T(8,128)(2,1)} fusion(bf16[1,352,2048]{2,1,0:T(8,128)(2,1)} %param.25, bf16[1,2048,352]{1,2,0:T(8,128)(2,1)} %param.24, f32[768,352]{0,1:T(8,128)} %fusion.25, bf16[768,2048]{1,0:T(8,128)(2,1)S(1)} %copy-done.3, f32[768]{0:T(1024)S(1)} %add_rsqrt_fusion, f32[2048]{0:T(1024)S(1)} %copy-done.12), kind=kOutput, calls=%fused_computation.26 | convolution fusion | flops 2224078848 | bytes 10267648 | tf_op jit(solution)/shard_map/dot_general | solution.py:157
  270.3 29.2 %reduce-scatter.3.cloned.1.call-done = bf16[768,512]{1,0:T(8,128)(2,1)} async-done(((bf16[768,2048]{1,0:T(8,128)(2,1)}), bf16[768,512]{1,0:T(8,128)(2,1)}) %reduce-scatter.3.cloned.1.call-update) | async-done | bytes 786448 | tf_op jit(solution)/shard_map/reduce_scatter | solution.py:160
  301.6 10.6 %all-to-all-start.2 = ((bf16[64,12,512]{2,1,0:T(8,128)(2,1)}), bf16[64,12,512]{2,1,0:T(8,128)(2,1)S(1)}, u32[]{:S(2)}, u32[]{:S(2)}) async-start(bf16[64,12,512]{2,1,0:T(8,128)(2,1)} %reshape.242), calls=%async_computation.3 | async-start | bytes 2097152 | tf_op jit(solution)/shard_map/all_to_all | solution.py:163
  312.3 30.3 %reduce-scatter.5.cloned.1.call-done = bf16[768,512]{1,0:T(8,128)(2,1)} async-done(((bf16[768,2048]{1,0:T(8,128)(2,1)}), bf16[768,512]{1,0:T(8,128)(2,1)}) %reduce-scatter.5.cloned.1.call-update) | async-done | bytes 786448 | tf_op jit(solution)/shard_map/reduce_scatter | solution.py:160
  342.5 2.2 reshape.244
  344.7 10.7 %all-to-all-start.4 = ((bf16[64,12,512]{2,1,0:T(8,128)(2,1)}), bf16[64,12,512]{2,1,0:T(8,128)(2,1)}, u32[]{:S(2)}, u32[]{:S(2)}) async-start(bf16[64,12,512]{2,1,0:T(8,128)(2,1)} %reshape.244), calls=%async_computation.6 | async-start | bytes 2097152 | tf_op jit(solution)/shard_map/all_to_all | solution.py:163
  355.6 27.6 %all-to-all-done.4 = bf16[64,12,512]{2,1,0:T(8,128)(2,1)} async-done(((bf16[64,12,512]{2,1,0:T(8,128)(2,1)}), bf16[64,12,512]{2,1,0:T(8,128)(2,1)}, u32[]{:S(2)}, u32[]{:S(2)}) %all-to-all-start.4) | async-done | bytes 786464 | tf_op jit(solution)/shard_map/all_to_all | solution.py:163
  384.9 3.3 gather_fusion
  392.0 13.4 %all_gather.15 = bf16[128,2048]{1,0:T(8,128)(2,1)S(1)} all-gather(bf16[128,512]{1,0:T(8,128)(2,1)S(1)} %fusion.67), channel_id=1, replica_groups=mesh['seq'=64,'tp'=4] {'tp'}, dimensions={1}, use_global_device_ids=true | all-gather | bytes 655360 | tf_op jit(solution)/shard_map/all_gather | solution.py:175
  (96 shorter events, 26.8 us)
Async XLA Ops:
  7.2 1.9 copy-start
  7.2 5.3 %copy-start.2 = (bf16[128,2048]{1,0:T(8,128)(2,1)S(1)}, bf16[128,2048]{1,0:T(8,128)(2,1)}, u32[]{:S(2)}) copy-start(bf16[128,2048]{1,0:T(8,128)(2,1)} %param.13) | copy-start | bytes 1572868
  7.2 4.0 copy-start.11
  7.2 4.8 %copy-start.9 = (s32[128,6]{0,1:T(8,128)S(1)}, s32[128,6]{0,1:T(8,128)}, u32[]{:S(2)}) copy-start(s32[128,6]{0,1:T(8,128)} %param.21) | copy-start | bytes 9220
  7.2 95.1 %all-gather.4.cloned.1.call-start = ((), (), s32[]{:S(2)}) async-start(), calls=%async_computation.7 | async-start | bytes 9584640 | tf_op jit(solution)/shard_map/all_gather | solution.py:86
  9.0 6.1 %copy-start.8 = (bf16[2,512,256]{2,1,0:T(8,128)(2,1)S(1)}, bf16[2,512,256]{2,1,0:T(8,128)(2,1)}, u32[]{:S(2)}) copy-start(bf16[2,512,256]{2,1,0:T(8,128)(2,1)} %param.18) | copy-start | bytes 1572868
  111.9 7.2 %copy-start.7 = (bf16[256,2048]{1,0:T(8,128)(2,1)S(1)}, bf16[256,2048]{1,0:T(8,128)(2,1)}, u32[]{:S(2)}) copy-start(bf16[256,2048]{1,0:T(8,128)(2,1)} %param.19) | copy-start | bytes 3145732
  120.3 14.1 %all-to-all-start = ((bf16[4,128,512]{2,1,0:T(8,128)(2,1)}), bf16[4,128,512]{2,1,0:T(8,128)(2,1)S(1)}, u32[]{:S(2)}, u32[]{:S(2)}) async-start(bf16[4,128,512]{2,1,0:T(8,128)(2,1)} %bitcast.117), calls=%async_computation | async-start | bytes 1048576 | tf_op jit(solution)/shard_map/all_to_all | solution.py:116
  124.5 87.5 %all-gather.6.cloned.1.call-start = ((), (), s32[]{:S(2)}) async-start(), calls=%async_computation.8 | async-start | bytes 3932160 | tf_op jit(solution)/shard_map/all_gather | solution.py:148
  134.5 0.7 copy-start.5
  173.9 82.1 %all-gather.8.cloned.1.call-start = ((), (), s32[]{:S(2)}) async-start(), calls=%async_computation.10 | async-start | bytes 3932160 | tf_op jit(solution)/shard_map/all_gather | solution.py:148
  208.5 6.2 %copy-start.12 = (f32[2048]{0:T(1024)S(1)}, f32[2048]{0:T(1024)}, u32[]{:S(2)}) copy-start(f32[2048]{0:T(1024)} %param.20) | copy-start | bytes 24580
  209.7 89.8 %reduce-scatter.3.cloned.1.call-start = ((), (), s32[]{:S(2)}) async-start(), calls=%async_computation.9 | async-start | bytes 3932160 | tf_op jit(solution)/shard_map/reduce_scatter | solution.py:160
  212.0 2.8 copy-start.4
  226.2 116.3 %reduce-scatter.5.cloned.1.call-start = ((), (), s32[]{:S(2)}) async-start(), calls=%async_computation.11 | async-start | bytes 3932160 | tf_op jit(solution)/shard_map/reduce_scatter | solution.py:160
  256.0 2.8 copy-start.3
  301.6 53.9 %copy-start.10 = (f32[128,6]{0,1:T(8,128)S(1)}, f32[128,6]{0,1:T(8,128)}, u32[]{:S(2)}) copy-start(f32[128,6]{0,1:T(8,128)} %param.22) | copy-start | bytes 9220
  301.6 43.1 %all-to-all-start.2 = ((bf16[64,12,512]{2,1,0:T(8,128)(2,1)}), bf16[64,12,512]{2,1,0:T(8,128)(2,1)S(1)}, u32[]{:S(2)}, u32[]{:S(2)}) async-start(bf16[64,12,512]{2,1,0:T(8,128)(2,1)} %reshape.242), calls=%async_computation.3 | async-start | bytes 2097152 | tf_op jit(solution)/shard_map/all_to_all | solution.py:163
  344.7 38.5 %all-to-all-start.4 = ((bf16[64,12,512]{2,1,0:T(8,128)(2,1)}), bf16[64,12,512]{2,1,0:T(8,128)(2,1)}, u32[]{:S(2)}, u32[]{:S(2)}) async-start(bf16[64,12,512]{2,1,0:T(8,128)(2,1)} %reshape.244), calls=%async_computation.6 | async-start | bytes 2097152 | tf_op jit(solution)/shard_map/all_to_all | solution.py:163
  388.2 18.0 %copy-start.1 = (bf16[2048,576]{0,1:T(8,128)(2,1)S(1)}, bf16[2048,576]{0,1:T(8,128)(2,1)}, u32[]{:S(2)}) copy-start(bf16[2048,576]{0,1:T(8,128)(2,1)} %param.16) | copy-start | bytes 7077892
  389.7 1.1 copy-start.6
Sparse Core Ops, SparseCore 0:
  12.2 90.1 all-gather.3
  174.1 37.8 all-gather.5
  213.8 42.2 all-gather.7
  258.5 41.0 reduce-scatter.2
  301.9 40.5 reduce-scatter.4

commit v11 on v10

--- a/solution.py
+++ b/solution.py
@@ -172,7 +172,9 @@
             jnp.float32
         )
     layer_part = (hidden + moe).astype(jnp.bfloat16)
-    layer_out = lax.all_gather(layer_part, "tp", axis=1, tiled=True)
+    repeated_part = jnp.broadcast_to(layer_part[None], (tp_count,) + layer_part.shape)
+    layer_pieces = lax.all_to_all(repeated_part, "tp", split_axis=0, concat_axis=0, tiled=True)
+    layer_out = layer_pieces.transpose(1, 0, 2).reshape(tok_count, D)
     return (layer_out, latent)
 
 

time: 413 us -> 412 us (level)
    all_gather x1 -> x0, blocking collectives: 13.4 us -> none  [on_device(): layer_out = lax.all_gather(layer_part, 'tp', axis=1, tiled=True)]
    all_to_all x0 -> x1, blocking collectives: none -> 12.3 us  [on_device(): lax.all_to_all(repeated_part, 'tp', split_axis=0, concat_axis=0, tiled=True)]
where the time goes in v11:
time: 412 us; the launch traced here: 410 us
  waiting for transfers between devices  212 us (51%)
  blocking collectives  84.1 us (20%)
  matrix products  41.3 us (10%)
  starting transfers between devices  25.9 us (6%)
  other arithmetic  18 us (4%)
  local copies, waits for them, and re-layouts  15.3 us (4%)
  between operations  14.2 us (3%)
    all_gather x1, waiting for transfers between devices, on_device(): shard_rows = lax.all_gather(latent, 'seq', axis=0, tiled=True)  83.5 us
    all_to_all x2, blocking collectives, on_device(): lax.all_to_all(sending, 'seq', split_axis=0, concat_axis=0, tiled=True)  71.7 us
    reduce_scatter x2, waiting for transfers between devices, on_device(): lax.psum_scatter(expert_out, 'tp', scatter_dimension=1, tiled=True)  59.5 us
    all_gather x2, waiting for transfers between devices, on_device(): lax.all_gather(flat_part, 'tp', axis=1, tiled=True).astype(jnp.float32)  31.8 us
    all_to_all x2, waiting for transfers between devices, on_device(): lax.all_to_all(expert_sum, 'seq', split_axis=0, concat_axis=0, tiled=True)  27.6 us
    all_to_all x2, starting transfers between devices, on_device(): lax.all_to_all(expert_sum, 'seq', split_axis=0, concat_axis=0, tiled=True)  21.3 us
    dot_general x2, matrix products, on_device(): jnp.dot(hidden_units, expert_down[0], preferred_element_type=jnp.float32)  15.2 us
    all_to_all x1, blocking collectives, on_device(): lax.all_to_all(repeated_part, 'tp', split_axis=0, concat_axis=0, tiled=True)  12.3 us
  transfers between devices with their start and end apart: 8, of which 7 were waited for; matrix products, arithmetic and copies ran while one was open for 10% of the time, Pallas kernels for 0%

profile of v11, /device:TPU:32, one launch (start us, length us, event | category | flops | bytes accessed | tf_op | source)
XLA Modules:
  0.0 410.3 jit_solution(14239379274214092569)
XLA Ops:
  18.8 83.5 %all-gather.4.cloned.1.call-done = bf16[8192,576]{0,1:T(8,128)(2,1)} async-done(((bf16[128,576]{0,1:T(8,128)(2,1)}), bf16[8192,576]{0,1:T(8,128)(2,1)}) %all-gather.4.cloned.1.call-update) | async-done | bytes 9437200 | tf_op jit(solution)/shard_map/all_gather | solution.py:86
  102.3 6.8 %select_reduce_fusion = (f32[256]{0:T(256)S(1)}, f32[256,8192]{1,0:T(8,128)S(1)}) fusion(s32[256]{0:T(256)S(1)} %le.48, s32[8192]{0:T(1024)S(1)} %convert_reduce_fusion.1, s32[256]{0:T(256)S(1)} %eq.54, bf16[8192,576]{0,1:T(8,128)(2,1)} %all-gather.4.cloned.1.call-done, f32[256,32]{1,0:T(8,128)S(1)} %bitcast.130, f32[256,32]{1,0:T(8,128)S(1)} %bitcast.129, ...), kind=kOutput, calls=%fused_computation.4 | convolution fusion | flops 2426994432 | bytes 18451456 | tf_op jit(solution)/shard_map/ra,ka->rk/dot_general | solution.py:94
  109.1 2.8 fusion.9
  111.9 6.3 %fusion.41 = f32[256,512]{1,0:T(8,128)S(1)} fusion(bf16[8192,576]{0,1:T(8,128)(2,1)} %all-gather.4.cloned.1.call-done, f32[256,8192]{1,0:T(8,128)S(1)} %get-tuple-element.33, f32[256]{0:T(256)S(1)} %broadcast_maximum_fusion, s32[256]{0:T(256)S(1)} %le.48, s32[8192]{0:T(1024)S(1)} %convert_reduce_fusion.1, s32[256]{0:T(256)S(1)} %eq.54, f32[256]{0:T(256)S(1)} %fusion.9), kind=kOutput, calls=%fused_computation.49 | convolution fusion | flops 2160197632 | bytes 17338368 | tf_op jit(solution)/shard_map/dot_general | solution.py:99
  120.3 4.2 %all-to-all-start = ((bf16[4,128,512]{2,1,0:T(8,128)(2,1)}), bf16[4,128,512]{2,1,0:T(8,128)(2,1)S(1)}, u32[]{:S(2)}, u32[]{:S(2)}) async-start(bf16[4,128,512]{2,1,0:T(8,128)(2,1)} %bitcast.120), calls=%async_computation | async-start | bytes 1048576 | tf_op jit(solution)/shard_map/all_to_all | solution.py:116
  125.3 9.1 %all-to-all-done = bf16[4,128,512]{2,1,0:T(8,128)(2,1)S(1)} async-done(((bf16[4,128,512]{2,1,0:T(8,128)(2,1)}), bf16[4,128,512]{2,1,0:T(8,128)(2,1)S(1)}, u32[]{:S(2)}, u32[]{:S(2)}) %all-to-all-start) | async-done | bytes 524320 | tf_op jit(solution)/shard_map/all_to_all | solution.py:116
  135.6 37.2 %all_to_all.30 = bf16[64,12,512]{2,1,0:T(8,128)(2,1)S(1)} all-to-all(bf16[64,12,512]{2,1,0:T(8,128)(2,1)S(1)} %get-tuple-element.8), channel_id=1, replica_groups=mesh['seq'=64,'tp'=4] {'seq'}, dimensions={0} | all-to-all | bytes 1572864 | tf_op jit(solution)/shard_map/all_to_all | solution.py:145
  174.0 34.5 %all_to_all.31 = bf16[64,12,512]{2,1,0:T(8,128)(2,1)S(1)} all-to-all(bf16[64,12,512]{2,1,0:T(8,128)(2,1)S(1)} %get-tuple-element.9), channel_id=1, replica_groups=mesh['seq'=64,'tp'=4] {'seq'}, dimensions={0} | all-to-all | bytes 1572864 | tf_op jit(solution)/shard_map/all_to_all | solution.py:145
  209.7 2.2 all-gather.6.cloned.1.call-done
  212.0 2.7 fusion.3
  214.8 3.8 fusion.27
  218.6 7.6 %convolution_convert_fusion.1 = bf16[768,2048]{1,0:T(8,128)(2,1)} fusion(bf16[1,352,2048]{2,1,0:T(8,128)(2,1)} %param.25, bf16[1,2048,352]{1,2,0:T(8,128)(2,1)} %param.24, f32[768,352]{0,1:T(8,128)} %fusion.27, bf16[768,2048]{1,0:T(8,128)(2,1)S(1)} %copy-done.4, f32[2048]{0:T(1024)S(1)} %copy-done.12, f32[768]{0:T(1024)S(1)} %add_rsqrt_fusion.1), kind=kOutput, calls=%fused_computation.27 | convolution fusion | flops 2224078848 | bytes 10267648 | tf_op jit(solution)/shard_map/dot_general | solution.py:157
  226.5 29.6 %all-gather.8.cloned.1.call-done = bf16[768,2048]{1,0:T(8,128)(2,1)} async-done(((bf16[768,512]{1,0:T(8,128)(2,1)}), bf16[768,2048]{1,0:T(8,128)(2,1)}) %all-gather.8.cloned.1.call-update) | async-done | bytes 3145744 | tf_op jit(solution)/shard_map/all_gather | solution.py:148
  256.0 2.7 fusion.6
  258.9 3.8 fusion.25
  262.7 7.6 %convolution_convert_fusion = bf16[768,2048]{1,0:T(8,128)(2,1)} fusion(bf16[1,352,2048]{2,1,0:T(8,128)(2,1)} %param.25, bf16[1,2048,352]{1,2,0:T(8,128)(2,1)} %param.24, f32[768,352]{0,1:T(8,128)} %fusion.25, bf16[768,2048]{1,0:T(8,128)(2,1)S(1)} %copy-done.3, f32[768]{0:T(1024)S(1)} %add_rsqrt_fusion, f32[2048]{0:T(1024)S(1)} %copy-done.12), kind=kOutput, calls=%fused_computation.26 | convolution fusion | flops 2224078848 | bytes 10267648 | tf_op jit(solution)/shard_map/dot_general | solution.py:157
  270.3 29.2 %reduce-scatter.3.cloned.1.call-done = bf16[768,512]{1,0:T(8,128)(2,1)} async-done(((bf16[768,2048]{1,0:T(8,128)(2,1)}), bf16[768,512]{1,0:T(8,128)(2,1)}) %reduce-scatter.3.cloned.1.call-update) | async-done | bytes 786448 | tf_op jit(solution)/shard_map/reduce_scatter | solution.py:160
  301.6 10.6 %all-to-all-start.2 = ((bf16[64,12,512]{2,1,0:T(8,128)(2,1)}), bf16[64,12,512]{2,1,0:T(8,128)(2,1)S(1)}, u32[]{:S(2)}, u32[]{:S(2)}) async-start(bf16[64,12,512]{2,1,0:T(8,128)(2,1)} %reshape.246), calls=%async_computation.3 | async-start | bytes 2097152 | tf_op jit(solution)/shard_map/all_to_all | solution.py:163
  312.3 30.3 %reduce-scatter.5.cloned.1.call-done = bf16[768,512]{1,0:T(8,128)(2,1)} async-done(((bf16[768,2048]{1,0:T(8,128)(2,1)}), bf16[768,512]{1,0:T(8,128)(2,1)}) %reduce-scatter.5.cloned.1.call-update) | async-done | bytes 786448 | tf_op jit(solution)/shard_map/reduce_scatter | solution.py:160
  342.5 2.2 reshape.248
  344.7 10.7 %all-to-all-start.4 = ((bf16[64,12,512]{2,1,0:T(8,128)(2,1)}), bf16[64,12,512]{2,1,0:T(8,128)(2,1)}, u32[]{:S(2)}, u32[]{:S(2)}) async-start(bf16[64,12,512]{2,1,0:T(8,128)(2,1)} %reshape.248), calls=%async_computation.6 | async-start | bytes 2097152 | tf_op jit(solution)/shard_map/all_to_all | solution.py:163
  355.6 27.6 %all-to-all-done.4 = bf16[64,12,512]{2,1,0:T(8,128)(2,1)} async-done(((bf16[64,12,512]{2,1,0:T(8,128)(2,1)}), bf16[64,12,512]{2,1,0:T(8,128)(2,1)}, u32[]{:S(2)}, u32[]{:S(2)}) %all-to-all-start.4) | async-done | bytes 786464 | tf_op jit(solution)/shard_map/all_to_all | solution.py:163
  384.9 2.7 gather_fusion
  390.2 12.3 %all_to_all.32 = bf16[4,128,512]{2,1,0:T(8,128)(2,1)S(1)} all-to-all(bf16[4,128,512]{2,1,0:T(8,128)(2,1)S(1)} %broadcast_in_dim.20), channel_id=1, replica_groups=mesh['seq'=64,'tp'=4] {'tp'}, dimensions={0} | all-to-all | bytes 1048576 | tf_op jit(solution)/shard_map/all_to_all | solution.py:176
  (98 shorter events, 26.1 us)
Async XLA Ops:
  7.2 1.9 copy-start
  7.2 5.3 %copy-start.2 = (bf16[128,2048]{1,0:T(8,128)(2,1)S(1)}, bf16[128,2048]{1,0:T(8,128)(2,1)}, u32[]{:S(2)}) copy-start(bf16[128,2048]{1,0:T(8,128)(2,1)} %param.13) | copy-start | bytes 1572868
  7.2 4.0 copy-start.11
  7.2 4.8 %copy-start.9 = (s32[128,6]{0,1:T(8,128)S(1)}, s32[128,6]{0,1:T(8,128)}, u32[]{:S(2)}) copy-start(s32[128,6]{0,1:T(8,128)} %param.21) | copy-start | bytes 9220
  7.2 95.1 %all-gather.4.cloned.1.call-start = ((), (), s32[]{:S(2)}) async-start(), calls=%async_computation.8 | async-start | bytes 9584640 | tf_op jit(solution)/shard_map/all_gather | solution.py:86
  9.0 6.1 %copy-start.8 = (bf16[2,512,256]{2,1,0:T(8,128)(2,1)S(1)}, bf16[2,512,256]{2,1,0:T(8,128)(2,1)}, u32[]{:S(2)}) copy-start(bf16[2,512,256]{2,1,0:T(8,128)(2,1)} %param.18) | copy-start | bytes 1572868
  111.9 7.2 %copy-start.7 = (bf16[256,2048]{1,0:T(8,128)(2,1)S(1)}, bf16[256,2048]{1,0:T(8,128)(2,1)}, u32[]{:S(2)}) copy-start(bf16[256,2048]{1,0:T(8,128)(2,1)} %param.19) | copy-start | bytes 3145732
  120.3 14.1 %all-to-all-start = ((bf16[4,128,512]{2,1,0:T(8,128)(2,1)}), bf16[4,128,512]{2,1,0:T(8,128)(2,1)S(1)}, u32[]{:S(2)}, u32[]{:S(2)}) async-start(bf16[4,128,512]{2,1,0:T(8,128)(2,1)} %bitcast.120), calls=%async_computation | async-start | bytes 1048576 | tf_op jit(solution)/shard_map/all_to_all | solution.py:116
  124.5 87.5 %all-gather.6.cloned.1.call-start = ((), (), s32[]{:S(2)}) async-start(), calls=%async_computation.9 | async-start | bytes 3932160 | tf_op jit(solution)/shard_map/all_gather | solution.py:148
  134.5 0.7 copy-start.5
  173.9 82.1 %all-gather.8.cloned.1.call-start = ((), (), s32[]{:S(2)}) async-start(), calls=%async_computation.11 | async-start | bytes 3932160 | tf_op jit(solution)/shard_map/all_gather | solution.py:148
  208.5 6.2 %copy-start.12 = (f32[2048]{0:T(1024)S(1)}, f32[2048]{0:T(1024)}, u32[]{:S(2)}) copy-start(f32[2048]{0:T(1024)} %param.20) | copy-start | bytes 24580
  209.7 89.8 %reduce-scatter.3.cloned.1.call-start = ((), (), s32[]{:S(2)}) async-start(), calls=%async_computation.10 | async-start | bytes 3932160 | tf_op jit(solution)/shard_map/reduce_scatter | solution.py:160
  212.0 2.8 copy-start.4
  226.2 116.3 %reduce-scatter.5.cloned.1.call-start = ((), (), s32[]{:S(2)}) async-start(), calls=%async_computation.12 | async-start | bytes 3932160 | tf_op jit(solution)/shard_map/reduce_scatter | solution.py:160
  256.0 2.8 copy-start.3
  301.6 53.9 %copy-start.10 = (f32[128,6]{0,1:T(8,128)S(1)}, f32[128,6]{0,1:T(8,128)}, u32[]{:S(2)}) copy-start(f32[128,6]{0,1:T(8,128)} %param.22) | copy-start | bytes 9220
  301.6 43.1 %all-to-all-start.2 = ((bf16[64,12,512]{2,1,0:T(8,128)(2,1)}), bf16[64,12,512]{2,1,0:T(8,128)(2,1)S(1)}, u32[]{:S(2)}, u32[]{:S(2)}) async-start(bf16[64,12,512]{2,1,0:T(8,128)(2,1)} %reshape.246), calls=%async_computation.3 | async-start | bytes 2097152 | tf_op jit(solution)/shard_map/all_to_all | solution.py:163
  344.7 38.5 %all-to-all-start.4 = ((bf16[64,12,512]{2,1,0:T(8,128)(2,1)}), bf16[64,12,512]{2,1,0:T(8,128)(2,1)}, u32[]{:S(2)}, u32[]{:S(2)}) async-start(bf16[64,12,512]{2,1,0:T(8,128)(2,1)} %reshape.248), calls=%async_computation.6 | async-start | bytes 2097152 | tf_op jit(solution)/shard_map/all_to_all | solution.py:163
  387.8 1.2 copy-start.6
  387.9 16.0 %copy-start.1 = (bf16[2048,576]{0,1:T(8,128)(2,1)S(1)}, bf16[2048,576]{0,1:T(8,128)(2,1)}, u32[]{:S(2)}) copy-start(bf16[2048,576]{0,1:T(8,128)(2,1)} %param.16) | copy-start | bytes 7077892
Sparse Core Ops, SparseCore 0:
  12.2 90.1 all-gather.3
  174.1 37.8 all-gather.5
  213.8 42.2 all-gather.7
  258.5 41.0 reduce-scatter.2
  301.9 40.5 reduce-scatter.4

commit v12 on v11

--- a/solution.py
+++ b/solution.py
@@ -140,9 +140,9 @@
     chunk_count = 2
     chunk_slots = capacity // chunk_count
     returned_chunks = []
+    received_all = lax.all_to_all(outgoing, "seq", split_axis=0, concat_axis=0, tiled=True)
     for chunk in range(chunk_count):
-        sending = outgoing[:, chunk * chunk_slots : (chunk + 1) * chunk_slots]
-        received = lax.all_to_all(sending, "seq", split_axis=0, concat_axis=0, tiled=True)
+        received = received_all[:, chunk * chunk_slots : (chunk + 1) * chunk_slots]
         sources, slot_count, _ = received.shape
         flat_part = received.reshape(sources * slot_count, col_width)
         flat_rows = lax.all_gather(flat_part, "tp", axis=1, tiled=True).astype(jnp.float32)

time: 412 us -> 424 us (1.029)
  waiting for transfers between devices: 212 us -> 246 us
  blocking collectives: 84.1 us -> 60.8 us
    all_gather x2, waiting for transfers between devices: 31.8 us -> 66.2 us  [on_device(): lax.all_gather(flat_part, 'tp', axis=1, tiled=True).astype(jnp.float32)]
    all_to_all x2 -> x1, blocking collectives: 71.7 us -> 48.5 us  [on_device(): lax.all_to_all(outgoing, 'seq', split_axis=0, concat_axis=0, tiled=True)]
where the time goes in v12:
time: 424 us; the launch traced here: 421 us
  waiting for transfers between devices  246 us (58%)
  blocking collectives  60.8 us (14%)
  matrix products  41.3 us (10%)
  starting transfers between devices  25.9 us (6%)
  other arithmetic  18 us (4%)
  local copies, waits for them, and re-layouts  15.3 us (4%)
  between operations  14.2 us (3%)
    all_gather x1, waiting for transfers between devices, on_device(): shard_rows = lax.all_gather(latent, 'seq', axis=0, tiled=True)  83.5 us
    all_gather x2, waiting for transfers between devices, on_device(): lax.all_gather(flat_part, 'tp', axis=1, tiled=True).astype(jnp.float32)  66.2 us
    reduce_scatter x2, waiting for transfers between devices, on_device(): lax.psum_scatter(expert_out, 'tp', scatter_dimension=1, tiled=True)  59.5 us
    all_to_all x1, blocking collectives, on_device(): lax.all_to_all(outgoing, 'seq', split_axis=0, concat_axis=0, tiled=True)  48.5 us
    all_to_all x2, waiting for transfers between devices, on_device(): lax.all_to_all(expert_sum, 'seq', split_axis=0, concat_axis=0, tiled=True)  27.6 us
    all_to_all x2, starting transfers between devices, on_device(): lax.all_to_all(expert_sum, 'seq', split_axis=0, concat_axis=0, tiled=True)  21.3 us
    dot_general x2, matrix products, on_device(): jnp.dot(hidden_units, expert_down[0], preferred_element_type=jnp.float32)  15.2 us
    all_to_all x1, blocking collectives, on_device(): lax.all_to_all(repeated_part, 'tp', split_axis=0, concat_axis=0, tiled=True)  12.3 us
  transfers between devices with their start and end apart: 8, of which 7 were waited for; matrix products, arithmetic and copies ran while one was open for 10% of the time, Pallas kernels for 0%

profile of v12, /device:TPU:32, one launch (start us, length us, event | category | flops | bytes accessed | tf_op | source)
XLA Modules:
  0.0 421.5 jit_solution(11290351698439217234)
XLA Ops:
  18.8 83.5 %all-gather.4.cloned.1.call-done = bf16[8192,576]{0,1:T(8,128)(2,1)} async-done(((bf16[128,576]{0,1:T(8,128)(2,1)}), bf16[8192,576]{0,1:T(8,128)(2,1)}) %all-gather.4.cloned.1.call-update) | async-done | bytes 9437200 | tf_op jit(solution)/shard_map/all_gather | solution.py:86
  102.3 6.8 %select_reduce_fusion = (f32[256]{0:T(256)S(1)}, f32[256,8192]{1,0:T(8,128)S(1)}) fusion(s32[256]{0:T(256)S(1)} %le.48, s32[8192]{0:T(1024)S(1)} %convert_reduce_fusion.1, s32[256]{0:T(256)S(1)} %eq.54, bf16[8192,576]{0,1:T(8,128)(2,1)} %all-gather.4.cloned.1.call-done, f32[256,32]{1,0:T(8,128)S(1)} %bitcast.130, f32[256,32]{1,0:T(8,128)S(1)} %bitcast.129, ...), kind=kOutput, calls=%fused_computation.4 | convolution fusion | flops 2426994432 | bytes 18451456 | tf_op jit(solution)/shard_map/ra,ka->rk/dot_general | solution.py:94
  109.1 2.8 fusion.9
  111.9 6.3 %fusion.41 = f32[256,512]{1,0:T(8,128)S(1)} fusion(bf16[8192,576]{0,1:T(8,128)(2,1)} %all-gather.4.cloned.1.call-done, f32[256,8192]{1,0:T(8,128)S(1)} %get-tuple-element.33, f32[256]{0:T(256)S(1)} %broadcast_maximum_fusion, s32[256]{0:T(256)S(1)} %le.48, s32[8192]{0:T(1024)S(1)} %convert_reduce_fusion.1, s32[256]{0:T(256)S(1)} %eq.54, f32[256]{0:T(256)S(1)} %fusion.9), kind=kOutput, calls=%fused_computation.49 | convolution fusion | flops 2160197632 | bytes 17338368 | tf_op jit(solution)/shard_map/dot_general | solution.py:99
  120.3 4.2 %all-to-all-start = ((bf16[4,128,512]{2,1,0:T(8,128)(2,1)}), bf16[4,128,512]{2,1,0:T(8,128)(2,1)S(1)}, u32[]{:S(2)}, u32[]{:S(2)}) async-start(bf16[4,128,512]{2,1,0:T(8,128)(2,1)} %bitcast.120), calls=%async_computation | async-start | bytes 1048576 | tf_op jit(solution)/shard_map/all_to_all | solution.py:116
  125.3 9.1 %all-to-all-done = bf16[4,128,512]{2,1,0:T(8,128)(2,1)S(1)} async-done(((bf16[4,128,512]{2,1,0:T(8,128)(2,1)}), bf16[4,128,512]{2,1,0:T(8,128)(2,1)S(1)}, u32[]{:S(2)}, u32[]{:S(2)}) %all-to-all-start) | async-done | bytes 524320 | tf_op jit(solution)/shard_map/all_to_all | solution.py:116
  135.2 48.5 %all_to_all.25 = bf16[64,24,512]{2,1,0:T(8,128)(2,1)S(1)} all-to-all(bf16[64,24,512]{2,1,0:T(8,128)(2,1)S(1)} %bitcast.123), channel_id=1, replica_groups=mesh['seq'=64,'tp'=4] {'seq'}, dimensions={0} | all-to-all | bytes 3145728 | tf_op jit(solution)/shard_map/all_to_all | solution.py:143
  186.5 36.6 %all-gather.6.cloned.1.call-done = bf16[768,2048]{1,0:T(8,128)(2,1)} async-done(((bf16[768,512]{1,0:T(8,128)(2,1)}), bf16[768,2048]{1,0:T(8,128)(2,1)}) %all-gather.6.cloned.1.call-update) | async-done | bytes 3145744 | tf_op jit(solution)/shard_map/all_gather | solution.py:148
  223.1 2.7 fusion.3
  226.0 3.8 fusion.27
  229.7 7.6 %convolution_convert_fusion.1 = bf16[768,2048]{1,0:T(8,128)(2,1)} fusion(bf16[1,352,2048]{2,1,0:T(8,128)(2,1)} %param.25, bf16[1,2048,352]{1,2,0:T(8,128)(2,1)} %param.24, f32[768,352]{0,1:T(8,128)} %fusion.27, bf16[768,2048]{1,0:T(8,128)(2,1)S(1)} %copy-done.4, f32[2048]{0:T(1024)S(1)} %copy-done.12, f32[768]{0:T(1024)S(1)} %add_rsqrt_fusion.1), kind=kOutput, calls=%fused_computation.27 | convolution fusion | flops 2224078848 | bytes 10267648 | tf_op jit(solution)/shard_map/dot_general | solution.py:157
  237.6 29.6 %all-gather.8.cloned.1.call-done = bf16[768,2048]{1,0:T(8,128)(2,1)} async-done(((bf16[768,512]{1,0:T(8,128)(2,1)}), bf16[768,2048]{1,0:T(8,128)(2,1)}) %all-gather.8.cloned.1.call-update) | async-done | bytes 3145744 | tf_op jit(solution)/shard_map/all_gather | solution.py:148
  267.2 2.7 fusion.6
  270.0 3.8 fusion.25
  273.8 7.6 %convolution_convert_fusion = bf16[768,2048]{1,0:T(8,128)(2,1)} fusion(bf16[1,352,2048]{2,1,0:T(8,128)(2,1)} %param.25, bf16[1,2048,352]{1,2,0:T(8,128)(2,1)} %param.24, f32[768,352]{0,1:T(8,128)} %fusion.25, bf16[768,2048]{1,0:T(8,128)(2,1)S(1)} %copy-done.3, f32[768]{0:T(1024)S(1)} %add_rsqrt_fusion, f32[2048]{0:T(1024)S(1)} %copy-done.12), kind=kOutput, calls=%fused_computation.26 | convolution fusion | flops 2224078848 | bytes 10267648 | tf_op jit(solution)/shard_map/dot_general | solution.py:157
  281.5 29.2 %reduce-scatter.3.cloned.1.call-done = bf16[768,512]{1,0:T(8,128)(2,1)} async-done(((bf16[768,2048]{1,0:T(8,128)(2,1)}), bf16[768,512]{1,0:T(8,128)(2,1)}) %reduce-scatter.3.cloned.1.call-update) | async-done | bytes 786448 | tf_op jit(solution)/shard_map/reduce_scatter | solution.py:160
  310.7 2.1 reshape.246
  312.8 10.6 %all-to-all-start.2 = ((bf16[64,12,512]{2,1,0:T(8,128)(2,1)}), bf16[64,12,512]{2,1,0:T(8,128)(2,1)S(1)}, u32[]{:S(2)}, u32[]{:S(2)}) async-start(bf16[64,12,512]{2,1,0:T(8,128)(2,1)} %reshape.246), calls=%async_computation.3 | async-start | bytes 2097152 | tf_op jit(solution)/shard_map/all_to_all | solution.py:163
  323.4 30.3 %reduce-scatter.5.cloned.1.call-done = bf16[768,512]{1,0:T(8,128)(2,1)} async-done(((bf16[768,2048]{1,0:T(8,128)(2,1)}), bf16[768,512]{1,0:T(8,128)(2,1)}) %reduce-scatter.5.cloned.1.call-update) | async-done | bytes 786448 | tf_op jit(solution)/shard_map/reduce_scatter | solution.py:160
  353.7 2.2 reshape.248
  355.9 10.7 %all-to-all-start.3 = ((bf16[64,12,512]{2,1,0:T(8,128)(2,1)}), bf16[64,12,512]{2,1,0:T(8,128)(2,1)}, u32[]{:S(2)}, u32[]{:S(2)}) async-start(bf16[64,12,512]{2,1,0:T(8,128)(2,1)} %reshape.248), calls=%async_computation.5 | async-start | bytes 2097152 | tf_op jit(solution)/shard_map/all_to_all | solution.py:163
  366.7 27.6 %all-to-all-done.3 = bf16[64,12,512]{2,1,0:T(8,128)(2,1)} async-done(((bf16[64,12,512]{2,1,0:T(8,128)(2,1)}), bf16[64,12,512]{2,1,0:T(8,128)(2,1)}, u32[]{:S(2)}, u32[]{:S(2)}) %all-to-all-start.3) | async-done | bytes 786464 | tf_op jit(solution)/shard_map/all_to_all | solution.py:163
  396.0 2.7 gather_fusion
  401.3 12.3 %all_to_all.26 = bf16[4,128,512]{2,1,0:T(8,128)(2,1)S(1)} all-to-all(bf16[4,128,512]{2,1,0:T(8,128)(2,1)S(1)} %broadcast_in_dim.20), channel_id=1, replica_groups=mesh['seq'=64,'tp'=4] {'tp'}, dimensions={0} | all-to-all | bytes 1048576 | tf_op jit(solution)/shard_map/all_to_all | solution.py:176
  (97 shorter events, 24.0 us)
Async XLA Ops:
  7.2 1.9 copy-start
  7.2 5.3 %copy-start.2 = (bf16[128,2048]{1,0:T(8,128)(2,1)S(1)}, bf16[128,2048]{1,0:T(8,128)(2,1)}, u32[]{:S(2)}) copy-start(bf16[128,2048]{1,0:T(8,128)(2,1)} %param.13) | copy-start | bytes 1572868
  7.2 4.0 copy-start.11
  7.2 4.8 %copy-start.9 = (s32[128,6]{0,1:T(8,128)S(1)}, s32[128,6]{0,1:T(8,128)}, u32[]{:S(2)}) copy-start(s32[128,6]{0,1:T(8,128)} %param.21) | copy-start | bytes 9220
  7.2 95.1 %all-gather.4.cloned.1.call-start = ((), (), s32[]{:S(2)}) async-start(), calls=%async_computation.7 | async-start | bytes 9584640 | tf_op jit(solution)/shard_map/all_gather | solution.py:86
  9.0 6.1 %copy-start.8 = (bf16[2,512,256]{2,1,0:T(8,128)(2,1)S(1)}, bf16[2,512,256]{2,1,0:T(8,128)(2,1)}, u32[]{:S(2)}) copy-start(bf16[2,512,256]{2,1,0:T(8,128)(2,1)} %param.18) | copy-start | bytes 1572868
  111.9 7.2 %copy-start.7 = (bf16[256,2048]{1,0:T(8,128)(2,1)S(1)}, bf16[256,2048]{1,0:T(8,128)(2,1)}, u32[]{:S(2)}) copy-start(bf16[256,2048]{1,0:T(8,128)(2,1)} %param.19) | copy-start | bytes 3145732
  120.3 14.1 %all-to-all-start = ((bf16[4,128,512]{2,1,0:T(8,128)(2,1)}), bf16[4,128,512]{2,1,0:T(8,128)(2,1)S(1)}, u32[]{:S(2)}, u32[]{:S(2)}) async-start(bf16[4,128,512]{2,1,0:T(8,128)(2,1)} %bitcast.120), calls=%async_computation | async-start | bytes 1048576 | tf_op jit(solution)/shard_map/all_to_all | solution.py:116
  124.5 98.6 %all-gather.6.cloned.1.call-start = ((), (), s32[]{:S(2)}) async-start(), calls=%async_computation.8 | async-start | bytes 3932160 | tf_op jit(solution)/shard_map/all_gather | solution.py:148
  134.5 0.7 copy-start.5
  185.2 40.6 %copy-start.12 = (f32[2048]{0:T(1024)S(1)}, f32[2048]{0:T(1024)}, u32[]{:S(2)}) copy-start(f32[2048]{0:T(1024)} %param.20) | copy-start | bytes 24580
  185.2 82.0 %all-gather.8.cloned.1.call-start = ((), (), s32[]{:S(2)}) async-start(), calls=%async_computation.10 | async-start | bytes 3932160 | tf_op jit(solution)/shard_map/all_gather | solution.py:148
  186.4 124.2 %reduce-scatter.3.cloned.1.call-start = ((), (), s32[]{:S(2)}) async-start(), calls=%async_computation.9 | async-start | bytes 3932160 | tf_op jit(solution)/shard_map/reduce_scatter | solution.py:160
  223.1 2.8 copy-start.4
  237.4 116.3 %reduce-scatter.5.cloned.1.call-start = ((), (), s32[]{:S(2)}) async-start(), calls=%async_computation.11 | async-start | bytes 3932160 | tf_op jit(solution)/shard_map/reduce_scatter | solution.py:160
  267.2 2.8 copy-start.3
  312.8 53.9 %copy-start.10 = (f32[128,6]{0,1:T(8,128)S(1)}, f32[128,6]{0,1:T(8,128)}, u32[]{:S(2)}) copy-start(f32[128,6]{0,1:T(8,128)} %param.22) | copy-start | bytes 9220
  312.8 43.1 %all-to-all-start.2 = ((bf16[64,12,512]{2,1,0:T(8,128)(2,1)}), bf16[64,12,512]{2,1,0:T(8,128)(2,1)S(1)}, u32[]{:S(2)}, u32[]{:S(2)}) async-start(bf16[64,12,512]{2,1,0:T(8,128)(2,1)} %reshape.246), calls=%async_computation.3 | async-start | bytes 2097152 | tf_op jit(solution)/shard_map/all_to_all | solution.py:163
  355.9 38.5 %all-to-all-start.3 = ((bf16[64,12,512]{2,1,0:T(8,128)(2,1)}), bf16[64,12,512]{2,1,0:T(8,128)(2,1)}, u32[]{:S(2)}, u32[]{:S(2)}) async-start(bf16[64,12,512]{2,1,0:T(8,128)(2,1)} %reshape.248), calls=%async_computation.5 | async-start | bytes 2097152 | tf_op jit(solution)/shard_map/all_to_all | solution.py:163
  399.0 1.2 copy-start.6
  399.0 16.0 %copy-start.1 = (bf16[2048,576]{0,1:T(8,128)(2,1)S(1)}, bf16[2048,576]{0,1:T(8,128)(2,1)}, u32[]{:S(2)}) copy-start(bf16[2048,576]{0,1:T(8,128)(2,1)} %param.16) | copy-start | bytes 7077892
Sparse Core Ops, SparseCore 0:
  12.2 90.1 all-gather.3
  185.4 37.7 all-gather.5
  224.9 42.2 all-gather.7
  269.6 41.0 reduce-scatter.2
  313.1 40.5 reduce-scatter.4
